TPU v7x, 128 devices: a whole 4x4x4 slice. The times are simulated.
128 devices in a mesh: node: 4 (over x), intra: 32 (over z, y, core).
Axes of the slice: x: 4, y: 4, z: 4, core: 2. Of those that a mesh axis runs over, the one named last changes fastest.
Arguments:
- gradients: bfloat16 [4, 32, 12288, 512], P('node', 'intra'), as said below
- sign_table: int32 [64, 512], replicated, may hold values from -1 to 1, as said below
- loss_scale: float32 [1], replicated, may hold values from 256 to 65536
- step_count: int32 [1], replicated, may hold values from 1 to 8
- weights: float32 [12288, 512], P('intra', 'node'), may hold values from -6 to 6
- first_moment: float32 [12288, 512], P('intra', 'node'), may hold values from -3 to 3
- second_moment: float32 [12288, 512], P('intra', 'node'), may hold values from 0.01 to 0.1
Outputs:
- new_weights: float32 [12288, 512], P('intra', 'node')
- new_first: float32 [12288, 512], P('intra', 'node')
- new_second: float32 [12288, 512], P('intra', 'node')
Inputs may be any that keep to these rules, and one draw needn't show every extreme that they name: `gradients`: each replica's gradient is multiplied by loss_scale. `sign_table`: every entry is -1 or 1.
All inputs are finite; a program needn't handle non-finite values.
Results may differ from a plain program's by a relative error of at most 0.0003.
Values sent between devices are 32-bit elements; how exact they have to be, the bound alone decides.
No kernel may reach another device: no remote copies, remote signals or barrier semaphores. Data moves between devices by JAX's collectives and lax.ppermute only.
A program may use at most 128 MiB of HBM per device.

v0:
```python
import functools
import math

import jax
import jax.numpy as jnp
from jax import lax
from jax.sharding import Mesh
from jax.sharding import PartitionSpec as P

BLOCK = 128
SIGN_ROWS = 64
NODE_INTRA = ("node", "intra_0", "intra_1", "intra_2")
INTRA = ("intra_0", "intra_1", "intra_2")


def over_axes(value, axes):
    return functools.reduce(lax.pmax, axes, value)


def hadamard(order):
    index = jnp.arange(order, dtype=jnp.int32)
    common = index[:, None] & index[None, :]
    parity = jnp.zeros((order, order), jnp.int32)
    for bit_index in range(order.bit_length() - 1):
        parity = parity ^ common >> bit_index & 1
    return 1 - 2 * parity


def shards(gradients, sign_table, loss_scale, step_count, weights, first_moment, second_moment):
    local_grad = gradients[0, 0]
    row_count, col_count = local_grad.shape
    owned_rows = weights.shape[0]
    table_int = hadamard(BLOCK)
    table_half = table_int.astype(jnp.bfloat16)
    table_full = table_int.astype(jnp.float32)
    inverse_root = 1.0 / math.sqrt(BLOCK)
    sign_half = sign_table.astype(jnp.bfloat16)
    repeats = local_grad.shape[0] // SIGN_ROWS
    signed = (local_grad * jnp.tile(sign_half, (repeats, 1))).reshape(-1, BLOCK)
    spun = jnp.dot(signed, table_half, preferred_element_type=jnp.float32) * inverse_root
    rotated = spun.reshape(local_grad.shape[0], col_count)
    local_top = jnp.max(jnp.abs(rotated))
    top_value = over_axes(local_top, NODE_INTRA)
    level_scale = 127.0 / top_value
    spun = rotated
    partial_value = lax.psum_scatter(
        jnp.floor(spun * level_scale + 0.5), INTRA, scatter_dimension=0, tiled=True
    )
    summed = lax.psum_scatter(partial_value, "node", scatter_dimension=1, tiled=True)
    replicas = lax.axis_size("node") * lax.axis_size(INTRA)
    factor = top_value / (127.0 * replicas * loss_scale[0])
    scaled = summed * factor
    back = jnp.dot(scaled, table_full, precision=lax.Precision.HIGHEST) * inverse_root
    column_start = lax.axis_index("node") * BLOCK
    own_signs = lax.dynamic_slice_in_dim(sign_table, column_start, BLOCK, 1)
    own_tile = jnp.tile(own_signs, (owned_rows // SIGN_ROWS, 1)).astype(jnp.float32)
    grad = back * own_tile
    new_first = 0.9 * first_moment + 0.1 * grad
    new_second = 0.95 * second_moment + 0.05 * grad * grad
    steps_float = step_count[0].astype(jnp.float32)
    first_hat = new_first / (1.0 - jnp.power(jnp.float32(0.9), steps_float))
    second_hat = new_second / (1.0 - jnp.power(jnp.float32(0.95), steps_float))
    update = first_hat / (jnp.sqrt(second_hat) + 1e-08) + 0.1 * weights
    new_weights = weights - 0.2 * update
    return (new_weights, new_first, new_second)


def solution(mesh):
    torus = Mesh(
        mesh.devices.reshape(mesh.shape["node"], 4, 4, 2), ("node", "intra_0", "intra_1", "intra_2")
    )
    placed = (
        P("node", INTRA, None, None),
        P(),
        P(),
        P(),
        P(INTRA, "node"),
        P(INTRA, "node"),
        P(INTRA, "node"),
    )
    return jax.shard_map(
        shards,
        mesh=torus,
        in_specs=placed,
        out_specs=(P(INTRA, "node"), P(INTRA, "node"), P(INTRA, "node")),
        check_vma=False,
    )
```

profile of v0, /device:TPU:0, one launch (start us, length us, event | category | flops | bytes accessed | tf_op | source)
XLA Modules:
  0.0 322.6 jit_solution(6129322327200025307)
XLA Ops:
  7.2 0.0 reduce-scatter.3.cloned.1.call-start
  7.2 0.9 convert_element_type.20
  8.1 6.2 %tile.6 = bf16[192,64,1,512]{3,1,0,2:T(8,128)(2,1)} broadcast(bf16[64,512]{1,0:T(8,128)(2,1)S(1)} %convert_element_type.20), dimensions={1,3} | broadcast | bytes 12648448 | tf_op jit(solution)/shard_map/tile | solution.py:39
  14.3 20.4 %tile.7 = bf16[49152,128]{1,0:T(8,128)(2,1)} reshape(bf16[192,64,1,512]{3,1,0,2:T(8,128)(2,1)} %tile.6) | data formatting | bytes 25165824 | tf_op jit(solution)/shard_map/tile | solution.py:39
  34.6 20.2 %squeeze.2 = bf16[49152,128]{1,0:T(8,128)(2,1)} reshape(bf16[1,1,12288,512]{3,2,1,0:T(8,128)(2,1)} %param.7) | data formatting | bytes 25165824 | tf_op jit(solution)/shard_map/squeeze | solution.py:30
  54.9 16.2 %abs_reduce_fusion = (f32[]{:T(128)}, f32[49152,128]{1,0:T(8,128)}) fusion(bf16[49152,128]{1,0:T(8,128)(2,1)} %squeeze.2, bf16[49152,128]{1,0:T(8,128)(2,1)} %tile.7), kind=kOutput, calls=%fused_computation.1 | convolution fusion | flops 1636171776 | bytes 50331652 | tf_op jit(solution)/shard_map/dot_general | solution.py:40
  71.1 11.2 %pmax.28 = f32[]{:T(128)} all-reduce(f32[]{:T(128)} %get-tuple-element.6), channel_id=1, replica_groups=mesh['node'=4,'intra_0'=4,'intra_1'=4,'intra_2'=2] {'node'}, use_global_device_ids=true, to_apply=%region_1.0 | all-reduce | flops 1 | bytes 8 | tf_op jit(solution)/shard_map/pmax | solution.py:17
  82.3 12.4 %pmax.29 = f32[]{:T(128)} all-reduce(f32[]{:T(128)} %pmax.28), channel_id=1, replica_groups=mesh['node'=4,'intra_0'=4,'intra_1'=4,'intra_2'=2] {'intra_0'}, use_global_device_ids=true, to_apply=%region_2.0 | all-reduce | flops 1 | bytes 8 | tf_op jit(solution)/shard_map/pmax | solution.py:17
  94.6 11.3 %pmax.30 = f32[]{:T(128)} all-reduce(f32[]{:T(128)} %pmax.29), channel_id=1, replica_groups=mesh['node'=4,'intra_0'=4,'intra_1'=4,'intra_2'=2] {'intra_1'}, use_global_device_ids=true, to_apply=%region_3.0 | all-reduce | flops 1 | bytes 8 | tf_op jit(solution)/shard_map/pmax | solution.py:17
  106.0 3.1 pmax.31
  109.8 17.1 %add_floor_fusion = f32[49152,128]{1,0:T(8,128)} fusion(f32[49152,128]{1,0:T(8,128)} %get-tuple-element.7, f32[]{:T(128)S(6)} %mul.81), kind=kLoop, calls=%fused_computation | loop fusion | flops 18874368 | bytes 50331652 | tf_op jit(solution)/shard_map/floor | solution.py:47
  126.8 27.0 %floor.7 = f32[12288,512]{1,0:T(8,128)} reshape(f32[49152,128]{1,0:T(8,128)} %add_floor_fusion) | data formatting | bytes 50331648 | tf_op jit(solution)/shard_map/floor | solution.py:47
  153.8 0.0 copy-start
  153.8 0.0 copy-start.1
  153.8 0.0 copy-start.2
  153.8 0.0 reduce-scatter.3.cloned.1.call-update
  153.8 0.0 reduce-scatter.5.cloned.1.call-start
  153.9 135.8 %reduce-scatter.3.cloned.1.call-done = f32[384,512]{1,0:T(8,128)} async-done(((f32[12288,512]{1,0:T(8,128)}), f32[384,512]{1,0:T(8,128)}) %reduce-scatter.3.cloned.1.call-update) | async-done | bytes 786448 | tf_op jit(solution)/shard_map/reduce_scatter | solution.py:46
  289.6 0.0 reduce-scatter.5.cloned.1.call-update
  291.7 0.8 dynamic-slice_convert_fusion
  292.5 21.0 %reduce-scatter.5.cloned.1.call-done = f32[384,128]{1,0:T(8,128)} async-done(((f32[384,512]{1,0:T(8,128)}), f32[384,128]{1,0:T(8,128)}) %reduce-scatter.5.cloned.1.call-update) | async-done | bytes 196624 | tf_op jit(solution)/shard_map/reduce_scatter | solution.py:49
  313.5 0.0 copy-done
  313.5 0.0 copy-done.1
  313.5 0.0 copy-done.2
  313.5 2.2 multiply_subtract_fusion
  (1 shorter events, 0.0 us)
Async XLA Ops:
  7.2 282.5 %reduce-scatter.3.cloned.1.call-start = ((), (), s32[]{:S(2)}) async-start(), calls=%async_computation.2 | async-start | bytes 25952256 | tf_op jit(solution)/shard_map/reduce_scatter | solution.py:46
  153.8 159.7 %copy-start = (f32[384,128]{1,0:T(8,128)S(1)}, f32[384,128]{1,0:T(8,128)}, u32[]{:S(2)}) copy-start(f32[384,128]{1,0:T(8,128)} %param.11) | copy-start | bytes 589828
  153.8 159.7 %copy-start.1 = (f32[384,128]{1,0:T(8,128)S(1)}, f32[384,128]{1,0:T(8,128)}, u32[]{:S(2)}) copy-start(f32[384,128]{1,0:T(8,128)} %param.13) | copy-start | bytes 589828
  153.8 159.7 %copy-start.2 = (f32[384,128]{1,0:T(8,128)S(1)}, f32[384,128]{1,0:T(8,128)}, u32[]{:S(2)}) copy-start(f32[384,128]{1,0:T(8,128)} %param.12) | copy-start | bytes 589828
  153.8 159.7 %reduce-scatter.5.cloned.1.call-start = ((), (), s32[]{:S(2)}) async-start(), calls=%async_computation.3 | async-start | bytes 983040 | tf_op jit(solution)/shard_map/reduce_scatter | solution.py:49
Sparse Core Ops, SparseCore 0:
  154.0 135.6 reduce-scatter.2
  292.2 21.2 reduce-scatter.4
where the time goes:
time: 325 us; the launch traced here: 323 us
  waiting for transfers between devices  157 us (48%)
  local copies, waits for them, and re-layouts  73.7 us (23%)
  blocking collectives  38 us (12%)
  other arithmetic  18.8 us (6%)
  matrix products  18.4 us (6%)
  between operations  16.8 us (5%)
    reduce_scatter x1, waiting for transfers between devices, shards(): lax.psum_scatter(jnp.floor(spun * level_scale + 0.5), INTRA, scatter_dime...  136 us
    pmax x4, blocking collectives, over_axes(): return functools.reduce(lax.pmax, axes, value)  38 us
    floor x1, local copies, waits for them, and re-layouts, shards(): jnp.floor(spun * level_scale + 0.5)  27 us
    another operation x2, local copies, waits for them, and re-layouts, shards(): signed = (local_grad * jnp.tile(sign_half, (repeats, 1))).reshape(-1, BLOCK)  26.5 us
    reduce_scatter x1, waiting for transfers between devices, shards(): lax.psum_scatter(partial_value, 'node', scatter_dimension=1, tiled=True)  21 us
    squeeze x1, local copies, waits for them, and re-layouts, shards(): local_grad = gradients[0, 0]  20.2 us
    floor x1, other arithmetic, shards(): jnp.floor(spun * level_scale + 0.5)  17.1 us
    dot_general x1, matrix products, shards(): jnp.dot(signed, table_half, preferred_element_type=jnp.float32)  16.2 us
  transfers between devices with their start and end apart: 2, of which 2 were waited for; matrix products, arithmetic and copies ran while one was open for 0% of the time, Pallas kernels for 0%

commit v1 on v0

v1 whole, which is shorter than its diff:
```python
import functools
import math

import jax
import jax.numpy as jnp
from jax import lax
from jax.experimental import pallas as pl
from jax.experimental.pallas import tpu as pltpu
from jax.sharding import Mesh
from jax.sharding import PartitionSpec as P

BLOCK = 128
SIGN_ROWS = 64
ROOT = 1.0 / math.sqrt(BLOCK)
CHIPS = ("x", "z", "y")
ALL = ("x", "z", "y", "core")
INTRA = ("z", "y", "core")
FIRST = ("x", "y", "z")
FIELD = 4096.0
F32 = jnp.float32
BF16 = jnp.bfloat16


def hadamard(order):
    index = jnp.arange(order, dtype=jnp.int32)
    common = index[:, None] & index[None, :]
    parity = jnp.zeros((order, order), jnp.int32)
    for bit_index in range(order.bit_length() - 1):
        parity = parity ^ common >> bit_index & 1
    return 1 - 2 * parity


def rotate(block, signs, table):
    signed = block * signs
    halves = [
        jnp.dot(signed[:, 256 * h : 256 * h + 256], table, preferred_element_type=F32)
        for h in range(2)
    ]
    return jnp.concatenate(halves, axis=1) * ROOT


def rotate_kernel(place, own_ref, other_ref, sign_ref, table_ref, raw_ref, top_ref):
    signs = jnp.concatenate([sign_ref[...]] * 2, axis=0)
    table = table_ref[...]

    @pl.when(pl.program_id(0) == 0)
    def _():
        top_ref[...] = jnp.zeros_like(top_ref)

    def fold(value):
        return jnp.max(jnp.abs(value).reshape(-1, 8, 512), axis=0)

    best = jnp.zeros((8, 512), F32)
    for y in range(4):
        best = jnp.maximum(best, fold(rotate(own_ref[0, y, 0, 0], signs, table)))
        other = rotate(other_ref[0, y, 0, 0], signs, table)
        raw_ref[0, y] = other
        best = jnp.maximum(best, fold(other))
    top_ref[...] = jnp.maximum(top_ref[...], best)


def rotate_third(third, place, grads, signs, table):
    view = grads.reshape(4, 4, 2, 3, 128, 512)
    block = (1, 4, 1, 1, 128, 512)
    return pl.pallas_call(
        rotate_kernel,
        grid_spec=pltpu.PrefetchScalarGridSpec(
            num_scalar_prefetch=1,
            grid=(4,),
            in_specs=[
                pl.BlockSpec(block, lambda i, p: (i, 0, p[0], third, 0, 0)),
                pl.BlockSpec(block, lambda i, p: (i, 0, 1 - p[0], third, 0, 0)),
                pl.BlockSpec((64, 512), lambda i, p: (0, 0)),
                pl.BlockSpec((256, 256), lambda i, p: (0, 0)),
            ],
            out_specs=[
                pl.BlockSpec((1, 4, 128, 512), lambda i, p: (i, 0, 0, 0)),
                pl.BlockSpec((8, 512), lambda i, p: (0, 0)),
            ],
        ),
        out_shape=[
            jax.ShapeDtypeStruct((4, 4, 128, 512), F32),
            jax.ShapeDtypeStruct((8, 512), F32),
        ],
        compiler_params=pltpu.CompilerParams(vmem_limit_bytes=40 * 2**20),
        cost_estimate=pl.CostEstimate(flops=2 * 10**9, bytes_accessed=9 * 10**6, transcendentals=0),
    )(place, view, view, signs, table)


def spread_kernel(a_ref, b_ref, c_ref, out_ref):
    best = jnp.maximum(jnp.maximum(a_ref[...], b_ref[...]), c_ref[...])
    out_ref[...] = jnp.broadcast_to(jnp.max(best, axis=(0, 1), keepdims=True), (128, 128))


def level_kernel(
    place, own0, own1, own2, raw0, raw1, raw2, sign0, sign1, sign2, table_ref, top_ref, out0, out1, out2
):
    table = table_ref[...]
    scale = 127.0 / jnp.max(top_ref[...], axis=(0, 1), keepdims=True)
    for own, raw, sign, out in ((own0, raw0, sign0, out0), (own1, raw1, sign1, out1), (own2, raw2, sign2, out2)):
        signs = sign[...]
        for y in range(4):
            mine = rotate(own[0, y, 0, 0], signs, table)
            total = jnp.floor(mine * scale + 0.5) + jnp.floor(raw[0, y] * scale + 0.5)
            word = total[:16] + FIELD * total[16:]
            for x in range(4):
                out[x, 0, y] = word[:, 128 * x : 128 * x + 128]


def levels_for(place, grads, raws, signs, table, tops):
    view = grads.reshape(4, 4, 2, 12, 32, 512)
    own = [
        pl.BlockSpec((1, 4, 1, 1, 32, 512), lambda i, p, t=t: (i, 0, p[0], 4 * t + p[1 + t], 0, 0))
        for t in range(3)
    ]
    raw = [pl.BlockSpec((1, 4, 32, 512), lambda i, p, t=t: (i, 0, p[1 + t], 0)) for t in range(3)]
    sign = [pl.BlockSpec((32, 512), lambda i, p, t=t: (lax.rem(p[1 + t], 2), 0)) for t in range(3)]
    return pl.pallas_call(
        level_kernel,
        grid_spec=pltpu.PrefetchScalarGridSpec(
            num_scalar_prefetch=1,
            grid=(4,),
            in_specs=own
            + raw
            + sign
            + [
                pl.BlockSpec((256, 256), lambda i, p: (0, 0)),
                pl.BlockSpec((128, 128), lambda i, p: (0, 0)),
            ],
            out_specs=[pl.BlockSpec((4, 1, 4, 16, 128), lambda i, p: (0, i, 0, 0, 0))] * 3,
        ),
        out_shape=[jax.ShapeDtypeStruct((4, 4, 4, 16, 128), F32)] * 3,
        compiler_params=pltpu.CompilerParams(vmem_limit_bytes=40 * 2**20),
        cost_estimate=pl.CostEstimate(flops=10**9, bytes_accessed=6 * 10**6, transcendentals=0),
    )(place, view, view, view, *raws, signs, signs, signs, table, tops)


def gather_kernel(*refs):
    out = refs[-1]
    for t in range(3):
        a, b, c, d = (refs[4 * t + k][0] for k in range(4))
        out[:, 16 * t : 16 * t + 16, :] = ((a + b) + (c + d)).reshape(16, 16, 128)


def sum_four(parts):
    return pl.pallas_call(
        gather_kernel,
        grid=(4,),
        in_specs=[pl.BlockSpec((1, 4, 4, 16, 128), lambda i: (i, 0, 0, 0, 0))] * 12,
        out_specs=pl.BlockSpec((16, 48, 128), lambda i: (i, 0, 0)),
        out_shape=jax.ShapeDtypeStruct((64, 48, 128), F32),
        compiler_params=pltpu.CompilerParams(vmem_limit_bytes=40 * 2**20),
        cost_estimate=pl.CostEstimate(flops=10**6, bytes_accessed=8 * 10**6, transcendentals=0),
    )(*parts)


def update_kernel(
    scalars, words_ref, table_ref, sign_ref, weights_ref, first_ref, second_ref, weights_out, first_out, second_out
):
    table = table_ref[...]
    for t in range(3):
        for q in range(4):
            parts = []
            for a in range(4):
                for b in range(4):
                    x, z, y = ((q, a, b), (a, b, q), (a, q, b))[t]
                    parts.append(words_ref[x, z, y, 16 * t : 16 * t + 16, :])
            low = high = jnp.zeros((16, 128), F32)
            for word in parts:
                upper = jnp.floor(word * (1.0 / FIELD) + 0.5)
                high = high + upper
                low = low + (word - upper * FIELD)
            total = jnp.concatenate([low, high], axis=0)
            coarse = jnp.floor(total * (1.0 / 128.0) + 0.5)
            fine = total - coarse * 128.0
            back = 128.0 * jnp.dot(coarse.astype(BF16), table, preferred_element_type=F32) + jnp.dot(
                fine.astype(BF16), table, preferred_element_type=F32
            )
            rows = pl.ds(128 * t + 32 * q, 32)
            grad = (back * scalars[0]) * ROOT * sign_ref[pl.ds(32 * (q % 2), 32), :].astype(F32)
            first = 0.9 * first_ref[rows, :] + 0.1 * grad
            second = 0.95 * second_ref[rows, :] + 0.05 * grad * grad
            weights = weights_ref[rows, :]
            update = (first / scalars[1]) / (jnp.sqrt(second / scalars[2]) + 1e-08) + 0.1 * weights
            weights_out[rows, :] = weights - 0.2 * update
            first_out[rows, :] = first
            second_out[rows, :] = second


def shift(amount):
    return [(i, (i + amount) % 4) for i in range(4)]


def shards(gradients, sign_table, loss_scale, step_count, weights, first_moment, second_moment):
    grads = gradients[0, 0]
    table = hadamard(BLOCK).astype(BF16)
    empty = jnp.zeros_like(table)
    twice = jnp.block([[table, empty], [empty, table]])
    signs = sign_table.astype(BF16)
    core = lax.axis_index("core")
    here = [lax.axis_index(axis) for axis in FIRST]

    place = core.reshape(1)
    raws, tops = [], []
    for third in range(3):
        raw, top = rotate_third(third, place, grads, signs, twice)
        raws.append(lax.ppermute(raw, "core", [(0, 1), (1, 0)]))
        tops.append(top)
    top_tile = pl.pallas_call(spread_kernel, out_shape=jax.ShapeDtypeStruct((128, 128), F32))(*tops)
    tops = lax.all_to_all(top_tile, ALL, 0, 0, tiled=True)

    parts = [[] for _ in range(3)]
    for offset in (2, 1, 3, 0):
        quarter = [lax.rem(h + offset, 4) for h in here]
        outs = levels_for(jnp.stack([core, *quarter]), grads, raws, signs, twice, tops)
        for third, out in enumerate(outs):
            parts[third].append(lax.ppermute(out, FIRST[third], shift(offset)) if offset else out)
    words = sum_four([part for third in parts for part in third])
    words = lax.all_to_all(words, CHIPS, 0, 0, tiled=True)

    top_value = jnp.max(tops)
    factor = top_value / (127.0 * 128.0 * loss_scale[0])
    steps_float = step_count[0].astype(F32)
    scalars = jnp.stack(
        [
            factor,
            1.0 - jnp.power(F32(0.9), steps_float),
            1.0 - jnp.power(F32(0.95), steps_float),
        ]
    )
    own_signs = lax.dynamic_slice_in_dim(sign_table, lax.axis_index("x") * BLOCK, BLOCK, 1)
    vmem = pl.BlockSpec(memory_space=pltpu.VMEM)
    return pl.pallas_call(
        update_kernel,
        in_specs=[pl.BlockSpec(memory_space=pltpu.SMEM)] + [vmem] * 6,
        out_specs=[vmem] * 3,
        out_shape=[jax.ShapeDtypeStruct((384, 128), F32)] * 3,
        compiler_params=pltpu.CompilerParams(vmem_limit_bytes=40 * 2**20),
    )(scalars, words.reshape(4, 4, 4, 48, 128), table, own_signs, weights, first_moment, second_moment)


def solution(mesh):
    torus = Mesh(mesh.devices.reshape(4, 4, 4, 2), ("x", "z", "y", "core"))
    owned = P(INTRA, "x")
    return jax.shard_map(
        shards,
        mesh=torus,
        in_specs=(P("x", INTRA, None, None), P(), P(), P(), owned, owned, owned),
        out_specs=(owned, owned, owned),
        check_vma=False,
    )
```

time: 325 us -> 122 us (0.38)
  waiting for transfers between devices: 157 us -> 42 us
  local copies, waits for them, and re-layouts: 73.7 us -> 1.39 us
  Pallas kernels: 0 us -> 44.3 us
  blocking collectives: 38 us -> 0 us
  starting transfers between devices: 0.08 us -> 28.5 us
  matrix products: 18.4 us -> 0 us
  other arithmetic: 18.8 us -> 1.96 us
  between operations: 16.8 us -> 2.82 us
    reduce_scatter x2 -> x0, waiting for transfers between devices: 157 us -> none  [the longest x1 136 us: shards(): lax.psum_scatter(jnp.floor(spun * level_scale + 0.5), INTRA, scatter_dime...]
    pallas_call x0 -> x10, Pallas kernels: none -> 44.3 us  [the longest x4 22.1 us: levels_for(): pl.pallas_call(level_kernel, grid_spec=pltpu.PrefetchScalarGridSpec(num_s...]
    pmax x4 -> x0, blocking collectives: 38 us -> none  [over_axes(): return functools.reduce(lax.pmax, axes, value)]
    all_to_all x0 -> x2, waiting for transfers between devices: none -> 27.3 us  [the longest x1 18.3 us: shards(): words = lax.all_to_all(words, CHIPS, 0, 0, tiled=True)]
    floor x1 -> x0, local copies, waits for them, and re-layouts: 27 us -> none  [shards(): jnp.floor(spun * level_scale + 0.5)]
    another operation x3 -> x0, local copies, waits for them, and re-layouts: 26.5 us -> none  [the longest x2 26.5 us: shards(): signed = (local_grad * jnp.tile(sign_half, (repeats, 1))).reshape(-1, BLOCK)]
    squeeze x1 -> x0, local copies, waits for them, and re-layouts: 20.2 us -> none  [shards(): local_grad = gradients[0, 0]]
    dot_general x2 -> x0, matrix products: 18.4 us -> none  [the longest x1 16.2 us: shards(): jnp.dot(signed, table_half, preferred_element_type=jnp.float32)]
  transfers between devices with their start and end apart: 2 -> 14, of which waited for: 2 -> 5; matrix products, arithmetic and copies ran while one was open for 0% -> 1% of each run, Pallas kernels for 0% -> 24%
where the time goes in v1:
time: 122 us; the launch traced here: 121 us
  Pallas kernels  44.3 us (36%)
  waiting for transfers between devices  42 us (34%)
  starting transfers between devices  28.5 us (23%)
  between operations  2.82 us (2%)
  other arithmetic  1.96 us (2%)
  local copies, waits for them, and re-layouts  1.39 us (1%)
    pallas_call x4, Pallas kernels, levels_for(): pl.pallas_call(level_kernel, grid_spec=pltpu.PrefetchScalarGridSpec(num_s...  22.1 us
    all_to_all x1, waiting for transfers between devices, shards(): words = lax.all_to_all(words, CHIPS, 0, 0, tiled=True)  18.3 us
    pallas_call x3, Pallas kernels, rotate_third(): pl.pallas_call(rotate_kernel, grid_spec=pltpu.PrefetchScalarGridSpec(num_...  16.9 us
    ppermute x9, waiting for transfers between devices, shards(): lax.ppermute(out, FIRST[third], shift(offset))  14.6 us
    all_to_all x1, starting transfers between devices, shards(): tops = lax.all_to_all(top_tile, ALL, 0, 0, tiled=True)  11.2 us
    ppermute x9, starting transfers between devices, shards(): lax.ppermute(out, FIRST[third], shift(offset))  10 us
    all_to_all x1, waiting for transfers between devices, shards(): tops = lax.all_to_all(top_tile, ALL, 0, 0, tiled=True)  9.06 us
    all_to_all x1, starting transfers between devices, shards(): words = lax.all_to_all(words, CHIPS, 0, 0, tiled=True)  6.71 us
  transfers between devices with their start and end apart: 14, of which 5 were waited for; matrix products, arithmetic and copies ran while one was open for 1% of the time, Pallas kernels for 24%

profile of v1, /device:TPU:0, one launch (start us, length us, event | category | flops | bytes accessed | tf_op | source)
XLA Modules:
  0.0 121.0 jit_solution(1549836013884755145)
XLA Ops:
  0.6 0.1 subtract_convert_fusion.table_ref
  0.7 0.9 convert_element_type.14.sign_ref.sign0.sign1.sign2
  1.6 5.6 %shard_map.94 = (f32[4,4,128,512]{3,2,1,0:T(8,128)}, f32[8,512]{1,0:T(8,128)S(1)}) custom-call(s32[1]{0:T(128)} %bitcast.place, bf16[4,4,2,3,128,512]{5,4,3,2,1,0:T(8,128)(2,1)} %bitcast.27, bf16[4,4,2,3,128,512]{5,4,3,2,1,0:T(8,128)(2,1)} %bitcast.28, bf16[64,512]{1,0:T(8,128)(2,1)S(1)} %convert_element_type.14.sign_ref.sign0.sign1.sign2, ...), custom_call_target="tpu_custom_call" | custom-call | flops 2000000000 | bytes 9000000 | tf_op jit(solution)/shard_map/pallas_call | solution.py:65
  7.3 0.0 collective-permute-start
  7.3 5.6 %shard_map.95 = (f32[4,4,128,512]{3,2,1,0:T(8,128)}, f32[8,512]{1,0:T(8,128)S(1)}) custom-call(s32[1]{0:T(128)} %bitcast.place, bf16[4,4,2,3,128,512]{5,4,3,2,1,0:T(8,128)(2,1)} %bitcast.29, bf16[4,4,2,3,128,512]{5,4,3,2,1,0:T(8,128)(2,1)} %bitcast.30, bf16[64,512]{1,0:T(8,128)(2,1)S(1)} %convert_element_type.14.sign_ref.sign0.sign1.sign2, ...), custom_call_target="tpu_custom_call" | custom-call | flops 2000000000 | bytes 9000000 | tf_op jit(solution)/shard_map/pallas_call | solution.py:65
  12.9 0.5 collective-permute-start.1
  13.4 5.7 %shard_map.96 = (f32[4,4,128,512]{3,2,1,0:T(8,128)}, f32[8,512]{1,0:T(8,128)S(1)}) custom-call(s32[1]{0:T(128)} %bitcast.place, bf16[4,4,2,3,128,512]{5,4,3,2,1,0:T(8,128)(2,1)} %bitcast.31, bf16[4,4,2,3,128,512]{5,4,3,2,1,0:T(8,128)(2,1)} %bitcast.32, bf16[64,512]{1,0:T(8,128)(2,1)S(1)} %convert_element_type.14.sign_ref.sign0.sign1.sign2, ...), custom_call_target="tpu_custom_call" | custom-call | flops 2000000000 | bytes 9000000 | tf_op jit(solution)/shard_map/pallas_call | solution.py:65
  19.1 0.6 copy-done.5
  19.7 0.1 collective-permute-start.2
  19.7 1.5 %shard_map.97 = f32[128,128]{1,0:T(8,128)} custom-call(f32[8,512]{1,0:T(8,128)} %copy-done.3, f32[8,512]{1,0:T(8,128)} %copy-done.4, f32[8,512]{1,0:T(8,128)} %copy-done.5), custom_call_target="tpu_custom_call" | custom-call | tf_op jit(solution)/shard_map/pallas_call | solution.py:209
  21.2 11.2 %all-to-all-start = ((f32[128,1,128]{2,1,0:T(1,128)}), f32[128,1,128]{2,1,0:T(1,128)S(1)}, u32[]{:S(2)}, u32[]{:S(2)}) async-start(f32[128,1,128]{2,1,0:T(1,128)} %bitcast.45), calls=%async_computation | async-start | bytes 131072 | tf_op jit(solution)/shard_map/all_to_all | solution.py:210
  32.5 0.1 pad_add_fusion.2
  32.5 0.1 pad_add_fusion
  32.6 9.1 %all-to-all-done = f32[128,1,128]{2,1,0:T(1,128)S(1)} async-done(((f32[128,1,128]{2,1,0:T(1,128)}), f32[128,1,128]{2,1,0:T(1,128)S(1)}, u32[]{:S(2)}, u32[]{:S(2)}) %all-to-all-start) | async-done | bytes 65568 | tf_op jit(solution)/shard_map/all_to_all | solution.py:210
  41.7 0.0 collective-permute-done.raw0
  41.7 0.0 collective-permute-done.1.raw1
  41.7 0.0 collective-permute-done.2.raw2
  41.7 5.5 %shard_map.100 = (f32[4,4,4,16,128]{4,3,2,1,0:T(8,128)S(1)}, f32[4,4,4,16,128]{4,3,2,1,0:T(8,128)S(1)}, f32[4,4,4,16,128]{4,3,2,1,0:T(8,128)S(1)}) custom-call(s32[4]{0:T(128)S(1)} %get-tuple-element.41.place, bf16[4,4,2,12,32,512]{5,4,3,2,1,0:T(8,128)(2,1)} %bitcast.33, bf16[4,4,2,12,32,512]{5,4,3,2,1,0:T(8,128)(2,1)} %bitcast.34, ...), custom_call_target="tpu_custom_call" | custom-call | flops 1000000000 | bytes 6000000 | tf_op jit(solution)/shard_map/pallas_call | solution.py:118
  47.2 0.9 collective-permute-start.11
  48.1 1.2 collective-permute-start.5
  49.2 0.8 collective-permute-start.8
  50.0 5.5 %shard_map.99 = (f32[4,4,4,16,128]{4,3,2,1,0:T(8,128)S(1)}, f32[4,4,4,16,128]{4,3,2,1,0:T(8,128)S(1)}, f32[4,4,4,16,128]{4,3,2,1,0:T(8,128)S(1)}) custom-call(s32[4]{0:T(128)S(1)} %get-tuple-element.40.place, bf16[4,4,2,12,32,512]{5,4,3,2,1,0:T(8,128)(2,1)} %bitcast.36, bf16[4,4,2,12,32,512]{5,4,3,2,1,0:T(8,128)(2,1)} %bitcast.37, ...), custom_call_target="tpu_custom_call" | custom-call | flops 1000000000 | bytes 6000000 | tf_op jit(solution)/shard_map/pallas_call | solution.py:118
  55.5 1.6 %collective-permute-start.10 = (f32[4,4,4,16,128]{4,3,2,1,0:T(8,128)S(1)}, f32[4,4,4,16,128]{4,3,2,1,0:T(8,128)S(1)}, u32[]{:S(2)}, u32[]{:S(2)}) collective-permute-start(f32[4,4,4,16,128]{4,3,2,1,0:T(8,128)S(1)} %get-tuple-element.36), channel_id=1, source_target_pairs={{0,8},{8,16},{16,24},{24,0},{1,9},{9,17},{17,25},{25,1},{2,10},{10... | collective-permute-start | bytes 1572872 | tf_op jit(solution)/shard_map/ppermute | solution.py:217
  57.2 0.9 collective-permute-start.4
  58.0 5.5 %shard_map.98 = (f32[4,4,4,16,128]{4,3,2,1,0:T(8,128)S(1)}, f32[4,4,4,16,128]{4,3,2,1,0:T(8,128)S(1)}, f32[4,4,4,16,128]{4,3,2,1,0:T(8,128)S(1)}) custom-call(s32[4]{0:T(128)S(1)} %get-tuple-element.39.place, bf16[4,4,2,12,32,512]{5,4,3,2,1,0:T(8,128)(2,1)} %bitcast.39, bf16[4,4,2,12,32,512]{5,4,3,2,1,0:T(8,128)(2,1)} %bitcast.40, ...), custom_call_target="tpu_custom_call" | custom-call | flops 1000000000 | bytes 6000000 | tf_op jit(solution)/shard_map/pallas_call | solution.py:118
  63.6 0.0 collective-permute-done.11.refs_10_
  63.6 1.0 collective-permute-start.7
  64.6 0.0 collective-permute-done.5.refs_2_
  64.6 1.1 collective-permute-start.3
  65.7 0.0 collective-permute-done.8.refs_6_
  65.7 1.4 %collective-permute-start.6 = (f32[4,4,4,16,128]{4,3,2,1,0:T(8,128)S(1)}, f32[4,4,4,16,128]{4,3,2,1,0:T(8,128)S(1)}, u32[]{:S(2)}, u32[]{:S(2)}) collective-permute-start(f32[4,4,4,16,128]{4,3,2,1,0:T(8,128)S(1)} %get-tuple-element.31), channel_id=1, source_target_pairs={{0,4},{2,6},{4,0},{6,2},{1,5},{3,7},{5,1},{7,3},{8,12},{10,14},{12... | collective-permute-start | bytes 1572872 | tf_op jit(solution)/shard_map/ppermute | solution.py:217
  67.1 2.6 %collective-permute-done.10.refs_9_ = f32[4,4,4,16,128]{4,3,2,1,0:T(8,128)S(1)} collective-permute-done((f32[4,4,4,16,128]{4,3,2,1,0:T(8,128)S(1)}, f32[4,4,4,16,128]{4,3,2,1,0:T(8,128)S(1)}, u32[]{:S(2)}, u32[]{:S(2)}) %collective-permute-start.10) | collective-permute-done | bytes 524320 | tf_op jit(solution)/shard_map/ppermute | solution.py:217
  69.7 1.2 %collective-permute-start.9 = (f32[4,4,4,16,128]{4,3,2,1,0:T(8,128)S(1)}, f32[4,4,4,16,128]{4,3,2,1,0:T(8,128)S(1)}, u32[]{:S(2)}, u32[]{:S(2)}) collective-permute-start(f32[4,4,4,16,128]{4,3,2,1,0:T(8,128)S(1)} %get-tuple-element.35), channel_id=1, source_target_pairs={{0,16},{8,24},{16,0},{24,8},{1,17},{9,25},{17,1},{25,9},{2,18},{10... | collective-permute-start | bytes 1572872 | tf_op jit(solution)/shard_map/ppermute | solution.py:217
  70.9 5.5 %shard_map.101 = (f32[4,4,4,16,128]{4,3,2,1,0:T(8,128)S(1)}, f32[4,4,4,16,128]{4,3,2,1,0:T(8,128)S(1)}, f32[4,4,4,16,128]{4,3,2,1,0:T(8,128)S(1)}) custom-call(s32[4]{0:T(128)S(1)} %get-tuple-element.42.place, bf16[4,4,2,12,32,512]{5,4,3,2,1,0:T(8,128)(2,1)} %bitcast.42, bf16[4,4,2,12,32,512]{5,4,3,2,1,0:T(8,128)(2,1)} %bitcast.43, ...), custom_call_target="tpu_custom_call" | custom-call | flops 1000000000 | bytes 6000000 | tf_op jit(solution)/shard_map/pallas_call | solution.py:118
  76.5 5.8 %collective-permute-done.4.refs_1_ = f32[4,4,4,16,128]{4,3,2,1,0:T(8,128)S(1)} collective-permute-done((f32[4,4,4,16,128]{4,3,2,1,0:T(8,128)S(1)}, f32[4,4,4,16,128]{4,3,2,1,0:T(8,128)S(1)}, u32[]{:S(2)}, u32[]{:S(2)}) %collective-permute-start.4) | collective-permute-done | bytes 524320 | tf_op jit(solution)/shard_map/ppermute | solution.py:217
  82.2 6.2 %collective-permute-done.7.refs_5_ = f32[4,4,4,16,128]{4,3,2,1,0:T(8,128)S(1)} collective-permute-done((f32[4,4,4,16,128]{4,3,2,1,0:T(8,128)S(1)}, f32[4,4,4,16,128]{4,3,2,1,0:T(8,128)S(1)}, u32[]{:S(2)}, u32[]{:S(2)}) %collective-permute-start.7) | collective-permute-done | bytes 524320 | tf_op jit(solution)/shard_map/ppermute | solution.py:217
  88.4 0.0 collective-permute-done.3.refs_0_
  88.4 0.0 collective-permute-done.6.refs_4_
  88.4 0.0 copy-start
  88.5 0.0 copy-start.1
  88.5 0.0 copy-start.2
  88.5 1.9 %shard_map.102 = f32[64,48,128]{2,1,0:T(8,128)} custom-call(f32[4,4,4,16,128]{4,3,2,1,0:T(8,128)S(1)} %collective-permute-done.3.refs_0_, f32[4,4,4,16,128]{4,3,2,1,0:T(8,128)S(1)} %collective-permute-done.4.refs_1_, f32[4,4,4,16,128]{4,3,2,1,0:T(8,128)S(1)} %collective-permute-done.5.refs_2_, f32[4,4,4,16,128]{4,3,2,1,0:T(8,128)S(1)} %get-tuple-element.30.refs_3_, ...), custom_call_target="tpu_custom_call" | custom-call | flops 1000000 | bytes 8000000 | tf_op jit(solution)/shard_map/pallas_call | solution.py:146
  90.3 6.7 %all-to-all-start.1 = ((f32[64,48,128]{2,1,0:T(8,128)}), f32[64,48,128]{2,1,0:T(8,128)S(1)}, u32[]{:S(2)}, u32[]{:S(2)}) async-start(f32[64,48,128]{2,1,0:T(8,128)} %shard_map.102), calls=%async_computation.1 | async-start | bytes 3145728 | tf_op jit(solution)/shard_map/all_to_all | solution.py:219
  98.4 0.8 constant_dynamic-slice_fusion.sign_ref
  99.2 0.7 reduce_max.9
  100.6 0.1 pad_maximum_fusion.scalars
  100.7 18.3 %all-to-all-done.1 = f32[64,48,128]{2,1,0:T(8,128)S(1)} async-done(((f32[64,48,128]{2,1,0:T(8,128)}), f32[64,48,128]{2,1,0:T(8,128)S(1)}, u32[]{:S(2)}, u32[]{:S(2)}) %all-to-all-start.1) | async-done | bytes 1572896 | tf_op jit(solution)/shard_map/all_to_all | solution.py:219
  119.0 2.0 %shard_map.103 = (f32[384,128]{1,0:T(8,128)}, f32[384,128]{1,0:T(8,128)}, f32[384,128]{1,0:T(8,128)}) custom-call(f32[3]{0:T(128)S(1)} %pad_maximum_fusion.scalars, f32[4,4,4,48,128]{4,3,2,1,0:T(8,128)S(1)} %bitcast.22, bf16[128,128]{1,0:T(8,128)(2,1)S(1)} %subtract_convert_fusion.table_ref, s32[64,128]{1,0:T(8,128)S(1)} %constant_dynamic-slice_fusion.sign_ref, ...), custom_call_target="tpu_custom_call" | custom-call | tf_op jit(solution)/shard_map/pallas_call | solution.py:233
  (10 shorter events, 0.0 us)
Async XLA Ops:
  7.3 5.6 %copy-start.3 = (f32[8,512]{1,0:T(8,128)}, f32[8,512]{1,0:T(8,128)S(1)}, u32[]{:S(2)}) copy-start(f32[8,512]{1,0:T(8,128)S(1)} %get-tuple-element.21.a_ref) | copy-start | bytes 49156
  7.3 34.4 %collective-permute-start = (f32[4,4,128,512]{3,2,1,0:T(8,128)}, f32[4,4,128,512]{3,2,1,0:T(8,128)}, u32[]{:S(2)}, u32[]{:S(2)}) collective-permute-start(f32[4,4,128,512]{3,2,1,0:T(8,128)} %get-tuple-element.24), channel_id=1, source_target_pairs={{0,1},{1,0},{2,3},{3,2},{4,5},{5,4},{6,7},{7,6},{8,9},{9,8},{10,11... | collective-permute-start | bytes 12582920 | tf_op jit(solution)/shard_map/ppermute | solution.py:207
  12.9 6.2 %copy-start.4 = (f32[8,512]{1,0:T(8,128)}, f32[8,512]{1,0:T(8,128)S(1)}, u32[]{:S(2)}) copy-start(f32[8,512]{1,0:T(8,128)S(1)} %get-tuple-element.22.b_ref) | copy-start | bytes 49156
  12.9 28.8 %collective-permute-start.1 = (f32[4,4,128,512]{3,2,1,0:T(8,128)}, f32[4,4,128,512]{3,2,1,0:T(8,128)}, u32[]{:S(2)}, u32[]{:S(2)}) collective-permute-start(f32[4,4,128,512]{3,2,1,0:T(8,128)} %get-tuple-element.25), channel_id=1, source_target_pairs={{0,1},{1,0},{2,3},{3,2},{4,5},{5,4},{6,7},{7,6},{8,9},{9,8},{10,11... | collective-permute-start | bytes 12582920 | tf_op jit(solution)/shard_map/ppermute | solution.py:207
  19.1 0.6 copy-start.5
  19.7 22.0 %collective-permute-start.2 = (f32[4,4,128,512]{3,2,1,0:T(8,128)}, f32[4,4,128,512]{3,2,1,0:T(8,128)}, u32[]{:S(2)}, u32[]{:S(2)}) collective-permute-start(f32[4,4,128,512]{3,2,1,0:T(8,128)} %get-tuple-element.26), channel_id=1, source_target_pairs={{0,1},{1,0},{2,3},{3,2},{4,5},{5,4},{6,7},{7,6},{8,9},{9,8},{10,11... | collective-permute-start | bytes 12582920 | tf_op jit(solution)/shard_map/ppermute | solution.py:207
  21.2 20.4 %all-to-all-start = ((f32[128,1,128]{2,1,0:T(1,128)}), f32[128,1,128]{2,1,0:T(1,128)S(1)}, u32[]{:S(2)}, u32[]{:S(2)}) async-start(f32[128,1,128]{2,1,0:T(1,128)} %bitcast.45), calls=%async_computation | async-start | bytes 131072 | tf_op jit(solution)/shard_map/all_to_all | solution.py:210
  47.2 16.4 %collective-permute-start.11 = (f32[4,4,4,16,128]{4,3,2,1,0:T(8,128)S(1)}, f32[4,4,4,16,128]{4,3,2,1,0:T(8,128)S(1)}, u32[]{:S(2)}, u32[]{:S(2)}) collective-permute-start(f32[4,4,4,16,128]{4,3,2,1,0:T(8,128)S(1)} %get-tuple-element.37), channel_id=1, source_target_pairs={{0,24},{8,0},{16,8},{24,16},{1,25},{9,1},{17,9},{25,17},{2,26},{10... | collective-permute-start | bytes 1572872 | tf_op jit(solution)/shard_map/ppermute | solution.py:217
  48.1 16.5 %collective-permute-start.5 = (f32[4,4,4,16,128]{4,3,2,1,0:T(8,128)S(1)}, f32[4,4,4,16,128]{4,3,2,1,0:T(8,128)S(1)}, u32[]{:S(2)}, u32[]{:S(2)}) collective-permute-start(f32[4,4,4,16,128]{4,3,2,1,0:T(8,128)S(1)} %get-tuple-element.29), channel_id=1, source_target_pairs={{0,96},{32,0},{64,32},{96,64},{1,97},{33,1},{65,33},{97,65},{2,98}... | collective-permute-start | bytes 1572872 | tf_op jit(solution)/shard_map/ppermute | solution.py:217
  49.2 16.4 %collective-permute-start.8 = (f32[4,4,4,16,128]{4,3,2,1,0:T(8,128)S(1)}, f32[4,4,4,16,128]{4,3,2,1,0:T(8,128)S(1)}, u32[]{:S(2)}, u32[]{:S(2)}) collective-permute-start(f32[4,4,4,16,128]{4,3,2,1,0:T(8,128)S(1)} %get-tuple-element.33), channel_id=1, source_target_pairs={{0,6},{2,0},{4,2},{6,4},{1,7},{3,1},{5,3},{7,5},{8,14},{10,8},{12,... | collective-permute-start | bytes 1572872 | tf_op jit(solution)/shard_map/ppermute | solution.py:217
  55.5 14.2 %collective-permute-start.10 = (f32[4,4,4,16,128]{4,3,2,1,0:T(8,128)S(1)}, f32[4,4,4,16,128]{4,3,2,1,0:T(8,128)S(1)}, u32[]{:S(2)}, u32[]{:S(2)}) collective-permute-start(f32[4,4,4,16,128]{4,3,2,1,0:T(8,128)S(1)} %get-tuple-element.36), channel_id=1, source_target_pairs={{0,8},{8,16},{16,24},{24,0},{1,9},{9,17},{17,25},{25,1},{2,10},{10... | collective-permute-start | bytes 1572872 | tf_op jit(solution)/shard_map/ppermute | solution.py:217
  57.2 25.1 %collective-permute-start.4 = (f32[4,4,4,16,128]{4,3,2,1,0:T(8,128)S(1)}, f32[4,4,4,16,128]{4,3,2,1,0:T(8,128)S(1)}, u32[]{:S(2)}, u32[]{:S(2)}) collective-permute-start(f32[4,4,4,16,128]{4,3,2,1,0:T(8,128)S(1)} %get-tuple-element.28), channel_id=1, source_target_pairs={{0,32},{32,64},{64,96},{96,0},{1,33},{33,65},{65,97},{97,1},{2,34}... | collective-permute-start | bytes 1572872 | tf_op jit(solution)/shard_map/ppermute | solution.py:217
  63.6 24.8 %collective-permute-start.7 = (f32[4,4,4,16,128]{4,3,2,1,0:T(8,128)S(1)}, f32[4,4,4,16,128]{4,3,2,1,0:T(8,128)S(1)}, u32[]{:S(2)}, u32[]{:S(2)}) collective-permute-start(f32[4,4,4,16,128]{4,3,2,1,0:T(8,128)S(1)} %get-tuple-element.32), channel_id=1, source_target_pairs={{0,2},{2,4},{4,6},{6,0},{1,3},{3,5},{5,7},{7,1},{8,10},{10,12},{12... | collective-permute-start | bytes 1572872 | tf_op jit(solution)/shard_map/ppermute | solution.py:217
  64.6 23.9 %collective-permute-start.3 = (f32[4,4,4,16,128]{4,3,2,1,0:T(8,128)S(1)}, f32[4,4,4,16,128]{4,3,2,1,0:T(8,128)S(1)}, u32[]{:S(2)}, u32[]{:S(2)}) collective-permute-start(f32[4,4,4,16,128]{4,3,2,1,0:T(8,128)S(1)} %get-tuple-element.27), channel_id=1, source_target_pairs={{0,64},{32,96},{64,0},{96,32},{1,65},{33,97},{65,1},{97,33},{2,66}... | collective-permute-start | bytes 1572872 | tf_op jit(solution)/shard_map/ppermute | solution.py:217
  65.7 22.8 %collective-permute-start.6 = (f32[4,4,4,16,128]{4,3,2,1,0:T(8,128)S(1)}, f32[4,4,4,16,128]{4,3,2,1,0:T(8,128)S(1)}, u32[]{:S(2)}, u32[]{:S(2)}) collective-permute-start(f32[4,4,4,16,128]{4,3,2,1,0:T(8,128)S(1)} %get-tuple-element.31), channel_id=1, source_target_pairs={{0,4},{2,6},{4,0},{6,2},{1,5},{3,7},{5,1},{7,3},{8,12},{10,14},{12... | collective-permute-start | bytes 1572872 | tf_op jit(solution)/shard_map/ppermute | solution.py:217
  69.7 18.7 %collective-permute-start.9 = (f32[4,4,4,16,128]{4,3,2,1,0:T(8,128)S(1)}, f32[4,4,4,16,128]{4,3,2,1,0:T(8,128)S(1)}, u32[]{:S(2)}, u32[]{:S(2)}) collective-permute-start(f32[4,4,4,16,128]{4,3,2,1,0:T(8,128)S(1)} %get-tuple-element.35), channel_id=1, source_target_pairs={{0,16},{8,24},{16,0},{24,8},{1,17},{9,25},{17,1},{25,9},{2,18},{10... | collective-permute-start | bytes 1572872 | tf_op jit(solution)/shard_map/ppermute | solution.py:217
  88.4 30.5 %copy-start = (f32[384,128]{1,0:T(8,128)S(1)}, f32[384,128]{1,0:T(8,128)}, u32[]{:S(2)}) copy-start(f32[384,128]{1,0:T(8,128)} %weights_ref.1) | copy-start | bytes 589828
  88.5 30.5 %copy-start.1 = (f32[384,128]{1,0:T(8,128)S(1)}, f32[384,128]{1,0:T(8,128)}, u32[]{:S(2)}) copy-start(f32[384,128]{1,0:T(8,128)} %first_ref.1) | copy-start | bytes 589828
  88.5 30.5 %copy-start.2 = (f32[384,128]{1,0:T(8,128)S(1)}, f32[384,128]{1,0:T(8,128)}, u32[]{:S(2)}) copy-start(f32[384,128]{1,0:T(8,128)} %second_ref.1) | copy-start | bytes 589828
  90.3 28.6 %all-to-all-start.1 = ((f32[64,48,128]{2,1,0:T(8,128)}), f32[64,48,128]{2,1,0:T(8,128)S(1)}, u32[]{:S(2)}, u32[]{:S(2)}) async-start(f32[64,48,128]{2,1,0:T(8,128)} %shard_map.102), calls=%async_computation.1 | async-start | bytes 3145728 | tf_op jit(solution)/shard_map/all_to_all | solution.py:219

commit v2 on v1

v2 whole, which is shorter than its diff:
```python
import functools
import math

import jax
import jax.numpy as jnp
import numpy as np
from jax import lax
from jax.experimental import pallas as pl
from jax.experimental.pallas import tpu as pltpu
from jax.sharding import Mesh
from jax.sharding import PartitionSpec as P

BLOCK = 128
SIGN_ROWS = 64
ROOT = 1.0 / math.sqrt(BLOCK)
CHIPS = ("x", "z", "y")
ALL = ("x", "z", "y", "core")
INTRA = ("z", "y", "core")
FIRST = ("x", "y", "z")
FIELD = 4096.0
F32 = jnp.float32
BF16 = jnp.bfloat16


def hadamard(order):
    table = np.ones((1, 1), np.float32)
    while table.shape[0] < order:
        table = np.block([[table, table], [table, -table]])
    return table


def rotate_kernel(grads_ref, sign_ref, table_ref, raw0, raw1, raw2, own_ref, top_ref, buffer, sems):
    core = lax.axis_index("core")
    copies = [pltpu.make_async_copy(grads_ref.at[i], buffer.at[i], sems.at[i]) for i in range(16)]
    for copy in copies:
        copy.start()
    signs = sign_ref[...].astype(F32).astype(BF16)
    table = table_ref[...]

    def fold(value):
        return jnp.max(jnp.abs(value).reshape(-1, 8, 256), axis=0)

    best = jnp.zeros((8, 256), F32)
    for i in range(16):
        copies[i].wait()

        for third, raw_ref in enumerate((raw0, raw1, raw2)):
            rows = pl.ds(128 * third, 128)
            wide = jnp.concatenate([signs, signs], axis=0)
            mine = buffer[i, core, rows, :] * wide
            own_ref[i, rows, :] = mine
            other = buffer[i, 1 - core, rows, :] * wide
            block = jnp.concatenate([v[:, 256 * h : 256 * h + 256] for v in (other, mine) for h in range(2)], axis=0)
            turned = jnp.dot(block, table, preferred_element_type=F32) * ROOT
            raw_ref[i, :, :256] = turned[:128]
            raw_ref[i, :, 256:] = turned[128:256]
            best = jnp.maximum(best, fold(turned))
    top_ref[...] = jnp.broadcast_to(jnp.max(best, axis=(0, 1), keepdims=True), (128, 128))


VMEM = pl.BlockSpec(memory_space=pltpu.VMEM)


def rotate_all(grads, signs, table):
    return pl.pallas_call(
        rotate_kernel,
        in_specs=[pl.BlockSpec(memory_space=pl.ANY), VMEM, VMEM],
        out_specs=[VMEM] * 5,
        out_shape=[pltpu.VMEM((16, 128, 512), F32)] * 3
        + [
            pltpu.VMEM((16, 384, 512), BF16),
            jax.ShapeDtypeStruct((128, 128), F32),
        ],
        scratch_shapes=[pltpu.VMEM((16, 2, 384, 512), BF16), pltpu.SemaphoreType.DMA((16,))],
        compiler_params=pltpu.CompilerParams(vmem_limit_bytes=40 * 2**20),
        cost_estimate=pl.CostEstimate(flops=6 * 10**9, bytes_accessed=12 * 10**6, transcendentals=0),
    )(grads.reshape(16, 2, 384, 512), signs, table)


def level_kernel(offset, own_ref, raw0, raw1, raw2, table_ref, top_ref, *outs):
    table = table_ref[...]
    scale = 127.0 / jnp.max(top_ref[...], axis=(0, 1), keepdims=True)
    ahead = jnp.where(lax.axis_index("core") == 0, offset, 4 - offset)
    quarters = [lax.rem(lax.axis_index(axis) + ahead, 4) for axis in FIRST]
    raws = (raw0, raw1, raw2)

    def plane(z, carry):
        blocks = [own_ref[4 * z + y, 4 * t + quarters[t]] for t in range(3) for y in range(4)]
        stacked = jnp.concatenate([v[:, 256 * h : 256 * h + 256] for v in blocks for h in range(2)], axis=0)
        mine = jnp.dot(stacked, table, preferred_element_type=F32) * ROOT
        mine = jnp.floor(mine * scale + 0.5)
        for t in range(3):
            for y in range(4):
                for h in range(2):
                    row = 32 * ((t * 4 + y) * 2 + h)
                    other = raws[t][4 * z + y, quarters[t], :, 256 * h : 256 * h + 256]
                    total = mine[row : row + 32] + jnp.floor(other * scale + 0.5)
                    word = total[:16] + FIELD * total[16:]
                    for x in range(2):
                        outs[t][2 * h + x, z, y] = word[:, 128 * x : 128 * x + 128]
        return carry

    lax.fori_loop(0, 4, plane, 0)


def levels_for(offset, own, raws, table, tops):
    return pl.pallas_call(
        functools.partial(level_kernel, offset),
        in_specs=[VMEM] * 6,
        out_specs=[VMEM] * 3,
        out_shape=[pltpu.VMEM((4, 4, 4, 16, 128), F32)] * 3,
        compiler_params=pltpu.CompilerParams(vmem_limit_bytes=12 * 2**20),
        cost_estimate=pl.CostEstimate(flops=10**9, bytes_accessed=6 * 10**6, transcendentals=0),
    )(own.reshape(16, 12, 32, 512), *[raw.reshape(16, 4, 32, 512) for raw in raws], table, tops)


def gather_kernel(*refs):
    out = refs[-1]

    def some(i, carry):
        for t in range(3):
            a, b, c, d = (refs[4 * t + k][pl.ds(8 * i, 8)] for k in range(4))
            out[pl.ds(8 * i, 8), 16 * t : 16 * t + 16, :] = (a + b) + (c + d)
        return carry

    lax.fori_loop(0, 8, some, 0)


def sum_four(parts):
    return pl.pallas_call(
        gather_kernel,
        in_specs=[VMEM] * 12,
        out_specs=VMEM,
        out_shape=pltpu.VMEM((64, 48, 128), F32),
        compiler_params=pltpu.CompilerParams(vmem_limit_bytes=12 * 2**20),
        cost_estimate=pl.CostEstimate(flops=10**6, bytes_accessed=8 * 10**6, transcendentals=0),
    )(*[part.reshape(64, 16, 128) for part in parts])


def update_kernel(
    scalars, words_ref, table_ref, sign_ref, weights_ref, first_ref, second_ref, weights_out, first_out, second_out
):
    table = table_ref[...]
    for t in range(3):
        for q in range(4):
            parts = []
            for a in range(4):
                for b in range(4):
                    x, z, y = ((q, a, b), (a, b, q), (a, q, b))[t]
                    parts.append(words_ref[x, z, y, 16 * t : 16 * t + 16, :])
            low = high = jnp.zeros((16, 128), F32)
            for word in parts:
                upper = jnp.floor(word * (1.0 / FIELD) + 0.5)
                high = high + upper
                low = low + (word - upper * FIELD)
            total = jnp.concatenate([low, high], axis=0)
            coarse = jnp.floor(total * (1.0 / 128.0) + 0.5)
            fine = total - coarse * 128.0
            back = 128.0 * jnp.dot(coarse.astype(BF16), table, preferred_element_type=F32) + jnp.dot(
                fine.astype(BF16), table, preferred_element_type=F32
            )
            rows = pl.ds(128 * t + 32 * q, 32)
            grad = (back * scalars[0]) * ROOT * sign_ref[pl.ds(32 * (q % 2), 32), :].astype(F32)
            first = 0.9 * first_ref[rows, :] + 0.1 * grad
            second = 0.95 * second_ref[rows, :] + 0.05 * grad * grad
            weights = weights_ref[rows, :]
            update = (first / scalars[1]) / (jnp.sqrt(second / scalars[2]) + 1e-08) + 0.1 * weights
            weights_out[rows, :] = weights - 0.2 * update
            first_out[rows, :] = first
            second_out[rows, :] = second


def shift(amount):
    return [
        (2 * i + core, 2 * ((i + (amount if core == 0 else -amount)) % 4) + core)
        for i in range(4)
        for core in range(2)
    ]


def shards(gradients, sign_table, loss_scale, step_count, weights, first_moment, second_moment):
    grads = gradients[0, 0]
    table = jnp.asarray(hadamard(BLOCK), BF16)
    twice = jnp.asarray(np.kron(np.eye(2, dtype=np.float32), hadamard(BLOCK)), BF16)
    *raws, own, top_tile = rotate_all(grads, sign_table, twice)
    raws = [lax.ppermute(raw, "core", [(0, 1), (1, 0)]) for raw in raws]
    tops = lax.all_to_all(top_tile, ALL, 0, 0, tiled=True)

    parts = [[] for _ in range(3)]
    for offset in (1, 3, 2, 0):
        outs = levels_for(offset, own, raws, twice, tops)
        for third, out in enumerate(outs):
            parts[third].append(lax.ppermute(out, (FIRST[third], "core"), shift(offset)) if offset else out)
    words = sum_four([part for third in parts for part in third])
    words = lax.all_to_all(words, CHIPS, 0, 0, tiled=True)

    top_value = jnp.max(tops)
    factor = top_value / (127.0 * 128.0 * loss_scale[0])
    steps_float = step_count[0].astype(F32)
    scalars = jnp.stack(
        [
            factor,
            1.0 - jnp.power(F32(0.9), steps_float),
            1.0 - jnp.power(F32(0.95), steps_float),
        ]
    )
    own_signs = lax.dynamic_slice_in_dim(sign_table, lax.axis_index("x") * BLOCK, BLOCK, 1)
    return pl.pallas_call(
        update_kernel,
        in_specs=[pl.BlockSpec(memory_space=pltpu.SMEM)] + [VMEM] * 6,
        out_specs=[VMEM] * 3,
        out_shape=[jax.ShapeDtypeStruct((384, 128), F32)] * 3,
        compiler_params=pltpu.CompilerParams(vmem_limit_bytes=40 * 2**20),
    )(scalars, words.reshape(4, 4, 4, 48, 128), table, own_signs, weights, first_moment, second_moment)


def solution(mesh):
    torus = Mesh(mesh.devices.reshape(4, 4, 4, 2), ("x", "z", "y", "core"))
    owned = P(INTRA, "x")
    return jax.shard_map(
        shards,
        mesh=torus,
        in_specs=(P("x", INTRA, None, None), P(), P(), P(), owned, owned, owned),
        out_specs=(owned, owned, owned),
        check_vma=False,
    )
```

time: 122 us -> 103 us (0.84)
  Pallas kernels: 44.3 us -> 20.5 us
  blocking collectives: 0 us -> 20.4 us
  waiting for transfers between devices: 42 us -> 32.2 us
  starting transfers between devices: 28.5 us -> 25.6 us
    pallas_call x9 -> x6, Pallas kernels: 42.4 us -> 18.5 us  [the longest x1 9.83 us: rotate_all(): pl.pallas_call(rotate_kernel, in_specs=[pl.BlockSpec(memory_space=pl.ANY)...]
    all_to_all x0 -> x1, blocking collectives: none -> 20.4 us  [shards(): tops = lax.all_to_all(top_tile, ALL, 0, 0, tiled=True)]
    all_to_all x1 -> x0, starting transfers between devices: 11.2 us -> none  [shards(): tops = lax.all_to_all(top_tile, ALL, 0, 0, tiled=True)]
    all_to_all x1 -> x0, waiting for transfers between devices: 9.06 us -> none  [shards(): tops = lax.all_to_all(top_tile, ALL, 0, 0, tiled=True)]
    ppermute x12, starting transfers between devices: 10.6 us -> 16.1 us  [the longest x9 15.5 us: shards(): lax.ppermute(out, (FIRST[third], 'core'), shift(offset))]
    ppermute x12, waiting for transfers between devices: 14.6 us -> 11.1 us  [the longest x9 11.1 us: shards(): lax.ppermute(out, (FIRST[third], 'core'), shift(offset))]
    all_to_all x1, starting transfers between devices: 6.71 us -> 9.49 us  [shards(): words = lax.all_to_all(words, CHIPS, 0, 0, tiled=True)]
    all_to_all x1, waiting for transfers between devices: 18.3 us -> 21 us  [shards(): words = lax.all_to_all(words, CHIPS, 0, 0, tiled=True)]
  transfers between devices with their start and end apart: 14 -> 13, of which waited for: 5 -> 6; matrix products, arithmetic and copies ran while one was open for 1% -> 2% of each run, Pallas kernels for 24% -> 5%
where the time goes in v2:
time: 103 us
  waiting for transfers between devices  32.2 us (31%)
  starting transfers between devices  25.6 us (25%)
  Pallas kernels  20.5 us (20%)
  blocking collectives  20.4 us (20%)
  between operations  2.78 us (3%)
    all_to_all x1, waiting for transfers between devices, shards(): words = lax.all_to_all(words, CHIPS, 0, 0, tiled=True)  21 us
    all_to_all x1, blocking collectives, shards(): tops = lax.all_to_all(top_tile, ALL, 0, 0, tiled=True)  20.4 us
    ppermute x9, starting transfers between devices, shards(): lax.ppermute(out, (FIRST[third], 'core'), shift(offset))  15.5 us
    ppermute x9, waiting for transfers between devices, shards(): lax.ppermute(out, (FIRST[third], 'core'), shift(offset))  11.1 us
    pallas_call x1, Pallas kernels, rotate_all(): pl.pallas_call(rotate_kernel, in_specs=[pl.BlockSpec(memory_space=pl.ANY)...  9.83 us
    all_to_all x1, starting transfers between devices, shards(): words = lax.all_to_all(words, CHIPS, 0, 0, tiled=True)  9.49 us
    pallas_call x4, Pallas kernels, levels_for(): pl.pallas_call(functools.partial(level_kernel, offset), in_specs=[VMEM] *...  7.19 us
  transfers between devices with their start and end apart: 13, of which 6 were waited for; matrix products, arithmetic and copies ran while one was open for 2% of the time, Pallas kernels for 5%

profile of v2, /device:TPU:0, one launch (start us, length us, event | category | flops | bytes accessed | tf_op | source)
XLA Modules:
  0.0 103.1 jit_solution(5314401190072702877)
XLA Ops:
  0.6 0.0 copy-start
  0.6 9.8 %shard_map.112 = (f32[16,128,512]{2,1,0:T(8,128)S(1)}, f32[16,128,512]{2,1,0:T(8,128)S(1)}, f32[16,128,512]{2,1,0:T(8,128)S(1)}, bf16[16,384,512]{2,1,0:T(8,128)(2,1)S(1)}, f32[128,128]{1,0:T(8,128)}) custom-call(bf16[16,2,384,512]{3,2,1,0:T(8,128)(2,1)} %bitcast.58, s32[64,512]{1,0:T(8,128)} %sign_ref.1, bf16[256,256]{1,0:T(8,128)(2,1)} %constant.32.clone.table_ref), custom_call_target="tpu_custom_call" | custom-call | flops 6000000000 | bytes 12000000 | tf_op jit(solution)/shard_map/pallas_call | solution.py:65
  10.5 0.1 collective-permute-start
  10.6 0.5 collective-permute-start.1
  11.1 0.1 collective-permute-start.2
  11.2 20.4 %all_to_all.16 = f32[128,1,128]{2,1,0:T(1,128)S(1)} all-to-all(f32[128,1,128]{2,1,0:T(1,128)} %bitcast.57), channel_id=1, replica_groups=mesh['x'=4,'z'=4,'y'=4,'core'=2] {'x','z','y','core'}, dimensions={0} | all-to-all | bytes 131072 | tf_op jit(solution)/shard_map/all_to_all | solution.py:187
  31.6 0.0 collective-permute-done
  31.6 0.0 collective-permute-done.1
  31.6 0.0 collective-permute-done.2
  31.6 0.0 copy-done
  31.6 1.8 %shard_map.115 = (f32[4,4,4,16,128]{4,3,2,1,0:T(8,128)S(1)}, f32[4,4,4,16,128]{4,3,2,1,0:T(8,128)S(1)}, f32[4,4,4,16,128]{4,3,2,1,0:T(8,128)S(1)}) custom-call(bf16[16,12,32,512]{3,2,1,0:T(8,128)(2,1)S(1)} %bitcast.24, f32[16,4,32,512]{3,2,1,0:T(8,128)S(1)} %bitcast.28, f32[16,4,32,512]{3,2,1,0:T(8,128)S(1)} %bitcast.32, f32[16,4,32,512]{3,2,1,0:T(8,128)S(1)} %bitcast.36, ...), custom_call_target="tpu_custom_call" | custom-call | flops 1000000000 | bytes 6000000 | tf_op jit(solution)/shard_map/pallas_call | solution.py:107
  33.4 1.3 %collective-permute-start.5 = (f32[4,4,4,16,128]{4,3,2,1,0:T(8,128)S(1)}, f32[4,4,4,16,128]{4,3,2,1,0:T(8,128)S(1)}, u32[]{:S(2)}, u32[]{:S(2)}) collective-permute-start(f32[4,4,4,16,128]{4,3,2,1,0:T(8,128)S(1)} %get-tuple-element.27), channel_id=1, source_target_pairs={{0,64},{1,65},{32,96},{33,97},{64,0},{65,1},{96,32},{97,33},{2,66}... | collective-permute-start | bytes 1572872 | tf_op jit(solution)/shard_map/ppermute | solution.py:193
  34.7 3.2 %collective-permute-start.8 = (f32[4,4,4,16,128]{4,3,2,1,0:T(8,128)S(1)}, f32[4,4,4,16,128]{4,3,2,1,0:T(8,128)S(1)}, u32[]{:S(2)}, u32[]{:S(2)}) collective-permute-start(f32[4,4,4,16,128]{4,3,2,1,0:T(8,128)S(1)} %get-tuple-element.31), channel_id=1, source_target_pairs={{0,4},{1,5},{2,6},{3,7},{4,0},{5,1},{6,2},{7,3},{8,12},{9,13},{10,... | collective-permute-start | bytes 1572872 | tf_op jit(solution)/shard_map/ppermute | solution.py:193
  37.9 3.9 %collective-permute-start.11 = (f32[4,4,4,16,128]{4,3,2,1,0:T(8,128)S(1)}, f32[4,4,4,16,128]{4,3,2,1,0:T(8,128)S(1)}, u32[]{:S(2)}, u32[]{:S(2)}) collective-permute-start(f32[4,4,4,16,128]{4,3,2,1,0:T(8,128)S(1)} %get-tuple-element.35), channel_id=1, source_target_pairs={{0,16},{1,17},{8,24},{9,25},{16,0},{17,1},{24,8},{25,9},{2,18},{3,... | collective-permute-start | bytes 1572872 | tf_op jit(solution)/shard_map/ppermute | solution.py:193
  41.8 1.8 %shard_map.114 = (f32[4,4,4,16,128]{4,3,2,1,0:T(8,128)S(1)}, f32[4,4,4,16,128]{4,3,2,1,0:T(8,128)S(1)}, f32[4,4,4,16,128]{4,3,2,1,0:T(8,128)S(1)}) custom-call(bf16[16,12,32,512]{3,2,1,0:T(8,128)(2,1)S(1)} %bitcast.25, f32[16,4,32,512]{3,2,1,0:T(8,128)S(1)} %bitcast.29, f32[16,4,32,512]{3,2,1,0:T(8,128)S(1)} %bitcast.33, f32[16,4,32,512]{3,2,1,0:T(8,128)S(1)} %bitcast.37, ...), custom_call_target="tpu_custom_call" | custom-call | flops 1000000000 | bytes 6000000 | tf_op jit(solution)/shard_map/pallas_call | solution.py:107
  43.6 1.3 %collective-permute-start.4 = (f32[4,4,4,16,128]{4,3,2,1,0:T(8,128)S(1)}, f32[4,4,4,16,128]{4,3,2,1,0:T(8,128)S(1)}, u32[]{:S(2)}, u32[]{:S(2)}) collective-permute-start(f32[4,4,4,16,128]{4,3,2,1,0:T(8,128)S(1)} %get-tuple-element.26), channel_id=1, source_target_pairs={{0,96},{1,33},{32,0},{33,65},{64,32},{65,97},{96,64},{97,1},{2,98}... | collective-permute-start | bytes 1572872 | tf_op jit(solution)/shard_map/ppermute | solution.py:193
  44.8 1.1 %collective-permute-start.7 = (f32[4,4,4,16,128]{4,3,2,1,0:T(8,128)S(1)}, f32[4,4,4,16,128]{4,3,2,1,0:T(8,128)S(1)}, u32[]{:S(2)}, u32[]{:S(2)}) collective-permute-start(f32[4,4,4,16,128]{4,3,2,1,0:T(8,128)S(1)} %get-tuple-element.30), channel_id=1, source_target_pairs={{0,6},{1,3},{2,0},{3,5},{4,2},{5,7},{6,4},{7,1},{8,14},{9,11},{10,... | collective-permute-start | bytes 1572872 | tf_op jit(solution)/shard_map/ppermute | solution.py:193
  45.9 1.8 %shard_map.113 = (f32[4,4,4,16,128]{4,3,2,1,0:T(8,128)S(1)}, f32[4,4,4,16,128]{4,3,2,1,0:T(8,128)S(1)}, f32[4,4,4,16,128]{4,3,2,1,0:T(8,128)S(1)}) custom-call(bf16[16,12,32,512]{3,2,1,0:T(8,128)(2,1)S(1)} %bitcast.26, f32[16,4,32,512]{3,2,1,0:T(8,128)S(1)} %bitcast.30, f32[16,4,32,512]{3,2,1,0:T(8,128)S(1)} %bitcast.34, f32[16,4,32,512]{3,2,1,0:T(8,128)S(1)} %bitcast.38, ...), custom_call_target="tpu_custom_call" | custom-call | flops 1000000000 | bytes 6000000 | tf_op jit(solution)/shard_map/pallas_call | solution.py:107
  47.7 2.1 %collective-permute-done.5 = f32[4,4,4,16,128]{4,3,2,1,0:T(8,128)S(1)} collective-permute-done((f32[4,4,4,16,128]{4,3,2,1,0:T(8,128)S(1)}, f32[4,4,4,16,128]{4,3,2,1,0:T(8,128)S(1)}, u32[]{:S(2)}, u32[]{:S(2)}) %collective-permute-start.5) | collective-permute-done | bytes 524320 | tf_op jit(solution)/shard_map/ppermute | solution.py:193
  49.8 2.2 %collective-permute-start.10 = (f32[4,4,4,16,128]{4,3,2,1,0:T(8,128)S(1)}, f32[4,4,4,16,128]{4,3,2,1,0:T(8,128)S(1)}, u32[]{:S(2)}, u32[]{:S(2)}) collective-permute-start(f32[4,4,4,16,128]{4,3,2,1,0:T(8,128)S(1)} %get-tuple-element.34), channel_id=1, source_target_pairs={{0,24},{1,9},{8,0},{9,17},{16,8},{17,25},{24,16},{25,1},{2,26},{3,... | collective-permute-start | bytes 1572872 | tf_op jit(solution)/shard_map/ppermute | solution.py:193
  52.0 0.0 collective-permute-done.8
  52.1 0.7 collective-permute-start.3
  52.8 1.5 %collective-permute-done.11 = f32[4,4,4,16,128]{4,3,2,1,0:T(8,128)S(1)} collective-permute-done((f32[4,4,4,16,128]{4,3,2,1,0:T(8,128)S(1)}, f32[4,4,4,16,128]{4,3,2,1,0:T(8,128)S(1)}, u32[]{:S(2)}, u32[]{:S(2)}) %collective-permute-start.11) | collective-permute-done | bytes 524320 | tf_op jit(solution)/shard_map/ppermute | solution.py:193
  54.3 0.6 collective-permute-start.6
  54.8 0.0 collective-permute-done.4
  54.8 1.3 %collective-permute-start.9 = (f32[4,4,4,16,128]{4,3,2,1,0:T(8,128)S(1)}, f32[4,4,4,16,128]{4,3,2,1,0:T(8,128)S(1)}, u32[]{:S(2)}, u32[]{:S(2)}) collective-permute-start(f32[4,4,4,16,128]{4,3,2,1,0:T(8,128)S(1)} %get-tuple-element.33), channel_id=1, source_target_pairs={{0,8},{1,25},{8,16},{9,1},{16,24},{17,9},{24,0},{25,17},{2,10},{3,... | collective-permute-start | bytes 1572872 | tf_op jit(solution)/shard_map/ppermute | solution.py:193
  56.1 1.8 %shard_map.116 = (f32[4,4,4,16,128]{4,3,2,1,0:T(8,128)S(1)}, f32[4,4,4,16,128]{4,3,2,1,0:T(8,128)S(1)}, f32[4,4,4,16,128]{4,3,2,1,0:T(8,128)S(1)}) custom-call(bf16[16,12,32,512]{3,2,1,0:T(8,128)(2,1)S(1)} %bitcast.27, f32[16,4,32,512]{3,2,1,0:T(8,128)S(1)} %bitcast.31, f32[16,4,32,512]{3,2,1,0:T(8,128)S(1)} %bitcast.35, f32[16,4,32,512]{3,2,1,0:T(8,128)S(1)} %bitcast.39, ...), custom_call_target="tpu_custom_call" | custom-call | flops 1000000000 | bytes 6000000 | tf_op jit(solution)/shard_map/pallas_call | solution.py:107
  57.9 0.0 collective-permute-done.7
  57.9 4.8 %collective-permute-done.10 = f32[4,4,4,16,128]{4,3,2,1,0:T(8,128)S(1)} collective-permute-done((f32[4,4,4,16,128]{4,3,2,1,0:T(8,128)S(1)}, f32[4,4,4,16,128]{4,3,2,1,0:T(8,128)S(1)}, u32[]{:S(2)}, u32[]{:S(2)}) %collective-permute-start.10) | collective-permute-done | bytes 524320 | tf_op jit(solution)/shard_map/ppermute | solution.py:193
  62.8 0.0 collective-permute-done.3
  62.8 1.9 %collective-permute-done.6 = f32[4,4,4,16,128]{4,3,2,1,0:T(8,128)S(1)} collective-permute-done((f32[4,4,4,16,128]{4,3,2,1,0:T(8,128)S(1)}, f32[4,4,4,16,128]{4,3,2,1,0:T(8,128)S(1)}, u32[]{:S(2)}, u32[]{:S(2)}) %collective-permute-start.6) | collective-permute-done | bytes 524320 | tf_op jit(solution)/shard_map/ppermute | solution.py:193
  64.6 0.8 collective-permute-done.9
  65.5 0.0 copy-start.1
  65.5 0.0 copy-start.2
  65.5 0.0 copy-start.3
  65.5 0.0 copy-start.4
  65.5 1.5 %shard_map.117 = f32[64,48,128]{2,1,0:T(8,128)} custom-call(f32[64,16,128]{2,1,0:T(8,128)S(1)} %bitcast.51, f32[64,16,128]{2,1,0:T(8,128)S(1)} %bitcast.48, f32[64,16,128]{2,1,0:T(8,128)S(1)} %bitcast.45, f32[64,16,128]{2,1,0:T(8,128)S(1)} %bitcast.54, f32[64,16,128]{2,1,0:T(8,128)S(1)} %bitcast.52, f32[64,16,128]{2,1,0:T(8,128)S(1)} %bitcast.49, ...), custom_call_target="tpu_custom_call" | custom-call | flops 1000000 | bytes 8000000 | tf_op jit(solution)/shard_map/pallas_call | solution.py:130
  67.0 9.5 %all-to-all-start.1 = ((f32[64,48,128]{2,1,0:T(8,128)}), f32[64,48,128]{2,1,0:T(8,128)S(1)}, u32[]{:S(2)}, u32[]{:S(2)}) async-start(f32[64,48,128]{2,1,0:T(8,128)} %shard_map.117), calls=%async_computation.1 | async-start | bytes 3145728 | tf_op jit(solution)/shard_map/all_to_all | solution.py:195
  77.8 0.8 constant_dynamic-slice_fusion.sign_ref
  78.6 0.7 reduce_max.9
  80.0 0.1 pad_maximum_fusion.scalars
  80.1 21.0 %all-to-all-done.1 = f32[64,48,128]{2,1,0:T(8,128)S(1)} async-done(((f32[64,48,128]{2,1,0:T(8,128)}), f32[64,48,128]{2,1,0:T(8,128)S(1)}, u32[]{:S(2)}, u32[]{:S(2)}) %all-to-all-start.1) | async-done | bytes 1572896 | tf_op jit(solution)/shard_map/all_to_all | solution.py:195
  101.1 0.0 copy-done.1
  101.1 0.0 copy-done.2
  101.1 0.0 copy-done.3
  101.1 0.0 copy-done.4
  101.1 2.0 %shard_map.118 = (f32[384,128]{1,0:T(8,128)}, f32[384,128]{1,0:T(8,128)}, f32[384,128]{1,0:T(8,128)}) custom-call(f32[3]{0:T(128)S(1)} %pad_maximum_fusion.scalars, f32[4,4,4,48,128]{4,3,2,1,0:T(8,128)S(1)} %bitcast.40, bf16[128,128]{1,0:T(8,128)(2,1)S(1)} %copy-done.4, s32[64,128]{1,0:T(8,128)S(1)} %constant_dynamic-slice_fusion.sign_ref, ...), custom_call_target="tpu_custom_call" | custom-call | tf_op jit(solution)/shard_map/pallas_call | solution.py:208
Async XLA Ops:
  0.6 31.0 %copy-start = (bf16[256,256]{1,0:T(8,128)(2,1)S(1)}, bf16[256,256]{1,0:T(8,128)(2,1)}, u32[]{:S(2)}) copy-start(bf16[256,256]{1,0:T(8,128)(2,1)} %constant.32.clone.table_ref) | copy-start | bytes 393220
  10.5 21.1 %collective-permute-start = (f32[16,128,512]{2,1,0:T(8,128)S(1)}, f32[16,128,512]{2,1,0:T(8,128)S(1)}, u32[]{:S(2)}, u32[]{:S(2)}) collective-permute-start(f32[16,128,512]{2,1,0:T(8,128)S(1)} %get-tuple-element.22), channel_id=1, source_target_pairs={{0,1},{1,0},{2,3},{3,2},{4,5},{5,4},{6,7},{7,6},{8,9},{9,8},{10,11... | collective-permute-start | bytes 12582920 | tf_op jit(solution)/shard_map/ppermute | solution.py:186
  10.6 21.0 %collective-permute-start.1 = (f32[16,128,512]{2,1,0:T(8,128)S(1)}, f32[16,128,512]{2,1,0:T(8,128)S(1)}, u32[]{:S(2)}, u32[]{:S(2)}) collective-permute-start(f32[16,128,512]{2,1,0:T(8,128)S(1)} %get-tuple-element.23), channel_id=1, source_target_pairs={{0,1},{1,0},{2,3},{3,2},{4,5},{5,4},{6,7},{7,6},{8,9},{9,8},{10,11... | collective-permute-start | bytes 12582920 | tf_op jit(solution)/shard_map/ppermute | solution.py:186
  11.1 20.5 %collective-permute-start.2 = (f32[16,128,512]{2,1,0:T(8,128)S(1)}, f32[16,128,512]{2,1,0:T(8,128)S(1)}, u32[]{:S(2)}, u32[]{:S(2)}) collective-permute-start(f32[16,128,512]{2,1,0:T(8,128)S(1)} %get-tuple-element.24), channel_id=1, source_target_pairs={{0,1},{1,0},{2,3},{3,2},{4,5},{5,4},{6,7},{7,6},{8,9},{9,8},{10,11... | collective-permute-start | bytes 12582920 | tf_op jit(solution)/shard_map/ppermute | solution.py:186
  33.4 16.4 %collective-permute-start.5 = (f32[4,4,4,16,128]{4,3,2,1,0:T(8,128)S(1)}, f32[4,4,4,16,128]{4,3,2,1,0:T(8,128)S(1)}, u32[]{:S(2)}, u32[]{:S(2)}) collective-permute-start(f32[4,4,4,16,128]{4,3,2,1,0:T(8,128)S(1)} %get-tuple-element.27), channel_id=1, source_target_pairs={{0,64},{1,65},{32,96},{33,97},{64,0},{65,1},{96,32},{97,33},{2,66}... | collective-permute-start | bytes 1572872 | tf_op jit(solution)/shard_map/ppermute | solution.py:193
  34.7 17.3 %collective-permute-start.8 = (f32[4,4,4,16,128]{4,3,2,1,0:T(8,128)S(1)}, f32[4,4,4,16,128]{4,3,2,1,0:T(8,128)S(1)}, u32[]{:S(2)}, u32[]{:S(2)}) collective-permute-start(f32[4,4,4,16,128]{4,3,2,1,0:T(8,128)S(1)} %get-tuple-element.31), channel_id=1, source_target_pairs={{0,4},{1,5},{2,6},{3,7},{4,0},{5,1},{6,2},{7,3},{8,12},{9,13},{10,... | collective-permute-start | bytes 1572872 | tf_op jit(solution)/shard_map/ppermute | solution.py:193
  37.9 16.3 %collective-permute-start.11 = (f32[4,4,4,16,128]{4,3,2,1,0:T(8,128)S(1)}, f32[4,4,4,16,128]{4,3,2,1,0:T(8,128)S(1)}, u32[]{:S(2)}, u32[]{:S(2)}) collective-permute-start(f32[4,4,4,16,128]{4,3,2,1,0:T(8,128)S(1)} %get-tuple-element.35), channel_id=1, source_target_pairs={{0,16},{1,17},{8,24},{9,25},{16,0},{17,1},{24,8},{25,9},{2,18},{3,... | collective-permute-start | bytes 1572872 | tf_op jit(solution)/shard_map/ppermute | solution.py:193
  43.6 11.3 %collective-permute-start.4 = (f32[4,4,4,16,128]{4,3,2,1,0:T(8,128)S(1)}, f32[4,4,4,16,128]{4,3,2,1,0:T(8,128)S(1)}, u32[]{:S(2)}, u32[]{:S(2)}) collective-permute-start(f32[4,4,4,16,128]{4,3,2,1,0:T(8,128)S(1)} %get-tuple-element.26), channel_id=1, source_target_pairs={{0,96},{1,33},{32,0},{33,65},{64,32},{65,97},{96,64},{97,1},{2,98}... | collective-permute-start | bytes 1572872 | tf_op jit(solution)/shard_map/ppermute | solution.py:193
  44.8 13.1 %collective-permute-start.7 = (f32[4,4,4,16,128]{4,3,2,1,0:T(8,128)S(1)}, f32[4,4,4,16,128]{4,3,2,1,0:T(8,128)S(1)}, u32[]{:S(2)}, u32[]{:S(2)}) collective-permute-start(f32[4,4,4,16,128]{4,3,2,1,0:T(8,128)S(1)} %get-tuple-element.30), channel_id=1, source_target_pairs={{0,6},{1,3},{2,0},{3,5},{4,2},{5,7},{6,4},{7,1},{8,14},{9,11},{10,... | collective-permute-start | bytes 1572872 | tf_op jit(solution)/shard_map/ppermute | solution.py:193
  49.8 12.9 %collective-permute-start.10 = (f32[4,4,4,16,128]{4,3,2,1,0:T(8,128)S(1)}, f32[4,4,4,16,128]{4,3,2,1,0:T(8,128)S(1)}, u32[]{:S(2)}, u32[]{:S(2)}) collective-permute-start(f32[4,4,4,16,128]{4,3,2,1,0:T(8,128)S(1)} %get-tuple-element.34), channel_id=1, source_target_pairs={{0,24},{1,9},{8,0},{9,17},{16,8},{17,25},{24,16},{25,1},{2,26},{3,... | collective-permute-start | bytes 1572872 | tf_op jit(solution)/shard_map/ppermute | solution.py:193
  52.1 10.7 %collective-permute-start.3 = (f32[4,4,4,16,128]{4,3,2,1,0:T(8,128)S(1)}, f32[4,4,4,16,128]{4,3,2,1,0:T(8,128)S(1)}, u32[]{:S(2)}, u32[]{:S(2)}) collective-permute-start(f32[4,4,4,16,128]{4,3,2,1,0:T(8,128)S(1)} %get-tuple-element.25), channel_id=1, source_target_pairs={{0,32},{1,97},{32,64},{33,1},{64,96},{65,33},{96,0},{97,65},{2,34}... | collective-permute-start | bytes 1572872 | tf_op jit(solution)/shard_map/ppermute | solution.py:193
  54.3 10.4 %collective-permute-start.6 = (f32[4,4,4,16,128]{4,3,2,1,0:T(8,128)S(1)}, f32[4,4,4,16,128]{4,3,2,1,0:T(8,128)S(1)}, u32[]{:S(2)}, u32[]{:S(2)}) collective-permute-start(f32[4,4,4,16,128]{4,3,2,1,0:T(8,128)S(1)} %get-tuple-element.29), channel_id=1, source_target_pairs={{0,2},{1,7},{2,4},{3,1},{4,6},{5,3},{6,0},{7,5},{8,10},{9,15},{10,... | collective-permute-start | bytes 1572872 | tf_op jit(solution)/shard_map/ppermute | solution.py:193
  54.8 10.6 %collective-permute-start.9 = (f32[4,4,4,16,128]{4,3,2,1,0:T(8,128)S(1)}, f32[4,4,4,16,128]{4,3,2,1,0:T(8,128)S(1)}, u32[]{:S(2)}, u32[]{:S(2)}) collective-permute-start(f32[4,4,4,16,128]{4,3,2,1,0:T(8,128)S(1)} %get-tuple-element.33), channel_id=1, source_target_pairs={{0,8},{1,25},{8,16},{9,1},{16,24},{17,9},{24,0},{25,17},{2,10},{3,... | collective-permute-start | bytes 1572872 | tf_op jit(solution)/shard_map/ppermute | solution.py:193
  65.5 35.6 %copy-start.1 = (f32[384,128]{1,0:T(8,128)S(1)}, f32[384,128]{1,0:T(8,128)}, u32[]{:S(2)}) copy-start(f32[384,128]{1,0:T(8,128)} %weights_ref.1) | copy-start | bytes 589828
  65.5 35.6 %copy-start.2 = (f32[384,128]{1,0:T(8,128)S(1)}, f32[384,128]{1,0:T(8,128)}, u32[]{:S(2)}) copy-start(f32[384,128]{1,0:T(8,128)} %first_ref.1) | copy-start | bytes 589828
  65.5 35.6 %copy-start.3 = (f32[384,128]{1,0:T(8,128)S(1)}, f32[384,128]{1,0:T(8,128)}, u32[]{:S(2)}) copy-start(f32[384,128]{1,0:T(8,128)} %second_ref.1) | copy-start | bytes 589828
  65.5 35.7 %copy-start.4 = (bf16[128,128]{1,0:T(8,128)(2,1)S(1)}, bf16[128,128]{1,0:T(8,128)(2,1)}, u32[]{:S(2)}) copy-start(bf16[128,128]{1,0:T(8,128)(2,1)} %constant.31.clone.table_ref) | copy-start | bytes 98308
  67.0 34.1 %all-to-all-start.1 = ((f32[64,48,128]{2,1,0:T(8,128)}), f32[64,48,128]{2,1,0:T(8,128)S(1)}, u32[]{:S(2)}, u32[]{:S(2)}) async-start(f32[64,48,128]{2,1,0:T(8,128)} %shard_map.117), calls=%async_computation.1 | async-start | bytes 3145728 | tf_op jit(solution)/shard_map/all_to_all | solution.py:195

commit v3 on v2

--- a/solution.py
+++ b/solution.py
@@ -13,8 +13,8 @@
 BLOCK = 128
 SIGN_ROWS = 64
 ROOT = 1.0 / math.sqrt(BLOCK)
-CHIPS = ("x", "z", "y")
-ALL = ("x", "z", "y", "core")
+CHIPS = ("z", "y", "x")
+ALL = ("z", "y", "x", "core")
 INTRA = ("z", "y", "core")
 FIRST = ("x", "y", "z")
 FIELD = 4096.0
@@ -97,7 +97,7 @@
                     total = mine[row : row + 32] + jnp.floor(other * scale + 0.5)
                     word = total[:16] + FIELD * total[16:]
                     for x in range(2):
-                        outs[t][2 * h + x, z, y] = word[:, 128 * x : 128 * x + 128]
+                        outs[t][z, y, 2 * h + x] = word[:, 128 * x : 128 * x + 128]
         return carry
 
     lax.fori_loop(0, 4, plane, 0)
@@ -147,7 +147,7 @@
             for a in range(4):
                 for b in range(4):
                     x, z, y = ((q, a, b), (a, b, q), (a, q, b))[t]
-                    parts.append(words_ref[x, z, y, 16 * t : 16 * t + 16, :])
+                    parts.append(words_ref[z, y, x, 16 * t : 16 * t + 16, :])
             low = high = jnp.zeros((16, 128), F32)
             for word in parts:
                 upper = jnp.floor(word * (1.0 / FIELD) + 0.5)

time: 103 us -> 104 us (level)
  no operation moved by 1% of the time
where the time goes in v3:
time: 104 us; the launch traced here: 103 us
  waiting for transfers between devices  32.4 us (31%)
  starting transfers between devices  25.6 us (25%)
  Pallas kernels  20.5 us (20%)
  blocking collectives  20.4 us (20%)
  between operations  2.78 us (3%)
    all_to_all x1, waiting for transfers between devices, shards(): words = lax.all_to_all(words, CHIPS, 0, 0, tiled=True)  21.3 us
    all_to_all x1, blocking collectives, shards(): tops = lax.all_to_all(top_tile, ALL, 0, 0, tiled=True)  20.4 us
    ppermute x9, starting transfers between devices, shards(): lax.ppermute(out, (FIRST[third], 'core'), shift(offset))  15.5 us
    ppermute x9, waiting for transfers between devices, shards(): lax.ppermute(out, (FIRST[third], 'core'), shift(offset))  11.1 us
    pallas_call x1, Pallas kernels, rotate_all(): pl.pallas_call(rotate_kernel, in_specs=[pl.BlockSpec(memory_space=pl.ANY)...  9.83 us
    all_to_all x1, starting transfers between devices, shards(): words = lax.all_to_all(words, CHIPS, 0, 0, tiled=True)  9.49 us
    pallas_call x4, Pallas kernels, levels_for(): pl.pallas_call(functools.partial(level_kernel, offset), in_specs=[VMEM] *...  7.21 us
  transfers between devices with their start and end apart: 13, of which 6 were waited for; matrix products, arithmetic and copies ran while one was open for 2% of the time, Pallas kernels for 5%

profile of v3, /device:TPU:0, one launch (start us, length us, event | category | flops | bytes accessed | tf_op | source)
XLA Modules:
  0.0 103.4 jit_solution(15291899796502164616)
XLA Ops:
  0.6 0.0 copy-start
  0.6 9.8 %shard_map.112 = (f32[16,128,512]{2,1,0:T(8,128)S(1)}, f32[16,128,512]{2,1,0:T(8,128)S(1)}, f32[16,128,512]{2,1,0:T(8,128)S(1)}, bf16[16,384,512]{2,1,0:T(8,128)(2,1)S(1)}, f32[128,128]{1,0:T(8,128)}) custom-call(bf16[16,2,384,512]{3,2,1,0:T(8,128)(2,1)} %bitcast.58, s32[64,512]{1,0:T(8,128)} %sign_ref.1, bf16[256,256]{1,0:T(8,128)(2,1)} %constant.32.clone.table_ref), custom_call_target="tpu_custom_call" | custom-call | flops 6000000000 | bytes 12000000 | tf_op jit(solution)/shard_map/pallas_call | solution.py:65
  10.5 0.1 collective-permute-start
  10.6 0.5 collective-permute-start.1
  11.1 0.1 collective-permute-start.2
  11.2 20.4 %all_to_all.16 = f32[128,1,128]{2,1,0:T(1,128)S(1)} all-to-all(f32[128,1,128]{2,1,0:T(1,128)} %bitcast.57), channel_id=1, replica_groups=mesh['x'=4,'z'=4,'y'=4,'core'=2] {'z','y','x','core'}, dimensions={0} | all-to-all | bytes 131072 | tf_op jit(solution)/shard_map/all_to_all | solution.py:187
  31.6 0.0 collective-permute-done
  31.6 0.0 collective-permute-done.1
  31.6 0.0 collective-permute-done.2
  31.6 0.0 copy-done
  31.6 1.8 %shard_map.115 = (f32[4,4,4,16,128]{4,3,2,1,0:T(8,128)S(1)}, f32[4,4,4,16,128]{4,3,2,1,0:T(8,128)S(1)}, f32[4,4,4,16,128]{4,3,2,1,0:T(8,128)S(1)}) custom-call(bf16[16,12,32,512]{3,2,1,0:T(8,128)(2,1)S(1)} %bitcast.24, f32[16,4,32,512]{3,2,1,0:T(8,128)S(1)} %bitcast.28, f32[16,4,32,512]{3,2,1,0:T(8,128)S(1)} %bitcast.32, f32[16,4,32,512]{3,2,1,0:T(8,128)S(1)} %bitcast.36, ...), custom_call_target="tpu_custom_call" | custom-call | flops 1000000000 | bytes 6000000 | tf_op jit(solution)/shard_map/pallas_call | solution.py:107
  33.4 1.3 %collective-permute-start.5 = (f32[4,4,4,16,128]{4,3,2,1,0:T(8,128)S(1)}, f32[4,4,4,16,128]{4,3,2,1,0:T(8,128)S(1)}, u32[]{:S(2)}, u32[]{:S(2)}) collective-permute-start(f32[4,4,4,16,128]{4,3,2,1,0:T(8,128)S(1)} %get-tuple-element.27), channel_id=1, source_target_pairs={{0,64},{1,65},{32,96},{33,97},{64,0},{65,1},{96,32},{97,33},{2,66}... | collective-permute-start | bytes 1572872 | tf_op jit(solution)/shard_map/ppermute | solution.py:193
  34.7 3.2 %collective-permute-start.8 = (f32[4,4,4,16,128]{4,3,2,1,0:T(8,128)S(1)}, f32[4,4,4,16,128]{4,3,2,1,0:T(8,128)S(1)}, u32[]{:S(2)}, u32[]{:S(2)}) collective-permute-start(f32[4,4,4,16,128]{4,3,2,1,0:T(8,128)S(1)} %get-tuple-element.31), channel_id=1, source_target_pairs={{0,4},{1,5},{2,6},{3,7},{4,0},{5,1},{6,2},{7,3},{8,12},{9,13},{10,... | collective-permute-start | bytes 1572872 | tf_op jit(solution)/shard_map/ppermute | solution.py:193
  37.9 3.9 %collective-permute-start.11 = (f32[4,4,4,16,128]{4,3,2,1,0:T(8,128)S(1)}, f32[4,4,4,16,128]{4,3,2,1,0:T(8,128)S(1)}, u32[]{:S(2)}, u32[]{:S(2)}) collective-permute-start(f32[4,4,4,16,128]{4,3,2,1,0:T(8,128)S(1)} %get-tuple-element.35), channel_id=1, source_target_pairs={{0,16},{1,17},{8,24},{9,25},{16,0},{17,1},{24,8},{25,9},{2,18},{3,... | collective-permute-start | bytes 1572872 | tf_op jit(solution)/shard_map/ppermute | solution.py:193
  41.8 1.8 %shard_map.114 = (f32[4,4,4,16,128]{4,3,2,1,0:T(8,128)S(1)}, f32[4,4,4,16,128]{4,3,2,1,0:T(8,128)S(1)}, f32[4,4,4,16,128]{4,3,2,1,0:T(8,128)S(1)}) custom-call(bf16[16,12,32,512]{3,2,1,0:T(8,128)(2,1)S(1)} %bitcast.25, f32[16,4,32,512]{3,2,1,0:T(8,128)S(1)} %bitcast.29, f32[16,4,32,512]{3,2,1,0:T(8,128)S(1)} %bitcast.33, f32[16,4,32,512]{3,2,1,0:T(8,128)S(1)} %bitcast.37, ...), custom_call_target="tpu_custom_call" | custom-call | flops 1000000000 | bytes 6000000 | tf_op jit(solution)/shard_map/pallas_call | solution.py:107
  43.6 1.3 %collective-permute-start.4 = (f32[4,4,4,16,128]{4,3,2,1,0:T(8,128)S(1)}, f32[4,4,4,16,128]{4,3,2,1,0:T(8,128)S(1)}, u32[]{:S(2)}, u32[]{:S(2)}) collective-permute-start(f32[4,4,4,16,128]{4,3,2,1,0:T(8,128)S(1)} %get-tuple-element.26), channel_id=1, source_target_pairs={{0,96},{1,33},{32,0},{33,65},{64,32},{65,97},{96,64},{97,1},{2,98}... | collective-permute-start | bytes 1572872 | tf_op jit(solution)/shard_map/ppermute | solution.py:193
  44.8 1.1 %collective-permute-start.7 = (f32[4,4,4,16,128]{4,3,2,1,0:T(8,128)S(1)}, f32[4,4,4,16,128]{4,3,2,1,0:T(8,128)S(1)}, u32[]{:S(2)}, u32[]{:S(2)}) collective-permute-start(f32[4,4,4,16,128]{4,3,2,1,0:T(8,128)S(1)} %get-tuple-element.30), channel_id=1, source_target_pairs={{0,6},{1,3},{2,0},{3,5},{4,2},{5,7},{6,4},{7,1},{8,14},{9,11},{10,... | collective-permute-start | bytes 1572872 | tf_op jit(solution)/shard_map/ppermute | solution.py:193
  45.9 1.8 %shard_map.113 = (f32[4,4,4,16,128]{4,3,2,1,0:T(8,128)S(1)}, f32[4,4,4,16,128]{4,3,2,1,0:T(8,128)S(1)}, f32[4,4,4,16,128]{4,3,2,1,0:T(8,128)S(1)}) custom-call(bf16[16,12,32,512]{3,2,1,0:T(8,128)(2,1)S(1)} %bitcast.26, f32[16,4,32,512]{3,2,1,0:T(8,128)S(1)} %bitcast.30, f32[16,4,32,512]{3,2,1,0:T(8,128)S(1)} %bitcast.34, f32[16,4,32,512]{3,2,1,0:T(8,128)S(1)} %bitcast.38, ...), custom_call_target="tpu_custom_call" | custom-call | flops 1000000000 | bytes 6000000 | tf_op jit(solution)/shard_map/pallas_call | solution.py:107
  47.7 2.1 %collective-permute-done.5 = f32[4,4,4,16,128]{4,3,2,1,0:T(8,128)S(1)} collective-permute-done((f32[4,4,4,16,128]{4,3,2,1,0:T(8,128)S(1)}, f32[4,4,4,16,128]{4,3,2,1,0:T(8,128)S(1)}, u32[]{:S(2)}, u32[]{:S(2)}) %collective-permute-start.5) | collective-permute-done | bytes 524320 | tf_op jit(solution)/shard_map/ppermute | solution.py:193
  49.8 2.2 %collective-permute-start.10 = (f32[4,4,4,16,128]{4,3,2,1,0:T(8,128)S(1)}, f32[4,4,4,16,128]{4,3,2,1,0:T(8,128)S(1)}, u32[]{:S(2)}, u32[]{:S(2)}) collective-permute-start(f32[4,4,4,16,128]{4,3,2,1,0:T(8,128)S(1)} %get-tuple-element.34), channel_id=1, source_target_pairs={{0,24},{1,9},{8,0},{9,17},{16,8},{17,25},{24,16},{25,1},{2,26},{3,... | collective-permute-start | bytes 1572872 | tf_op jit(solution)/shard_map/ppermute | solution.py:193
  52.0 0.0 collective-permute-done.8
  52.1 0.7 collective-permute-start.3
  52.8 1.5 %collective-permute-done.11 = f32[4,4,4,16,128]{4,3,2,1,0:T(8,128)S(1)} collective-permute-done((f32[4,4,4,16,128]{4,3,2,1,0:T(8,128)S(1)}, f32[4,4,4,16,128]{4,3,2,1,0:T(8,128)S(1)}, u32[]{:S(2)}, u32[]{:S(2)}) %collective-permute-start.11) | collective-permute-done | bytes 524320 | tf_op jit(solution)/shard_map/ppermute | solution.py:193
  54.3 0.6 collective-permute-start.6
  54.8 0.0 collective-permute-done.4
  54.8 1.3 %collective-permute-start.9 = (f32[4,4,4,16,128]{4,3,2,1,0:T(8,128)S(1)}, f32[4,4,4,16,128]{4,3,2,1,0:T(8,128)S(1)}, u32[]{:S(2)}, u32[]{:S(2)}) collective-permute-start(f32[4,4,4,16,128]{4,3,2,1,0:T(8,128)S(1)} %get-tuple-element.33), channel_id=1, source_target_pairs={{0,8},{1,25},{8,16},{9,1},{16,24},{17,9},{24,0},{25,17},{2,10},{3,... | collective-permute-start | bytes 1572872 | tf_op jit(solution)/shard_map/ppermute | solution.py:193
  56.1 1.8 %shard_map.116 = (f32[4,4,4,16,128]{4,3,2,1,0:T(8,128)S(1)}, f32[4,4,4,16,128]{4,3,2,1,0:T(8,128)S(1)}, f32[4,4,4,16,128]{4,3,2,1,0:T(8,128)S(1)}) custom-call(bf16[16,12,32,512]{3,2,1,0:T(8,128)(2,1)S(1)} %bitcast.27, f32[16,4,32,512]{3,2,1,0:T(8,128)S(1)} %bitcast.31, f32[16,4,32,512]{3,2,1,0:T(8,128)S(1)} %bitcast.35, f32[16,4,32,512]{3,2,1,0:T(8,128)S(1)} %bitcast.39, ...), custom_call_target="tpu_custom_call" | custom-call | flops 1000000000 | bytes 6000000 | tf_op jit(solution)/shard_map/pallas_call | solution.py:107
  57.9 0.0 collective-permute-done.7
  57.9 4.7 %collective-permute-done.10 = f32[4,4,4,16,128]{4,3,2,1,0:T(8,128)S(1)} collective-permute-done((f32[4,4,4,16,128]{4,3,2,1,0:T(8,128)S(1)}, f32[4,4,4,16,128]{4,3,2,1,0:T(8,128)S(1)}, u32[]{:S(2)}, u32[]{:S(2)}) %collective-permute-start.10) | collective-permute-done | bytes 524320 | tf_op jit(solution)/shard_map/ppermute | solution.py:193
  62.7 0.0 collective-permute-done.3
  62.7 2.0 %collective-permute-done.6 = f32[4,4,4,16,128]{4,3,2,1,0:T(8,128)S(1)} collective-permute-done((f32[4,4,4,16,128]{4,3,2,1,0:T(8,128)S(1)}, f32[4,4,4,16,128]{4,3,2,1,0:T(8,128)S(1)}, u32[]{:S(2)}, u32[]{:S(2)}) %collective-permute-start.6) | collective-permute-done | bytes 524320 | tf_op jit(solution)/shard_map/ppermute | solution.py:193
  64.6 0.8 collective-permute-done.9
  65.5 0.0 copy-start.1
  65.5 0.0 copy-start.2
  65.5 0.0 copy-start.3
  65.5 0.0 copy-start.4
  65.5 1.5 %shard_map.117 = f32[64,48,128]{2,1,0:T(8,128)} custom-call(f32[64,16,128]{2,1,0:T(8,128)S(1)} %bitcast.51, f32[64,16,128]{2,1,0:T(8,128)S(1)} %bitcast.48, f32[64,16,128]{2,1,0:T(8,128)S(1)} %bitcast.45, f32[64,16,128]{2,1,0:T(8,128)S(1)} %bitcast.54, f32[64,16,128]{2,1,0:T(8,128)S(1)} %bitcast.52, f32[64,16,128]{2,1,0:T(8,128)S(1)} %bitcast.49, ...), custom_call_target="tpu_custom_call" | custom-call | flops 1000000 | bytes 8000000 | tf_op jit(solution)/shard_map/pallas_call | solution.py:130
  67.0 9.5 %all-to-all-start.1 = ((f32[64,48,128]{2,1,0:T(8,128)}), f32[64,48,128]{2,1,0:T(8,128)S(1)}, u32[]{:S(2)}, u32[]{:S(2)}) async-start(f32[64,48,128]{2,1,0:T(8,128)} %shard_map.117), calls=%async_computation.1 | async-start | bytes 3145728 | tf_op jit(solution)/shard_map/all_to_all | solution.py:195
  77.8 0.8 constant_dynamic-slice_fusion.sign_ref
  78.6 0.7 reduce_max.9
  80.0 0.1 pad_maximum_fusion.scalars
  80.1 21.3 %all-to-all-done.1 = f32[64,48,128]{2,1,0:T(8,128)S(1)} async-done(((f32[64,48,128]{2,1,0:T(8,128)}), f32[64,48,128]{2,1,0:T(8,128)S(1)}, u32[]{:S(2)}, u32[]{:S(2)}) %all-to-all-start.1) | async-done | bytes 1572896 | tf_op jit(solution)/shard_map/all_to_all | solution.py:195
  101.4 0.0 copy-done.1
  101.4 0.0 copy-done.2
  101.4 0.0 copy-done.3
  101.4 0.0 copy-done.4
  101.4 2.0 %shard_map.118 = (f32[384,128]{1,0:T(8,128)}, f32[384,128]{1,0:T(8,128)}, f32[384,128]{1,0:T(8,128)}) custom-call(f32[3]{0:T(128)S(1)} %pad_maximum_fusion.scalars, f32[4,4,4,48,128]{4,3,2,1,0:T(8,128)S(1)} %bitcast.40, bf16[128,128]{1,0:T(8,128)(2,1)S(1)} %copy-done.4, s32[64,128]{1,0:T(8,128)S(1)} %constant_dynamic-slice_fusion.sign_ref, ...), custom_call_target="tpu_custom_call" | custom-call | tf_op jit(solution)/shard_map/pallas_call | solution.py:208
Async XLA Ops:
  0.6 31.0 %copy-start = (bf16[256,256]{1,0:T(8,128)(2,1)S(1)}, bf16[256,256]{1,0:T(8,128)(2,1)}, u32[]{:S(2)}) copy-start(bf16[256,256]{1,0:T(8,128)(2,1)} %constant.32.clone.table_ref) | copy-start | bytes 393220
  10.5 21.1 %collective-permute-start = (f32[16,128,512]{2,1,0:T(8,128)S(1)}, f32[16,128,512]{2,1,0:T(8,128)S(1)}, u32[]{:S(2)}, u32[]{:S(2)}) collective-permute-start(f32[16,128,512]{2,1,0:T(8,128)S(1)} %get-tuple-element.22), channel_id=1, source_target_pairs={{0,1},{1,0},{2,3},{3,2},{4,5},{5,4},{6,7},{7,6},{8,9},{9,8},{10,11... | collective-permute-start | bytes 12582920 | tf_op jit(solution)/shard_map/ppermute | solution.py:186
  10.6 21.0 %collective-permute-start.1 = (f32[16,128,512]{2,1,0:T(8,128)S(1)}, f32[16,128,512]{2,1,0:T(8,128)S(1)}, u32[]{:S(2)}, u32[]{:S(2)}) collective-permute-start(f32[16,128,512]{2,1,0:T(8,128)S(1)} %get-tuple-element.23), channel_id=1, source_target_pairs={{0,1},{1,0},{2,3},{3,2},{4,5},{5,4},{6,7},{7,6},{8,9},{9,8},{10,11... | collective-permute-start | bytes 12582920 | tf_op jit(solution)/shard_map/ppermute | solution.py:186
  11.1 20.5 %collective-permute-start.2 = (f32[16,128,512]{2,1,0:T(8,128)S(1)}, f32[16,128,512]{2,1,0:T(8,128)S(1)}, u32[]{:S(2)}, u32[]{:S(2)}) collective-permute-start(f32[16,128,512]{2,1,0:T(8,128)S(1)} %get-tuple-element.24), channel_id=1, source_target_pairs={{0,1},{1,0},{2,3},{3,2},{4,5},{5,4},{6,7},{7,6},{8,9},{9,8},{10,11... | collective-permute-start | bytes 12582920 | tf_op jit(solution)/shard_map/ppermute | solution.py:186
  33.4 16.4 %collective-permute-start.5 = (f32[4,4,4,16,128]{4,3,2,1,0:T(8,128)S(1)}, f32[4,4,4,16,128]{4,3,2,1,0:T(8,128)S(1)}, u32[]{:S(2)}, u32[]{:S(2)}) collective-permute-start(f32[4,4,4,16,128]{4,3,2,1,0:T(8,128)S(1)} %get-tuple-element.27), channel_id=1, source_target_pairs={{0,64},{1,65},{32,96},{33,97},{64,0},{65,1},{96,32},{97,33},{2,66}... | collective-permute-start | bytes 1572872 | tf_op jit(solution)/shard_map/ppermute | solution.py:193
  34.7 17.3 %collective-permute-start.8 = (f32[4,4,4,16,128]{4,3,2,1,0:T(8,128)S(1)}, f32[4,4,4,16,128]{4,3,2,1,0:T(8,128)S(1)}, u32[]{:S(2)}, u32[]{:S(2)}) collective-permute-start(f32[4,4,4,16,128]{4,3,2,1,0:T(8,128)S(1)} %get-tuple-element.31), channel_id=1, source_target_pairs={{0,4},{1,5},{2,6},{3,7},{4,0},{5,1},{6,2},{7,3},{8,12},{9,13},{10,... | collective-permute-start | bytes 1572872 | tf_op jit(solution)/shard_map/ppermute | solution.py:193
  37.9 16.3 %collective-permute-start.11 = (f32[4,4,4,16,128]{4,3,2,1,0:T(8,128)S(1)}, f32[4,4,4,16,128]{4,3,2,1,0:T(8,128)S(1)}, u32[]{:S(2)}, u32[]{:S(2)}) collective-permute-start(f32[4,4,4,16,128]{4,3,2,1,0:T(8,128)S(1)} %get-tuple-element.35), channel_id=1, source_target_pairs={{0,16},{1,17},{8,24},{9,25},{16,0},{17,1},{24,8},{25,9},{2,18},{3,... | collective-permute-start | bytes 1572872 | tf_op jit(solution)/shard_map/ppermute | solution.py:193
  43.6 11.3 %collective-permute-start.4 = (f32[4,4,4,16,128]{4,3,2,1,0:T(8,128)S(1)}, f32[4,4,4,16,128]{4,3,2,1,0:T(8,128)S(1)}, u32[]{:S(2)}, u32[]{:S(2)}) collective-permute-start(f32[4,4,4,16,128]{4,3,2,1,0:T(8,128)S(1)} %get-tuple-element.26), channel_id=1, source_target_pairs={{0,96},{1,33},{32,0},{33,65},{64,32},{65,97},{96,64},{97,1},{2,98}... | collective-permute-start | bytes 1572872 | tf_op jit(solution)/shard_map/ppermute | solution.py:193
  44.8 13.1 %collective-permute-start.7 = (f32[4,4,4,16,128]{4,3,2,1,0:T(8,128)S(1)}, f32[4,4,4,16,128]{4,3,2,1,0:T(8,128)S(1)}, u32[]{:S(2)}, u32[]{:S(2)}) collective-permute-start(f32[4,4,4,16,128]{4,3,2,1,0:T(8,128)S(1)} %get-tuple-element.30), channel_id=1, source_target_pairs={{0,6},{1,3},{2,0},{3,5},{4,2},{5,7},{6,4},{7,1},{8,14},{9,11},{10,... | collective-permute-start | bytes 1572872 | tf_op jit(solution)/shard_map/ppermute | solution.py:193
  49.8 12.8 %collective-permute-start.10 = (f32[4,4,4,16,128]{4,3,2,1,0:T(8,128)S(1)}, f32[4,4,4,16,128]{4,3,2,1,0:T(8,128)S(1)}, u32[]{:S(2)}, u32[]{:S(2)}) collective-permute-start(f32[4,4,4,16,128]{4,3,2,1,0:T(8,128)S(1)} %get-tuple-element.34), channel_id=1, source_target_pairs={{0,24},{1,9},{8,0},{9,17},{16,8},{17,25},{24,16},{25,1},{2,26},{3,... | collective-permute-start | bytes 1572872 | tf_op jit(solution)/shard_map/ppermute | solution.py:193
  52.1 10.6 %collective-permute-start.3 = (f32[4,4,4,16,128]{4,3,2,1,0:T(8,128)S(1)}, f32[4,4,4,16,128]{4,3,2,1,0:T(8,128)S(1)}, u32[]{:S(2)}, u32[]{:S(2)}) collective-permute-start(f32[4,4,4,16,128]{4,3,2,1,0:T(8,128)S(1)} %get-tuple-element.25), channel_id=1, source_target_pairs={{0,32},{1,97},{32,64},{33,1},{64,96},{65,33},{96,0},{97,65},{2,34}... | collective-permute-start | bytes 1572872 | tf_op jit(solution)/shard_map/ppermute | solution.py:193
  54.3 10.4 %collective-permute-start.6 = (f32[4,4,4,16,128]{4,3,2,1,0:T(8,128)S(1)}, f32[4,4,4,16,128]{4,3,2,1,0:T(8,128)S(1)}, u32[]{:S(2)}, u32[]{:S(2)}) collective-permute-start(f32[4,4,4,16,128]{4,3,2,1,0:T(8,128)S(1)} %get-tuple-element.29), channel_id=1, source_target_pairs={{0,2},{1,7},{2,4},{3,1},{4,6},{5,3},{6,0},{7,5},{8,10},{9,15},{10,... | collective-permute-start | bytes 1572872 | tf_op jit(solution)/shard_map/ppermute | solution.py:193
  54.8 10.6 %collective-permute-start.9 = (f32[4,4,4,16,128]{4,3,2,1,0:T(8,128)S(1)}, f32[4,4,4,16,128]{4,3,2,1,0:T(8,128)S(1)}, u32[]{:S(2)}, u32[]{:S(2)}) collective-permute-start(f32[4,4,4,16,128]{4,3,2,1,0:T(8,128)S(1)} %get-tuple-element.33), channel_id=1, source_target_pairs={{0,8},{1,25},{8,16},{9,1},{16,24},{17,9},{24,0},{25,17},{2,10},{3,... | collective-permute-start | bytes 1572872 | tf_op jit(solution)/shard_map/ppermute | solution.py:193
  65.5 35.9 %copy-start.1 = (f32[384,128]{1,0:T(8,128)S(1)}, f32[384,128]{1,0:T(8,128)}, u32[]{:S(2)}) copy-start(f32[384,128]{1,0:T(8,128)} %weights_ref.1) | copy-start | bytes 589828
  65.5 35.9 %copy-start.2 = (f32[384,128]{1,0:T(8,128)S(1)}, f32[384,128]{1,0:T(8,128)}, u32[]{:S(2)}) copy-start(f32[384,128]{1,0:T(8,128)} %first_ref.1) | copy-start | bytes 589828
  65.5 35.9 %copy-start.3 = (f32[384,128]{1,0:T(8,128)S(1)}, f32[384,128]{1,0:T(8,128)}, u32[]{:S(2)}) copy-start(f32[384,128]{1,0:T(8,128)} %second_ref.1) | copy-start | bytes 589828
  65.5 35.9 %copy-start.4 = (bf16[128,128]{1,0:T(8,128)(2,1)S(1)}, bf16[128,128]{1,0:T(8,128)(2,1)}, u32[]{:S(2)}) copy-start(bf16[128,128]{1,0:T(8,128)(2,1)} %constant.31.clone.table_ref) | copy-start | bytes 98308
  67.0 34.4 %all-to-all-start.1 = ((f32[64,48,128]{2,1,0:T(8,128)}), f32[64,48,128]{2,1,0:T(8,128)S(1)}, u32[]{:S(2)}, u32[]{:S(2)}) async-start(f32[64,48,128]{2,1,0:T(8,128)} %shard_map.117), calls=%async_computation.1 | async-start | bytes 3145728 | tf_op jit(solution)/shard_map/all_to_all | solution.py:195

commit v4 on v3

--- a/solution.py
+++ b/solution.py
@@ -77,10 +77,33 @@
     )(grads.reshape(16, 2, 384, 512), signs, table)
 
 
+def nearest(value, unit):
+    return jnp.floor(value * (1.0 / unit) + 0.5)
+
+
+def pack_eight(v):
+    last = v[6] + 512.0 * v[7]
+    high = nearest(last, 4096.0)
+    rest = last - 4096.0 * high
+    middle = nearest(rest, 64.0)
+    thirds = (high, middle, rest - 64.0 * middle)
+    return [(v[2 * i] + 512.0 * v[2 * i + 1]) + 262144.0 * thirds[i] for i in range(3)]
+
+
+def unpack_eight(words):
+    thirds = [nearest(word, 262144.0) for word in words]
+    last = (thirds[0] * 4096.0 + thirds[1] * 64.0) + thirds[2]
+    values = []
+    for pair in [word - 262144.0 * third for word, third in zip(words, thirds)] + [last]:
+        upper = nearest(pair, 512.0)
+        values += [pair - 512.0 * upper, upper]
+    return values
+
+
 def level_kernel(offset, own_ref, raw0, raw1, raw2, table_ref, top_ref, *outs):
     table = table_ref[...]
     scale = 127.0 / jnp.max(top_ref[...], axis=(0, 1), keepdims=True)
-    ahead = jnp.where(lax.axis_index("core") == 0, offset, 4 - offset)
+    ahead = jnp.where(lax.axis_index("core") == 0, offset, (4 - offset) % 4)
     quarters = [lax.rem(lax.axis_index(axis) + ahead, 4) for axis in FIRST]
     raws = (raw0, raw1, raw2)
 
@@ -90,51 +113,66 @@
         mine = jnp.dot(stacked, table, preferred_element_type=F32) * ROOT
         mine = jnp.floor(mine * scale + 0.5)
         for t in range(3):
-            for y in range(4):
+            for pair in range(2):
                 for h in range(2):
-                    row = 32 * ((t * 4 + y) * 2 + h)
-                    other = raws[t][4 * z + y, quarters[t], :, 256 * h : 256 * h + 256]
-                    total = mine[row : row + 32] + jnp.floor(other * scale + 0.5)
-                    word = total[:16] + FIELD * total[16:]
-                    for x in range(2):
-                        outs[t][z, y, 2 * h + x] = word[:, 128 * x : 128 * x + 128]
+                    groups = []
+                    for y in (2 * pair, 2 * pair + 1):
+                        row = 32 * ((t * 4 + y) * 2 + h)
+                        other = raws[t][4 * z + y, quarters[t], :, 256 * h : 256 * h + 256]
+                        total = mine[row : row + 32] + jnp.floor(other * scale + 0.5)
+                        groups += [total[8 * g : 8 * g + 8] for g in range(4)]
+                    if offset:
+                        for i, word in enumerate(pack_eight(groups)):
+                            outs[t][z, pair, i, :, 256 * h : 256 * h + 256] = word
+                        continue
+                    for k in range(2):
+                        low, lower, high, higher = groups[4 * k : 4 * k + 4]
+                        word = jnp.concatenate([low + FIELD * high, lower + FIELD * higher], axis=0)
+                        for x in range(2):
+                            place = outs[0].at[z, 2 * pair + k, 2 * h + x, 16 * t : 16 * t + 16, :]
+                            place[...] = word[:, 128 * x : 128 * x + 128]
         return carry
 
     lax.fori_loop(0, 4, plane, 0)
 
 
 def levels_for(offset, own, raws, table, tops):
+    shapes = [(4, 2, 3, 8, 512)] * 3 if offset else [(4, 4, 4, 48, 128)]
     return pl.pallas_call(
         functools.partial(level_kernel, offset),
         in_specs=[VMEM] * 6,
-        out_specs=[VMEM] * 3,
-        out_shape=[pltpu.VMEM((4, 4, 4, 16, 128), F32)] * 3,
+        out_specs=[VMEM] * len(shapes),
+        out_shape=[pltpu.VMEM(shape, F32) for shape in shapes],
         compiler_params=pltpu.CompilerParams(vmem_limit_bytes=12 * 2**20),
         cost_estimate=pl.CostEstimate(flops=10**9, bytes_accessed=6 * 10**6, transcendentals=0),
     )(own.reshape(16, 12, 32, 512), *[raw.reshape(16, 4, 32, 512) for raw in raws], table, tops)
 
 
-def gather_kernel(*refs):
-    out = refs[-1]
-
-    def some(i, carry):
-        for t in range(3):
-            a, b, c, d = (refs[4 * t + k][pl.ds(8 * i, 8)] for k in range(4))
-            out[pl.ds(8 * i, 8), 16 * t : 16 * t + 16, :] = (a + b) + (c + d)
+def add_kernel(sums_ref, part0, part1, part2, out_ref):
+    def plane(z, carry):
+        for t, part in enumerate((part0, part1, part2)):
+            for pair in range(2):
+                v = unpack_eight([part[z, pair, i] for i in range(3)])
+                for k in range(2):
+                    low, lower, high, higher = v[4 * k : 4 * k + 4]
+                    for j, word in enumerate((low + FIELD * high, lower + FIELD * higher)):
+                        for x in range(4):
+                            where = (z, 2 * pair + k, x, pl.ds(16 * t + 8 * j, 8))
+                            out_ref[where] = sums_ref[where] + word[:, 128 * x : 128 * x + 128]
         return carry
 
-    lax.fori_loop(0, 8, some, 0)
-
-
-def sum_four(parts):
-    return pl.pallas_call(
-        gather_kernel,
-        in_specs=[VMEM] * 12,
+    lax.fori_loop(0, 4, plane, 0)
+
+
+def add_parts(sums, parts):
+    return pl.pallas_call(
+        add_kernel,
+        in_specs=[VMEM] * 4,
         out_specs=VMEM,
-        out_shape=pltpu.VMEM((64, 48, 128), F32),
+        out_shape=pltpu.VMEM((4, 4, 4, 48, 128), F32),
         compiler_params=pltpu.CompilerParams(vmem_limit_bytes=12 * 2**20),
-        cost_estimate=pl.CostEstimate(flops=10**6, bytes_accessed=8 * 10**6, transcendentals=0),
-    )(*[part.reshape(64, 16, 128) for part in parts])
+        cost_estimate=pl.CostEstimate(flops=10**7, bytes_accessed=4 * 10**6, transcendentals=0),
+    )(sums, *parts)
 
 
 def update_kernel(
@@ -186,12 +224,14 @@
     raws = [lax.ppermute(raw, "core", [(0, 1), (1, 0)]) for raw in raws]
     tops = lax.all_to_all(top_tile, ALL, 0, 0, tiled=True)
 
-    parts = [[] for _ in range(3)]
-    for offset in (1, 3, 2, 0):
+    arrived = []
+    for offset in (1, 3, 2):
         outs = levels_for(offset, own, raws, twice, tops)
-        for third, out in enumerate(outs):
-            parts[third].append(lax.ppermute(out, (FIRST[third], "core"), shift(offset)) if offset else out)
-    words = sum_four([part for third in parts for part in third])
+        arrived.append([lax.ppermute(out, (axis, "core"), shift(offset)) for out, axis in zip(outs, FIRST)])
+    (words,) = levels_for(0, own, raws, twice, tops)
+    for parts in arrived:
+        words = add_parts(words, parts)
+    words = words.reshape(64, 48, 128)
     words = lax.all_to_all(words, CHIPS, 0, 0, tiled=True)
 
     top_value = jnp.max(tops)

time: 104 us -> 96.9 us (0.932)
  waiting for transfers between devices: 32.4 us -> 23.3 us
  Pallas kernels: 20.5 us -> 22.9 us
    ppermute x9, waiting for transfers between devices: 11.1 us -> 5.82 us  [shards(): lax.ppermute(out, (axis, 'core'), shift(offset))]
    all_to_all x1, waiting for transfers between devices: 21.3 us -> 17.5 us  [shards(): words = lax.all_to_all(words, CHIPS, 0, 0, tiled=True)]
    pallas_call x1 -> x3, Pallas kernels: 1.49 us -> 3.15 us  [add_parts(): pl.pallas_call(add_kernel, in_specs=[VMEM] * 4, out_specs=VMEM, out_shape...]
    all_to_all x1, starting transfers between devices: 9.49 us -> 8.06 us  [shards(): words = lax.all_to_all(words, CHIPS, 0, 0, tiled=True)]
    ppermute x9, starting transfers between devices: 15.5 us -> 16.8 us  [shards(): lax.ppermute(out, (axis, 'core'), shift(offset))]
  transfers between devices with their start and end apart: 13 -> 13, of which waited for: 6 -> 3; matrix products, arithmetic and copies ran while one was open for 2% -> 2% of each run, Pallas kernels for 5% -> 7%
where the time goes in v4:
time: 96.9 us; the launch traced here: 96.5 us
  starting transfers between devices  25.5 us (26%)
  waiting for transfers between devices  23.3 us (24%)
  Pallas kernels  22.9 us (24%)
  blocking collectives  20.4 us (21%)
  between operations  2.85 us (3%)
    all_to_all x1, blocking collectives, shards(): tops = lax.all_to_all(top_tile, ALL, 0, 0, tiled=True)  20.4 us
    all_to_all x1, waiting for transfers between devices, shards(): words = lax.all_to_all(words, CHIPS, 0, 0, tiled=True)  17.5 us
    ppermute x9, starting transfers between devices, shards(): lax.ppermute(out, (axis, 'core'), shift(offset))  16.8 us
    pallas_call x1, Pallas kernels, rotate_all(): pl.pallas_call(rotate_kernel, in_specs=[pl.BlockSpec(memory_space=pl.ANY)...  9.83 us
    all_to_all x1, starting transfers between devices, shards(): words = lax.all_to_all(words, CHIPS, 0, 0, tiled=True)  8.06 us
    pallas_call x4, Pallas kernels, levels_for(): pl.pallas_call(functools.partial(level_kernel, offset), in_specs=[VMEM] *...  7.92 us
    ppermute x9, waiting for transfers between devices, shards(): lax.ppermute(out, (axis, 'core'), shift(offset))  5.82 us
    pallas_call x3, Pallas kernels, add_parts(): pl.pallas_call(add_kernel, in_specs=[VMEM] * 4, out_specs=VMEM, out_shape...  3.15 us
  transfers between devices with their start and end apart: 13, of which 3 were waited for; matrix products, arithmetic and copies ran while one was open for 2% of the time, Pallas kernels for 7%

profile of v4, /device:TPU:0, one launch (start us, length us, event | category | flops | bytes accessed | tf_op | source)
XLA Modules:
  0.0 96.5 jit_solution(3041034382587294416)
XLA Ops:
  0.6 0.0 copy-start
  0.6 9.8 %shard_map.112 = (f32[16,128,512]{2,1,0:T(8,128)S(1)}, f32[16,128,512]{2,1,0:T(8,128)S(1)}, f32[16,128,512]{2,1,0:T(8,128)S(1)}, bf16[16,384,512]{2,1,0:T(8,128)(2,1)S(1)}, f32[128,128]{1,0:T(8,128)}) custom-call(bf16[16,2,384,512]{3,2,1,0:T(8,128)(2,1)} %bitcast.35, s32[64,512]{1,0:T(8,128)} %sign_ref.1, bf16[256,256]{1,0:T(8,128)(2,1)} %constant.32.clone.table_ref), custom_call_target="tpu_custom_call" | custom-call | flops 6000000000 | bytes 12000000 | tf_op jit(solution)/shard_map/pallas_call | solution.py:65
  10.5 0.1 collective-permute-start
  10.6 0.5 collective-permute-start.1
  11.1 0.1 collective-permute-start.2
  11.2 20.4 %all_to_all.16 = f32[128,1,128]{2,1,0:T(1,128)S(1)} all-to-all(f32[128,1,128]{2,1,0:T(1,128)} %bitcast.34), channel_id=1, replica_groups=mesh['x'=4,'z'=4,'y'=4,'core'=2] {'z','y','x','core'}, dimensions={0} | all-to-all | bytes 131072 | tf_op jit(solution)/shard_map/all_to_all | solution.py:225
  31.6 0.0 collective-permute-done
  31.6 0.0 collective-permute-done.1
  31.6 0.0 collective-permute-done.2
  31.6 0.0 copy-done
  31.6 2.0 %shard_map.114 = (f32[4,2,3,8,512]{4,3,2,1,0:T(8,128)S(1)}, f32[4,2,3,8,512]{4,3,2,1,0:T(8,128)S(1)}, f32[4,2,3,8,512]{4,3,2,1,0:T(8,128)S(1)}) custom-call(bf16[16,12,32,512]{3,2,1,0:T(8,128)(2,1)S(1)} %bitcast.13, f32[16,4,32,512]{3,2,1,0:T(8,128)S(1)} %bitcast.17, f32[16,4,32,512]{3,2,1,0:T(8,128)S(1)} %bitcast.21, f32[16,4,32,512]{3,2,1,0:T(8,128)S(1)} %bitcast.25, ...), custom_call_target="tpu_custom_call" | custom-call | flops 1000000000 | bytes 6000000 | tf_op jit(solution)/shard_map/pallas_call | solution.py:141
  33.6 0.6 collective-permute-start.3
  34.3 0.7 collective-permute-start.4
  35.0 1.9 %collective-permute-start.5 = (f32[4,2,3,8,512]{4,3,2,1,0:T(8,128)S(1)}, f32[4,2,3,8,512]{4,3,2,1,0:T(8,128)S(1)}, u32[]{:S(2)}, u32[]{:S(2)}) collective-permute-start(f32[4,2,3,8,512]{4,3,2,1,0:T(8,128)S(1)} %get-tuple-element.24), channel_id=1, source_target_pairs={{0,8},{1,25},{8,16},{9,1},{16,24},{17,9},{24,0},{25,17},{2,10},{3,... | collective-permute-start | bytes 1179656 | tf_op jit(solution)/shard_map/ppermute | solution.py:230
  36.9 2.0 %shard_map.116 = (f32[4,2,3,8,512]{4,3,2,1,0:T(8,128)S(1)}, f32[4,2,3,8,512]{4,3,2,1,0:T(8,128)S(1)}, f32[4,2,3,8,512]{4,3,2,1,0:T(8,128)S(1)}) custom-call(bf16[16,12,32,512]{3,2,1,0:T(8,128)(2,1)S(1)} %bitcast.14, f32[16,4,32,512]{3,2,1,0:T(8,128)S(1)} %bitcast.18, f32[16,4,32,512]{3,2,1,0:T(8,128)S(1)} %bitcast.22, f32[16,4,32,512]{3,2,1,0:T(8,128)S(1)} %bitcast.26, ...), custom_call_target="tpu_custom_call" | custom-call | flops 1000000000 | bytes 6000000 | tf_op jit(solution)/shard_map/pallas_call | solution.py:141
  39.0 1.8 %collective-permute-start.6 = (f32[4,2,3,8,512]{4,3,2,1,0:T(8,128)S(1)}, f32[4,2,3,8,512]{4,3,2,1,0:T(8,128)S(1)}, u32[]{:S(2)}, u32[]{:S(2)}) collective-permute-start(f32[4,2,3,8,512]{4,3,2,1,0:T(8,128)S(1)} %get-tuple-element.25), channel_id=1, source_target_pairs={{0,96},{1,33},{32,0},{33,65},{64,32},{65,97},{96,64},{97,1},{2,98}... | collective-permute-start | bytes 1179656 | tf_op jit(solution)/shard_map/ppermute | solution.py:230
  40.8 2.3 %collective-permute-start.7 = (f32[4,2,3,8,512]{4,3,2,1,0:T(8,128)S(1)}, f32[4,2,3,8,512]{4,3,2,1,0:T(8,128)S(1)}, u32[]{:S(2)}, u32[]{:S(2)}) collective-permute-start(f32[4,2,3,8,512]{4,3,2,1,0:T(8,128)S(1)} %get-tuple-element.26), channel_id=1, source_target_pairs={{0,6},{1,3},{2,0},{3,5},{4,2},{5,7},{6,4},{7,1},{8,14},{9,11},{10,... | collective-permute-start | bytes 1179656 | tf_op jit(solution)/shard_map/ppermute | solution.py:230
  43.1 0.0 collective-permute-done.3.part0
  43.1 2.4 %collective-permute-start.8 = (f32[4,2,3,8,512]{4,3,2,1,0:T(8,128)S(1)}, f32[4,2,3,8,512]{4,3,2,1,0:T(8,128)S(1)}, u32[]{:S(2)}, u32[]{:S(2)}) collective-permute-start(f32[4,2,3,8,512]{4,3,2,1,0:T(8,128)S(1)} %get-tuple-element.27), channel_id=1, source_target_pairs={{0,24},{1,9},{8,0},{9,17},{16,8},{17,25},{24,16},{25,1},{2,26},{3,... | collective-permute-start | bytes 1179656 | tf_op jit(solution)/shard_map/ppermute | solution.py:230
  45.6 2.1 %shard_map.118 = (f32[4,2,3,8,512]{4,3,2,1,0:T(8,128)S(1)}, f32[4,2,3,8,512]{4,3,2,1,0:T(8,128)S(1)}, f32[4,2,3,8,512]{4,3,2,1,0:T(8,128)S(1)}) custom-call(bf16[16,12,32,512]{3,2,1,0:T(8,128)(2,1)S(1)} %bitcast.15, f32[16,4,32,512]{3,2,1,0:T(8,128)S(1)} %bitcast.19, f32[16,4,32,512]{3,2,1,0:T(8,128)S(1)} %bitcast.23, f32[16,4,32,512]{3,2,1,0:T(8,128)S(1)} %bitcast.27, ...), custom_call_target="tpu_custom_call" | custom-call | flops 1000000000 | bytes 6000000 | tf_op jit(solution)/shard_map/pallas_call | solution.py:141
  47.6 0.0 collective-permute-done.4.part1
  47.6 2.8 %collective-permute-start.10 = (f32[4,2,3,8,512]{4,3,2,1,0:T(8,128)S(1)}, f32[4,2,3,8,512]{4,3,2,1,0:T(8,128)S(1)}, u32[]{:S(2)}, u32[]{:S(2)}) collective-permute-start(f32[4,2,3,8,512]{4,3,2,1,0:T(8,128)S(1)} %get-tuple-element.29), channel_id=1, source_target_pairs={{0,4},{1,5},{2,6},{3,7},{4,0},{5,1},{6,2},{7,3},{8,12},{9,13},{10,... | collective-permute-start | bytes 1179656 | tf_op jit(solution)/shard_map/ppermute | solution.py:230
  50.4 0.0 collective-permute-done.5.part2
  50.4 0.2 collective-permute-start.11
  50.6 0.0 collective-permute-done.6.part0
  50.6 3.9 %collective-permute-start.9 = (f32[4,2,3,8,512]{4,3,2,1,0:T(8,128)S(1)}, f32[4,2,3,8,512]{4,3,2,1,0:T(8,128)S(1)}, u32[]{:S(2)}, u32[]{:S(2)}) collective-permute-start(f32[4,2,3,8,512]{4,3,2,1,0:T(8,128)S(1)} %get-tuple-element.28), channel_id=1, source_target_pairs={{0,64},{1,65},{32,96},{33,97},{64,0},{65,1},{96,32},{97,33},{2,66}... | collective-permute-start | bytes 1179656 | tf_op jit(solution)/shard_map/ppermute | solution.py:230
  54.5 1.8 %shard_map.113.sums_ref = f32[4,4,4,48,128]{4,3,2,1,0:T(8,128)S(1)} custom-call(bf16[16,12,32,512]{3,2,1,0:T(8,128)(2,1)S(1)} %bitcast.16, f32[16,4,32,512]{3,2,1,0:T(8,128)S(1)} %bitcast.20, f32[16,4,32,512]{3,2,1,0:T(8,128)S(1)} %bitcast.24, f32[16,4,32,512]{3,2,1,0:T(8,128)S(1)} %bitcast.28, bf16[256,256]{1,0:T(8,128)(2,1)S(1)} %copy-done, ...), custom_call_target="tpu_custom_call" | custom-call | flops 1000000000 | bytes 6000000 | tf_op jit(solution)/shard_map/pallas_call | solution.py:141
  56.3 0.7 shard_map.115.sums_ref
  57.0 0.0 collective-permute-done.7.part1
  57.0 2.3 %collective-permute-done.8.part2 = f32[4,2,3,8,512]{4,3,2,1,0:T(8,128)S(1)} collective-permute-done((f32[4,2,3,8,512]{4,3,2,1,0:T(8,128)S(1)}, f32[4,2,3,8,512]{4,3,2,1,0:T(8,128)S(1)}, u32[]{:S(2)}, u32[]{:S(2)}) %collective-permute-start.8) | collective-permute-done | bytes 393248 | tf_op jit(solution)/shard_map/ppermute | solution.py:230
  59.3 0.7 shard_map.117.sums_ref
  60.0 0.0 copy-start.1
  60.0 0.0 copy-start.2
  60.0 0.0 copy-start.3
  60.0 0.0 copy-start.4
  60.0 0.0 collective-permute-done.10.part1
  60.0 0.0 collective-permute-done.11.part2
  60.0 3.5 %collective-permute-done.9.part0 = f32[4,2,3,8,512]{4,3,2,1,0:T(8,128)S(1)} collective-permute-done((f32[4,2,3,8,512]{4,3,2,1,0:T(8,128)S(1)}, f32[4,2,3,8,512]{4,3,2,1,0:T(8,128)S(1)}, u32[]{:S(2)}, u32[]{:S(2)}) %collective-permute-start.9) | collective-permute-done | bytes 393248 | tf_op jit(solution)/shard_map/ppermute | solution.py:230
  63.5 1.8 %shard_map.119 = f32[4,4,4,48,128]{4,3,2,1,0:T(8,128)} custom-call(f32[4,4,4,48,128]{4,3,2,1,0:T(8,128)S(1)} %shard_map.117.sums_ref, f32[4,2,3,8,512]{4,3,2,1,0:T(8,128)S(1)} %collective-permute-done.9.part0, f32[4,2,3,8,512]{4,3,2,1,0:T(8,128)S(1)} %collective-permute-done.10.part1, f32[4,2,3,8,512]{4,3,2,1,0:T(8,128)S(1)} %collective-permute-done.11.part2), custom_call_target="tpu_custom_call" | custom-call | flops 10000000 | bytes 4000000 | tf_op jit(solution)/shard_map/pallas_call | solution.py:168
  65.4 8.1 %all-to-all-start.1 = ((f32[64,48,128]{2,1,0:T(8,128)}), f32[64,48,128]{2,1,0:T(8,128)S(1)}, u32[]{:S(2)}, u32[]{:S(2)}) async-start(f32[64,48,128]{2,1,0:T(8,128)} %bitcast.10), calls=%async_computation.1 | async-start | bytes 3145728 | tf_op jit(solution)/shard_map/all_to_all | solution.py:235
  74.8 0.8 constant_dynamic-slice_fusion.sign_ref
  75.6 0.7 reduce_max.9
  77.0 0.1 pad_maximum_fusion.scalars
  77.1 17.5 %all-to-all-done.1 = f32[64,48,128]{2,1,0:T(8,128)S(1)} async-done(((f32[64,48,128]{2,1,0:T(8,128)}), f32[64,48,128]{2,1,0:T(8,128)S(1)}, u32[]{:S(2)}, u32[]{:S(2)}) %all-to-all-start.1) | async-done | bytes 1572896 | tf_op jit(solution)/shard_map/all_to_all | solution.py:235
  94.5 0.0 copy-done.1
  94.5 0.0 copy-done.2
  94.5 0.0 copy-done.4
  94.6 2.0 %shard_map.120 = (f32[384,128]{1,0:T(8,128)}, f32[384,128]{1,0:T(8,128)}, f32[384,128]{1,0:T(8,128)}) custom-call(f32[3]{0:T(128)S(1)} %pad_maximum_fusion.scalars, f32[4,4,4,48,128]{4,3,2,1,0:T(8,128)S(1)} %bitcast.29, bf16[128,128]{1,0:T(8,128)(2,1)S(1)} %copy-done.4, s32[64,128]{1,0:T(8,128)S(1)} %constant_dynamic-slice_fusion.sign_ref, ...), custom_call_target="tpu_custom_call" | custom-call | tf_op jit(solution)/shard_map/pallas_call | solution.py:248
  (1 shorter events, 0.0 us)
Async XLA Ops:
  0.6 31.0 %copy-start = (bf16[256,256]{1,0:T(8,128)(2,1)S(1)}, bf16[256,256]{1,0:T(8,128)(2,1)}, u32[]{:S(2)}) copy-start(bf16[256,256]{1,0:T(8,128)(2,1)} %constant.32.clone.table_ref) | copy-start | bytes 393220
  10.5 21.1 %collective-permute-start = (f32[16,128,512]{2,1,0:T(8,128)S(1)}, f32[16,128,512]{2,1,0:T(8,128)S(1)}, u32[]{:S(2)}, u32[]{:S(2)}) collective-permute-start(f32[16,128,512]{2,1,0:T(8,128)S(1)} %get-tuple-element.19), channel_id=1, source_target_pairs={{0,1},{1,0},{2,3},{3,2},{4,5},{5,4},{6,7},{7,6},{8,9},{9,8},{10,11... | collective-permute-start | bytes 12582920 | tf_op jit(solution)/shard_map/ppermute | solution.py:224
  10.6 21.0 %collective-permute-start.1 = (f32[16,128,512]{2,1,0:T(8,128)S(1)}, f32[16,128,512]{2,1,0:T(8,128)S(1)}, u32[]{:S(2)}, u32[]{:S(2)}) collective-permute-start(f32[16,128,512]{2,1,0:T(8,128)S(1)} %get-tuple-element.20), channel_id=1, source_target_pairs={{0,1},{1,0},{2,3},{3,2},{4,5},{5,4},{6,7},{7,6},{8,9},{9,8},{10,11... | collective-permute-start | bytes 12582920 | tf_op jit(solution)/shard_map/ppermute | solution.py:224
  11.1 20.5 %collective-permute-start.2 = (f32[16,128,512]{2,1,0:T(8,128)S(1)}, f32[16,128,512]{2,1,0:T(8,128)S(1)}, u32[]{:S(2)}, u32[]{:S(2)}) collective-permute-start(f32[16,128,512]{2,1,0:T(8,128)S(1)} %get-tuple-element.21), channel_id=1, source_target_pairs={{0,1},{1,0},{2,3},{3,2},{4,5},{5,4},{6,7},{7,6},{8,9},{9,8},{10,11... | collective-permute-start | bytes 12582920 | tf_op jit(solution)/shard_map/ppermute | solution.py:224
  33.6 9.5 %collective-permute-start.3 = (f32[4,2,3,8,512]{4,3,2,1,0:T(8,128)S(1)}, f32[4,2,3,8,512]{4,3,2,1,0:T(8,128)S(1)}, u32[]{:S(2)}, u32[]{:S(2)}) collective-permute-start(f32[4,2,3,8,512]{4,3,2,1,0:T(8,128)S(1)} %get-tuple-element.22), channel_id=1, source_target_pairs={{0,32},{1,97},{32,64},{33,1},{64,96},{65,33},{96,0},{97,65},{2,34}... | collective-permute-start | bytes 1179656 | tf_op jit(solution)/shard_map/ppermute | solution.py:230
  34.3 13.3 %collective-permute-start.4 = (f32[4,2,3,8,512]{4,3,2,1,0:T(8,128)S(1)}, f32[4,2,3,8,512]{4,3,2,1,0:T(8,128)S(1)}, u32[]{:S(2)}, u32[]{:S(2)}) collective-permute-start(f32[4,2,3,8,512]{4,3,2,1,0:T(8,128)S(1)} %get-tuple-element.23), channel_id=1, source_target_pairs={{0,2},{1,7},{2,4},{3,1},{4,6},{5,3},{6,0},{7,5},{8,10},{9,15},{10,... | collective-permute-start | bytes 1179656 | tf_op jit(solution)/shard_map/ppermute | solution.py:230
  35.0 15.4 %collective-permute-start.5 = (f32[4,2,3,8,512]{4,3,2,1,0:T(8,128)S(1)}, f32[4,2,3,8,512]{4,3,2,1,0:T(8,128)S(1)}, u32[]{:S(2)}, u32[]{:S(2)}) collective-permute-start(f32[4,2,3,8,512]{4,3,2,1,0:T(8,128)S(1)} %get-tuple-element.24), channel_id=1, source_target_pairs={{0,8},{1,25},{8,16},{9,1},{16,24},{17,9},{24,0},{25,17},{2,10},{3,... | collective-permute-start | bytes 1179656 | tf_op jit(solution)/shard_map/ppermute | solution.py:230
  39.0 11.6 %collective-permute-start.6 = (f32[4,2,3,8,512]{4,3,2,1,0:T(8,128)S(1)}, f32[4,2,3,8,512]{4,3,2,1,0:T(8,128)S(1)}, u32[]{:S(2)}, u32[]{:S(2)}) collective-permute-start(f32[4,2,3,8,512]{4,3,2,1,0:T(8,128)S(1)} %get-tuple-element.25), channel_id=1, source_target_pairs={{0,96},{1,33},{32,0},{33,65},{64,32},{65,97},{96,64},{97,1},{2,98}... | collective-permute-start | bytes 1179656 | tf_op jit(solution)/shard_map/ppermute | solution.py:230
  40.8 16.2 %collective-permute-start.7 = (f32[4,2,3,8,512]{4,3,2,1,0:T(8,128)S(1)}, f32[4,2,3,8,512]{4,3,2,1,0:T(8,128)S(1)}, u32[]{:S(2)}, u32[]{:S(2)}) collective-permute-start(f32[4,2,3,8,512]{4,3,2,1,0:T(8,128)S(1)} %get-tuple-element.26), channel_id=1, source_target_pairs={{0,6},{1,3},{2,0},{3,5},{4,2},{5,7},{6,4},{7,1},{8,14},{9,11},{10,... | collective-permute-start | bytes 1179656 | tf_op jit(solution)/shard_map/ppermute | solution.py:230
  43.1 16.2 %collective-permute-start.8 = (f32[4,2,3,8,512]{4,3,2,1,0:T(8,128)S(1)}, f32[4,2,3,8,512]{4,3,2,1,0:T(8,128)S(1)}, u32[]{:S(2)}, u32[]{:S(2)}) collective-permute-start(f32[4,2,3,8,512]{4,3,2,1,0:T(8,128)S(1)} %get-tuple-element.27), channel_id=1, source_target_pairs={{0,24},{1,9},{8,0},{9,17},{16,8},{17,25},{24,16},{25,1},{2,26},{3,... | collective-permute-start | bytes 1179656 | tf_op jit(solution)/shard_map/ppermute | solution.py:230
  47.6 12.4 %collective-permute-start.10 = (f32[4,2,3,8,512]{4,3,2,1,0:T(8,128)S(1)}, f32[4,2,3,8,512]{4,3,2,1,0:T(8,128)S(1)}, u32[]{:S(2)}, u32[]{:S(2)}) collective-permute-start(f32[4,2,3,8,512]{4,3,2,1,0:T(8,128)S(1)} %get-tuple-element.29), channel_id=1, source_target_pairs={{0,4},{1,5},{2,6},{3,7},{4,0},{5,1},{6,2},{7,3},{8,12},{9,13},{10,... | collective-permute-start | bytes 1179656 | tf_op jit(solution)/shard_map/ppermute | solution.py:230
  50.4 9.6 %collective-permute-start.11 = (f32[4,2,3,8,512]{4,3,2,1,0:T(8,128)S(1)}, f32[4,2,3,8,512]{4,3,2,1,0:T(8,128)S(1)}, u32[]{:S(2)}, u32[]{:S(2)}) collective-permute-start(f32[4,2,3,8,512]{4,3,2,1,0:T(8,128)S(1)} %get-tuple-element.30), channel_id=1, source_target_pairs={{0,16},{1,17},{8,24},{9,25},{16,0},{17,1},{24,8},{25,9},{2,18},{3,... | collective-permute-start | bytes 1179656 | tf_op jit(solution)/shard_map/ppermute | solution.py:230
  50.6 13.0 %collective-permute-start.9 = (f32[4,2,3,8,512]{4,3,2,1,0:T(8,128)S(1)}, f32[4,2,3,8,512]{4,3,2,1,0:T(8,128)S(1)}, u32[]{:S(2)}, u32[]{:S(2)}) collective-permute-start(f32[4,2,3,8,512]{4,3,2,1,0:T(8,128)S(1)} %get-tuple-element.28), channel_id=1, source_target_pairs={{0,64},{1,65},{32,96},{33,97},{64,0},{65,1},{96,32},{97,33},{2,66}... | collective-permute-start | bytes 1179656 | tf_op jit(solution)/shard_map/ppermute | solution.py:230
  60.0 34.6 %copy-start.1 = (f32[384,128]{1,0:T(8,128)S(1)}, f32[384,128]{1,0:T(8,128)}, u32[]{:S(2)}) copy-start(f32[384,128]{1,0:T(8,128)} %weights_ref.1) | copy-start | bytes 589828
  60.0 34.6 %copy-start.2 = (f32[384,128]{1,0:T(8,128)S(1)}, f32[384,128]{1,0:T(8,128)}, u32[]{:S(2)}) copy-start(f32[384,128]{1,0:T(8,128)} %first_ref.1) | copy-start | bytes 589828
  60.0 34.5 %copy-start.3 = (f32[384,128]{1,0:T(8,128)S(1)}, f32[384,128]{1,0:T(8,128)}, u32[]{:S(2)}) copy-start(f32[384,128]{1,0:T(8,128)} %second_ref.1) | copy-start | bytes 589828
  60.0 34.5 %copy-start.4 = (bf16[128,128]{1,0:T(8,128)(2,1)S(1)}, bf16[128,128]{1,0:T(8,128)(2,1)}, u32[]{:S(2)}) copy-start(bf16[128,128]{1,0:T(8,128)(2,1)} %constant.31.clone.table_ref) | copy-start | bytes 98308
  65.4 29.2 %all-to-all-start.1 = ((f32[64,48,128]{2,1,0:T(8,128)}), f32[64,48,128]{2,1,0:T(8,128)S(1)}, u32[]{:S(2)}, u32[]{:S(2)}) async-start(f32[64,48,128]{2,1,0:T(8,128)} %bitcast.10), calls=%async_computation.1 | async-start | bytes 3145728 | tf_op jit(solution)/shard_map/all_to_all | solution.py:235

commit v5 on v4

--- a/solution.py
+++ b/solution.py
@@ -16,7 +16,7 @@
 CHIPS = ("z", "y", "x")
 ALL = ("z", "y", "x", "core")
 INTRA = ("z", "y", "core")
-FIRST = ("x", "y", "z")
+MESH = ("x", "z", "y", "core")
 FIELD = 4096.0
 F32 = jnp.float32
 BF16 = jnp.bfloat16
@@ -50,12 +50,14 @@
             mine = buffer[i, core, rows, :] * wide
             own_ref[i, rows, :] = mine
             other = buffer[i, 1 - core, rows, :] * wide
-            block = jnp.concatenate([v[:, 256 * h : 256 * h + 256] for v in (other, mine) for h in range(2)], axis=0)
-            turned = jnp.dot(block, table, preferred_element_type=F32) * ROOT
-            raw_ref[i, :, :256] = turned[:128]
-            raw_ref[i, :, 256:] = turned[128:256]
-            best = jnp.maximum(best, fold(turned))
-    top_ref[...] = jnp.broadcast_to(jnp.max(best, axis=(0, 1), keepdims=True), (128, 128))
+            for v, keep in ((other, True), (mine, False)):
+                block = jnp.concatenate([v[:, :256], v[:, 256:]], axis=0)
+                turned = jnp.dot(block, table, preferred_element_type=F32)
+                if keep:
+                    raw_ref[i, :, :256] = turned[:128] * ROOT
+                    raw_ref[i, :, 256:] = turned[128:] * ROOT
+                best = jnp.maximum(best, fold(turned))
+    top_ref[...] = jnp.broadcast_to(jnp.max(best, axis=(0, 1), keepdims=True) * ROOT, (128, 128))
 
 
 VMEM = pl.BlockSpec(memory_space=pltpu.VMEM)
@@ -103,8 +105,10 @@
 def level_kernel(offset, own_ref, raw0, raw1, raw2, table_ref, top_ref, *outs):
     table = table_ref[...]
     scale = 127.0 / jnp.max(top_ref[...], axis=(0, 1), keepdims=True)
-    ahead = jnp.where(lax.axis_index("core") == 0, offset, (4 - offset) % 4)
-    quarters = [lax.rem(lax.axis_index(axis) + ahead, 4) for axis in FIRST]
+    even = lax.axis_index("core") == 0
+    flat = lax.rem(jnp.where(even, lax.axis_index("x"), lax.axis_index("y")) + offset, 4)
+    ahead = jnp.where(even, offset, (4 - offset) % 4)
+    quarters = [flat, flat, lax.rem(lax.axis_index("z") + ahead, 4)]
     raws = (raw0, raw1, raw2)
 
     def plane(z, carry):
@@ -123,7 +127,11 @@
                         groups += [total[8 * g : 8 * g + 8] for g in range(4)]
                     if offset:
                         for i, word in enumerate(pack_eight(groups)):
-                            outs[t][z, pair, i, :, 256 * h : 256 * h + 256] = word
+                            cols = slice(256 * h, 256 * h + 256)
+                            if t < 2:
+                                outs[0][t, z, pair, i, :, cols] = word
+                            else:
+                                outs[1][z, pair, i, :, cols] = word
                         continue
                     for k in range(2):
                         low, lower, high, higher = groups[4 * k : 4 * k + 4]
@@ -137,20 +145,20 @@
 
 
 def levels_for(offset, own, raws, table, tops):
-    shapes = [(4, 2, 3, 8, 512)] * 3 if offset else [(4, 4, 4, 48, 128)]
+    shapes = [(2, 4, 2, 3, 8, 512), (4, 2, 3, 8, 512)] if offset else [(4, 4, 4, 48, 128)]
     return pl.pallas_call(
         functools.partial(level_kernel, offset),
         in_specs=[VMEM] * 6,
         out_specs=[VMEM] * len(shapes),
         out_shape=[pltpu.VMEM(shape, F32) for shape in shapes],
         compiler_params=pltpu.CompilerParams(vmem_limit_bytes=12 * 2**20),
-        cost_estimate=pl.CostEstimate(flops=10**9, bytes_accessed=6 * 10**6, transcendentals=0),
+        cost_estimate=pl.CostEstimate(flops=10**6, bytes_accessed=10**4, transcendentals=0),
     )(own.reshape(16, 12, 32, 512), *[raw.reshape(16, 4, 32, 512) for raw in raws], table, tops)
 
 
-def add_kernel(sums_ref, part0, part1, part2, out_ref):
+def add_kernel(sums_ref, flat_ref, tall_ref, out_ref):
     def plane(z, carry):
-        for t, part in enumerate((part0, part1, part2)):
+        for t, part in enumerate((flat_ref.at[0], flat_ref.at[1], tall_ref)):
             for pair in range(2):
                 v = unpack_eight([part[z, pair, i] for i in range(3)])
                 for k in range(2):
@@ -167,7 +175,7 @@
 def add_parts(sums, parts):
     return pl.pallas_call(
         add_kernel,
-        in_specs=[VMEM] * 4,
+        in_specs=[VMEM] * 3,
         out_specs=VMEM,
         out_shape=pltpu.VMEM((4, 4, 4, 48, 128), F32),
         compiler_params=pltpu.CompilerParams(vmem_limit_bytes=12 * 2**20),
@@ -179,12 +187,13 @@
     scalars, words_ref, table_ref, sign_ref, weights_ref, first_ref, second_ref, weights_out, first_out, second_out
 ):
     table = table_ref[...]
+    even = lax.axis_index("core") == 0
     for t in range(3):
         for q in range(4):
             parts = []
             for a in range(4):
                 for b in range(4):
-                    x, z, y = ((q, a, b), (a, b, q), (a, q, b))[t]
+                    z, y, x = (a, jnp.where(even, b, q), jnp.where(even, q, b)) if t < 2 else (q, a, b)
                     parts.append(words_ref[z, y, x, 16 * t : 16 * t + 16, :])
             low = high = jnp.zeros((16, 128), F32)
             for word in parts:
@@ -208,7 +217,13 @@
             second_out[rows, :] = second
 
 
-def shift(amount):
+def shift_flat(amount):
+    index = np.arange(128).reshape(4, 4, 4, 2)
+    ahead = np.stack([np.roll(index[..., 0], -amount, axis=0), np.roll(index[..., 1], -amount, axis=2)], axis=-1)
+    return [(int(source), int(target)) for source, target in zip(index.ravel(), ahead.ravel())]
+
+
+def shift_tall(amount):
     return [
         (2 * i + core, 2 * ((i + (amount if core == 0 else -amount)) % 4) + core)
         for i in range(4)
@@ -226,8 +241,9 @@
 
     arrived = []
     for offset in (1, 3, 2):
-        outs = levels_for(offset, own, raws, twice, tops)
-        arrived.append([lax.ppermute(out, (axis, "core"), shift(offset)) for out, axis in zip(outs, FIRST)])
+        flat, tall = levels_for(offset, own, raws, twice, tops)
+        flat = lax.ppermute(flat, MESH, shift_flat(offset))
+        arrived.append((flat, lax.ppermute(tall, ("z", "core"), shift_tall(offset))))
     (words,) = levels_for(0, own, raws, twice, tops)
     for parts in arrived:
         words = add_parts(words, parts)

time: 96.9 us -> 96.3 us (level)
  waiting for transfers between devices: 23.3 us -> 29.9 us
  starting transfers between devices: 25.5 us -> 19.1 us
    ppermute x9 -> x6, starting transfers between devices: 16.8 us -> 10.1 us  [the longest x3 5.49 us: shards(): lax.ppermute(tall, ('z', 'core'), shift_tall(offset))]
    ppermute x9 -> x6, waiting for transfers between devices: 5.82 us -> 10.1 us  [the longest x3 10.1 us: shards(): lax.ppermute(tall, ('z', 'core'), shift_tall(offset))]
    all_to_all x1, waiting for transfers between devices: 17.5 us -> 19.8 us  [shards(): words = lax.all_to_all(words, CHIPS, 0, 0, tiled=True)]
  transfers between devices with their start and end apart: 13 -> 10, of which waited for: 3 -> 4; matrix products, arithmetic and copies ran while one was open for 2% -> 2% of each run, Pallas kernels for 7% -> 8%
where the time goes in v5:
time: 96.3 us; the launch traced here: 96 us
  waiting for transfers between devices  29.9 us (31%)
  Pallas kernels  22.1 us (23%)
  blocking collectives  20.4 us (21%)
  starting transfers between devices  19.1 us (20%)
  between operations  2.82 us (3%)
    all_to_all x1, blocking collectives, shards(): tops = lax.all_to_all(top_tile, ALL, 0, 0, tiled=True)  20.4 us
    all_to_all x1, waiting for transfers between devices, shards(): words = lax.all_to_all(words, CHIPS, 0, 0, tiled=True)  19.8 us
    ppermute x3, waiting for transfers between devices, shards(): lax.ppermute(tall, ('z', 'core'), shift_tall(offset))  10.1 us
    pallas_call x1, Pallas kernels, rotate_all(): pl.pallas_call(rotate_kernel, in_specs=[pl.BlockSpec(memory_space=pl.ANY)...  9.05 us
    all_to_all x1, starting transfers between devices, shards(): words = lax.all_to_all(words, CHIPS, 0, 0, tiled=True)  8.31 us
    pallas_call x4, Pallas kernels, levels_for(): pl.pallas_call(functools.partial(level_kernel, offset), in_specs=[VMEM] *...  7.93 us
    ppermute x3, starting transfers between devices, shards(): lax.ppermute(tall, ('z', 'core'), shift_tall(offset))  5.49 us
    ppermute x3, starting transfers between devices, shards(): flat = lax.ppermute(flat, MESH, shift_flat(offset))  4.61 us
  transfers between devices with their start and end apart: 10, of which 4 were waited for; matrix products, arithmetic and copies ran while one was open for 2% of the time, Pallas kernels for 8%

profile of v5, /device:TPU:0, one launch (start us, length us, event | category | flops | bytes accessed | tf_op | source)
XLA Modules:
  0.0 96.0 jit_solution(4715021605097076095)
XLA Ops:
  0.6 0.0 copy-start
  0.6 9.1 %shard_map.112 = (f32[16,128,512]{2,1,0:T(8,128)S(1)}, f32[16,128,512]{2,1,0:T(8,128)S(1)}, f32[16,128,512]{2,1,0:T(8,128)S(1)}, bf16[16,384,512]{2,1,0:T(8,128)(2,1)S(1)}, f32[128,128]{1,0:T(8,128)}) custom-call(bf16[16,2,384,512]{3,2,1,0:T(8,128)(2,1)} %bitcast.35, s32[64,512]{1,0:T(8,128)} %sign_ref.1, bf16[256,256]{1,0:T(8,128)(2,1)} %constant.32.clone.table_ref), custom_call_target="tpu_custom_call" | custom-call | flops 6000000000 | bytes 12000000 | tf_op jit(solution)/shard_map/pallas_call | solution.py:67
  9.7 0.1 collective-permute-start
  9.8 0.5 collective-permute-start.1
  10.3 0.1 collective-permute-start.2
  10.4 20.4 %all_to_all.16 = f32[128,1,128]{2,1,0:T(1,128)S(1)} all-to-all(f32[128,1,128]{2,1,0:T(1,128)} %bitcast.34), channel_id=1, replica_groups=mesh['x'=4,'z'=4,'y'=4,'core'=2] {'z','y','x','core'}, dimensions={0} | all-to-all | bytes 131072 | tf_op jit(solution)/shard_map/all_to_all | solution.py:240
  30.8 0.0 collective-permute-done
  30.8 0.0 collective-permute-done.1
  30.8 0.0 collective-permute-done.2
  30.8 0.0 copy-done
  30.8 2.0 %shard_map.114 = (f32[2,4,2,3,8,512]{5,4,3,2,1,0:T(8,128)S(1)}, f32[4,2,3,8,512]{4,3,2,1,0:T(8,128)S(1)}) custom-call(bf16[16,12,32,512]{3,2,1,0:T(8,128)(2,1)S(1)} %bitcast.13, f32[16,4,32,512]{3,2,1,0:T(8,128)S(1)} %bitcast.17, f32[16,4,32,512]{3,2,1,0:T(8,128)S(1)} %bitcast.21, f32[16,4,32,512]{3,2,1,0:T(8,128)S(1)} %bitcast.25, ...), custom_call_target="tpu_custom_call" | custom-call | flops 1000000 | bytes 10000 | tf_op jit(solution)/shard_map/pallas_call | solution.py:149
  32.9 0.7 collective-permute-start.3
  33.5 2.0 %shard_map.116 = (f32[2,4,2,3,8,512]{5,4,3,2,1,0:T(8,128)S(1)}, f32[4,2,3,8,512]{4,3,2,1,0:T(8,128)S(1)}) custom-call(bf16[16,12,32,512]{3,2,1,0:T(8,128)(2,1)S(1)} %bitcast.14, f32[16,4,32,512]{3,2,1,0:T(8,128)S(1)} %bitcast.18, f32[16,4,32,512]{3,2,1,0:T(8,128)S(1)} %bitcast.22, f32[16,4,32,512]{3,2,1,0:T(8,128)S(1)} %bitcast.26, ...), custom_call_target="tpu_custom_call" | custom-call | flops 1000000 | bytes 10000 | tf_op jit(solution)/shard_map/pallas_call | solution.py:149
  35.6 2.7 %collective-permute-start.5 = (f32[2,4,2,3,8,512]{5,4,3,2,1,0:T(8,128)S(1)}, f32[2,4,2,3,8,512]{5,4,3,2,1,0:T(8,128)S(1)}, u32[]{:S(2)}, u32[]{:S(2)}) collective-permute-start(f32[2,4,2,3,8,512]{5,4,3,2,1,0:T(8,128)S(1)} %get-tuple-element.21), channel_id=1, source_target_pairs={{0,96},{1,7},{2,98},{3,1},{4,100},{5,3},{6,102},{7,5},{8,104},{9,1... | collective-permute-start | bytes 2359304 | tf_op jit(solution)/shard_map/ppermute | solution.py:245
  38.3 0.8 collective-permute-start.4
  39.1 2.0 %shard_map.118 = (f32[2,4,2,3,8,512]{5,4,3,2,1,0:T(8,128)S(1)}, f32[4,2,3,8,512]{4,3,2,1,0:T(8,128)S(1)}) custom-call(bf16[16,12,32,512]{3,2,1,0:T(8,128)(2,1)S(1)} %bitcast.15, f32[16,4,32,512]{3,2,1,0:T(8,128)S(1)} %bitcast.19, f32[16,4,32,512]{3,2,1,0:T(8,128)S(1)} %bitcast.23, f32[16,4,32,512]{3,2,1,0:T(8,128)S(1)} %bitcast.27, ...), custom_call_target="tpu_custom_call" | custom-call | flops 1000000 | bytes 10000 | tf_op jit(solution)/shard_map/pallas_call | solution.py:149
  41.1 1.2 %collective-permute-start.7 = (f32[2,4,2,3,8,512]{5,4,3,2,1,0:T(8,128)S(1)}, f32[2,4,2,3,8,512]{5,4,3,2,1,0:T(8,128)S(1)}, u32[]{:S(2)}, u32[]{:S(2)}) collective-permute-start(f32[2,4,2,3,8,512]{5,4,3,2,1,0:T(8,128)S(1)} %get-tuple-element.23), channel_id=1, source_target_pairs={{0,64},{1,5},{2,66},{3,7},{4,68},{5,1},{6,70},{7,3},{8,72},{9,13},... | collective-permute-start | bytes 2359304 | tf_op jit(solution)/shard_map/ppermute | solution.py:245
  42.4 2.1 %collective-permute-start.6 = (f32[4,2,3,8,512]{4,3,2,1,0:T(8,128)S(1)}, f32[4,2,3,8,512]{4,3,2,1,0:T(8,128)S(1)}, u32[]{:S(2)}, u32[]{:S(2)}) collective-permute-start(f32[4,2,3,8,512]{4,3,2,1,0:T(8,128)S(1)} %get-tuple-element.22), channel_id=1, source_target_pairs={{0,24},{1,9},{8,0},{9,17},{16,8},{17,25},{24,16},{25,1},{2,26},{3,... | collective-permute-start | bytes 1179656 | tf_op jit(solution)/shard_map/ppermute | solution.py:246
  44.5 2.8 %collective-permute-done.4.tall_ref = f32[4,2,3,8,512]{4,3,2,1,0:T(8,128)S(1)} collective-permute-done((f32[4,2,3,8,512]{4,3,2,1,0:T(8,128)S(1)}, f32[4,2,3,8,512]{4,3,2,1,0:T(8,128)S(1)}, u32[]{:S(2)}, u32[]{:S(2)}) %collective-permute-start.4) | collective-permute-done | bytes 393248 | tf_op jit(solution)/shard_map/ppermute | solution.py:246
  47.3 2.6 %collective-permute-start.8 = (f32[4,2,3,8,512]{4,3,2,1,0:T(8,128)S(1)}, f32[4,2,3,8,512]{4,3,2,1,0:T(8,128)S(1)}, u32[]{:S(2)}, u32[]{:S(2)}) collective-permute-start(f32[4,2,3,8,512]{4,3,2,1,0:T(8,128)S(1)} %get-tuple-element.24), channel_id=1, source_target_pairs={{0,16},{1,17},{8,24},{9,25},{16,0},{17,1},{24,8},{25,9},{2,18},{3,... | collective-permute-start | bytes 1179656 | tf_op jit(solution)/shard_map/ppermute | solution.py:246
  49.8 1.8 %shard_map.113.sums_ref = f32[4,4,4,48,128]{4,3,2,1,0:T(8,128)S(1)} custom-call(bf16[16,12,32,512]{3,2,1,0:T(8,128)(2,1)S(1)} %bitcast.16, f32[16,4,32,512]{3,2,1,0:T(8,128)S(1)} %bitcast.20, f32[16,4,32,512]{3,2,1,0:T(8,128)S(1)} %bitcast.24, f32[16,4,32,512]{3,2,1,0:T(8,128)S(1)} %bitcast.28, bf16[256,256]{1,0:T(8,128)(2,1)S(1)} %copy-done, ...), custom_call_target="tpu_custom_call" | custom-call | flops 1000000 | bytes 10000 | tf_op jit(solution)/shard_map/pallas_call | solution.py:149
  51.7 0.0 collective-permute-done.3.flat_ref
  51.7 0.7 shard_map.115.sums_ref
  52.3 5.9 %collective-permute-done.6.tall_ref = f32[4,2,3,8,512]{4,3,2,1,0:T(8,128)S(1)} collective-permute-done((f32[4,2,3,8,512]{4,3,2,1,0:T(8,128)S(1)}, f32[4,2,3,8,512]{4,3,2,1,0:T(8,128)S(1)}, u32[]{:S(2)}, u32[]{:S(2)}) %collective-permute-start.6) | collective-permute-done | bytes 393248 | tf_op jit(solution)/shard_map/ppermute | solution.py:246
  58.3 0.0 collective-permute-done.5.flat_ref
  58.3 0.7 shard_map.117.sums_ref
  58.9 0.0 copy-start.1
  58.9 0.0 copy-start.2
  59.0 0.0 copy-start.3
  59.0 0.0 copy-start.4
  59.0 1.4 %collective-permute-done.8.tall_ref = f32[4,2,3,8,512]{4,3,2,1,0:T(8,128)S(1)} collective-permute-done((f32[4,2,3,8,512]{4,3,2,1,0:T(8,128)S(1)}, f32[4,2,3,8,512]{4,3,2,1,0:T(8,128)S(1)}, u32[]{:S(2)}, u32[]{:S(2)}) %collective-permute-start.8) | collective-permute-done | bytes 393248 | tf_op jit(solution)/shard_map/ppermute | solution.py:246
  60.4 0.0 collective-permute-done.7.flat_ref
  60.4 1.8 %shard_map.119 = f32[4,4,4,48,128]{4,3,2,1,0:T(8,128)} custom-call(f32[4,4,4,48,128]{4,3,2,1,0:T(8,128)S(1)} %shard_map.117.sums_ref, f32[2,4,2,3,8,512]{5,4,3,2,1,0:T(8,128)S(1)} %collective-permute-done.7.flat_ref, f32[4,2,3,8,512]{4,3,2,1,0:T(8,128)S(1)} %collective-permute-done.8.tall_ref), custom_call_target="tpu_custom_call" | custom-call | flops 10000000 | bytes 4000000 | tf_op jit(solution)/shard_map/pallas_call | solution.py:176
  62.2 8.3 %all-to-all-start.1 = ((f32[64,48,128]{2,1,0:T(8,128)}), f32[64,48,128]{2,1,0:T(8,128)S(1)}, u32[]{:S(2)}, u32[]{:S(2)}) async-start(f32[64,48,128]{2,1,0:T(8,128)} %bitcast.10), calls=%async_computation.1 | async-start | bytes 3145728 | tf_op jit(solution)/shard_map/all_to_all | solution.py:251
  71.9 0.8 constant_dynamic-slice_fusion.sign_ref
  72.7 0.7 reduce_max.9
  74.1 0.1 pad_maximum_fusion.scalars
  74.2 19.8 %all-to-all-done.1 = f32[64,48,128]{2,1,0:T(8,128)S(1)} async-done(((f32[64,48,128]{2,1,0:T(8,128)}), f32[64,48,128]{2,1,0:T(8,128)S(1)}, u32[]{:S(2)}, u32[]{:S(2)}) %all-to-all-start.1) | async-done | bytes 1572896 | tf_op jit(solution)/shard_map/all_to_all | solution.py:251
  94.0 0.0 copy-done.1
  94.0 0.0 copy-done.2
  94.0 0.0 copy-done.3
  94.0 0.0 copy-done.4
  94.0 2.0 %shard_map.120 = (f32[384,128]{1,0:T(8,128)}, f32[384,128]{1,0:T(8,128)}, f32[384,128]{1,0:T(8,128)}) custom-call(f32[3]{0:T(128)S(1)} %pad_maximum_fusion.scalars, f32[4,4,4,48,128]{4,3,2,1,0:T(8,128)S(1)} %bitcast.29, bf16[128,128]{1,0:T(8,128)(2,1)S(1)} %copy-done.4, s32[64,128]{1,0:T(8,128)S(1)} %constant_dynamic-slice_fusion.sign_ref, ...), custom_call_target="tpu_custom_call" | custom-call | tf_op jit(solution)/shard_map/pallas_call | solution.py:264
Async XLA Ops:
  0.6 30.2 %copy-start = (bf16[256,256]{1,0:T(8,128)(2,1)S(1)}, bf16[256,256]{1,0:T(8,128)(2,1)}, u32[]{:S(2)}) copy-start(bf16[256,256]{1,0:T(8,128)(2,1)} %constant.32.clone.table_ref) | copy-start | bytes 393220
  9.7 21.1 %collective-permute-start = (f32[16,128,512]{2,1,0:T(8,128)S(1)}, f32[16,128,512]{2,1,0:T(8,128)S(1)}, u32[]{:S(2)}, u32[]{:S(2)}) collective-permute-start(f32[16,128,512]{2,1,0:T(8,128)S(1)} %get-tuple-element.16), channel_id=1, source_target_pairs={{0,1},{1,0},{2,3},{3,2},{4,5},{5,4},{6,7},{7,6},{8,9},{9,8},{10,11... | collective-permute-start | bytes 12582920 | tf_op jit(solution)/shard_map/ppermute | solution.py:239
  9.8 21.0 %collective-permute-start.1 = (f32[16,128,512]{2,1,0:T(8,128)S(1)}, f32[16,128,512]{2,1,0:T(8,128)S(1)}, u32[]{:S(2)}, u32[]{:S(2)}) collective-permute-start(f32[16,128,512]{2,1,0:T(8,128)S(1)} %get-tuple-element.17), channel_id=1, source_target_pairs={{0,1},{1,0},{2,3},{3,2},{4,5},{5,4},{6,7},{7,6},{8,9},{9,8},{10,11... | collective-permute-start | bytes 12582920 | tf_op jit(solution)/shard_map/ppermute | solution.py:239
  10.3 20.5 %collective-permute-start.2 = (f32[16,128,512]{2,1,0:T(8,128)S(1)}, f32[16,128,512]{2,1,0:T(8,128)S(1)}, u32[]{:S(2)}, u32[]{:S(2)}) collective-permute-start(f32[16,128,512]{2,1,0:T(8,128)S(1)} %get-tuple-element.18), channel_id=1, source_target_pairs={{0,1},{1,0},{2,3},{3,2},{4,5},{5,4},{6,7},{7,6},{8,9},{9,8},{10,11... | collective-permute-start | bytes 12582920 | tf_op jit(solution)/shard_map/ppermute | solution.py:239
  32.9 18.8 %collective-permute-start.3 = (f32[2,4,2,3,8,512]{5,4,3,2,1,0:T(8,128)S(1)}, f32[2,4,2,3,8,512]{5,4,3,2,1,0:T(8,128)S(1)}, u32[]{:S(2)}, u32[]{:S(2)}) collective-permute-start(f32[2,4,2,3,8,512]{5,4,3,2,1,0:T(8,128)S(1)} %get-tuple-element.19), channel_id=1, source_target_pairs={{0,32},{1,3},{2,34},{3,5},{4,36},{5,7},{6,38},{7,1},{8,40},{9,11},... | collective-permute-start | bytes 2359304 | tf_op jit(solution)/shard_map/ppermute | solution.py:245
  35.6 22.7 %collective-permute-start.5 = (f32[2,4,2,3,8,512]{5,4,3,2,1,0:T(8,128)S(1)}, f32[2,4,2,3,8,512]{5,4,3,2,1,0:T(8,128)S(1)}, u32[]{:S(2)}, u32[]{:S(2)}) collective-permute-start(f32[2,4,2,3,8,512]{5,4,3,2,1,0:T(8,128)S(1)} %get-tuple-element.21), channel_id=1, source_target_pairs={{0,96},{1,7},{2,98},{3,1},{4,100},{5,3},{6,102},{7,5},{8,104},{9,1... | collective-permute-start | bytes 2359304 | tf_op jit(solution)/shard_map/ppermute | solution.py:245
  38.3 9.0 %collective-permute-start.4 = (f32[4,2,3,8,512]{4,3,2,1,0:T(8,128)S(1)}, f32[4,2,3,8,512]{4,3,2,1,0:T(8,128)S(1)}, u32[]{:S(2)}, u32[]{:S(2)}) collective-permute-start(f32[4,2,3,8,512]{4,3,2,1,0:T(8,128)S(1)} %get-tuple-element.20), channel_id=1, source_target_pairs={{0,8},{1,25},{8,16},{9,1},{16,24},{17,9},{24,0},{25,17},{2,10},{3,... | collective-permute-start | bytes 1179656 | tf_op jit(solution)/shard_map/ppermute | solution.py:246
  41.1 19.3 %collective-permute-start.7 = (f32[2,4,2,3,8,512]{5,4,3,2,1,0:T(8,128)S(1)}, f32[2,4,2,3,8,512]{5,4,3,2,1,0:T(8,128)S(1)}, u32[]{:S(2)}, u32[]{:S(2)}) collective-permute-start(f32[2,4,2,3,8,512]{5,4,3,2,1,0:T(8,128)S(1)} %get-tuple-element.23), channel_id=1, source_target_pairs={{0,64},{1,5},{2,66},{3,7},{4,68},{5,1},{6,70},{7,3},{8,72},{9,13},... | collective-permute-start | bytes 2359304 | tf_op jit(solution)/shard_map/ppermute | solution.py:245
  42.4 15.9 %collective-permute-start.6 = (f32[4,2,3,8,512]{4,3,2,1,0:T(8,128)S(1)}, f32[4,2,3,8,512]{4,3,2,1,0:T(8,128)S(1)}, u32[]{:S(2)}, u32[]{:S(2)}) collective-permute-start(f32[4,2,3,8,512]{4,3,2,1,0:T(8,128)S(1)} %get-tuple-element.22), channel_id=1, source_target_pairs={{0,24},{1,9},{8,0},{9,17},{16,8},{17,25},{24,16},{25,1},{2,26},{3,... | collective-permute-start | bytes 1179656 | tf_op jit(solution)/shard_map/ppermute | solution.py:246
  47.3 13.1 %collective-permute-start.8 = (f32[4,2,3,8,512]{4,3,2,1,0:T(8,128)S(1)}, f32[4,2,3,8,512]{4,3,2,1,0:T(8,128)S(1)}, u32[]{:S(2)}, u32[]{:S(2)}) collective-permute-start(f32[4,2,3,8,512]{4,3,2,1,0:T(8,128)S(1)} %get-tuple-element.24), channel_id=1, source_target_pairs={{0,16},{1,17},{8,24},{9,25},{16,0},{17,1},{24,8},{25,9},{2,18},{3,... | collective-permute-start | bytes 1179656 | tf_op jit(solution)/shard_map/ppermute | solution.py:246
  58.9 35.0 %copy-start.1 = (f32[384,128]{1,0:T(8,128)S(1)}, f32[384,128]{1,0:T(8,128)}, u32[]{:S(2)}) copy-start(f32[384,128]{1,0:T(8,128)} %weights_ref.1) | copy-start | bytes 589828
  58.9 35.0 %copy-start.2 = (f32[384,128]{1,0:T(8,128)S(1)}, f32[384,128]{1,0:T(8,128)}, u32[]{:S(2)}) copy-start(f32[384,128]{1,0:T(8,128)} %first_ref.1) | copy-start | bytes 589828
  59.0 35.0 %copy-start.3 = (f32[384,128]{1,0:T(8,128)S(1)}, f32[384,128]{1,0:T(8,128)}, u32[]{:S(2)}) copy-start(f32[384,128]{1,0:T(8,128)} %second_ref.1) | copy-start | bytes 589828
  59.0 35.0 %copy-start.4 = (bf16[128,128]{1,0:T(8,128)(2,1)S(1)}, bf16[128,128]{1,0:T(8,128)(2,1)}, u32[]{:S(2)}) copy-start(bf16[128,128]{1,0:T(8,128)(2,1)} %constant.31.clone.table_ref) | copy-start | bytes 98308
  62.2 31.7 %all-to-all-start.1 = ((f32[64,48,128]{2,1,0:T(8,128)}), f32[64,48,128]{2,1,0:T(8,128)S(1)}, u32[]{:S(2)}, u32[]{:S(2)}) async-start(f32[64,48,128]{2,1,0:T(8,128)} %bitcast.10), calls=%async_computation.1 | async-start | bytes 3145728 | tf_op jit(solution)/shard_map/all_to_all | solution.py:251

commit v6 on v5

--- a/solution.py
+++ b/solution.py
@@ -156,28 +156,46 @@
     )(own.reshape(16, 12, 32, 512), *[raw.reshape(16, 4, 32, 512) for raw in raws], table, tops)
 
 
+def add_plane(z, sums_ref, parts, out_ref):
+    for t, part in enumerate(parts):
+        for pair in range(2):
+            v = unpack_eight([part[z, pair, i] for i in range(3)])
+            for k in range(2):
+                low, lower, high, higher = v[4 * k : 4 * k + 4]
+                for j, word in enumerate((low + FIELD * high, lower + FIELD * higher)):
+                    for x in range(4):
+                        where = (z, 2 * pair + k, x, pl.ds(16 * t + 8 * j, 8))
+                        out_ref[where] = sums_ref[where] + word[:, 128 * x : 128 * x + 128]
+
+
 def add_kernel(sums_ref, flat_ref, tall_ref, out_ref):
+    parts = (flat_ref.at[0], flat_ref.at[1], tall_ref)
+
     def plane(z, carry):
-        for t, part in enumerate((flat_ref.at[0], flat_ref.at[1], tall_ref)):
-            for pair in range(2):
-                v = unpack_eight([part[z, pair, i] for i in range(3)])
-                for k in range(2):
-                    low, lower, high, higher = v[4 * k : 4 * k + 4]
-                    for j, word in enumerate((low + FIELD * high, lower + FIELD * higher)):
-                        for x in range(4):
-                            where = (z, 2 * pair + k, x, pl.ds(16 * t + 8 * j, 8))
-                            out_ref[where] = sums_ref[where] + word[:, 128 * x : 128 * x + 128]
+        add_plane(z, sums_ref, parts, out_ref)
         return carry
 
     lax.fori_loop(0, 4, plane, 0)
 
 
-def add_parts(sums, parts):
-    return pl.pallas_call(
-        add_kernel,
+def last_add_kernel(sums_ref, flat_ref, tall_ref, out_ref, buffer, sems):
+    parts = (flat_ref.at[0], flat_ref.at[1], tall_ref)
+    copies = [pltpu.make_async_copy(buffer.at[z], out_ref.at[z], sems.at[z]) for z in range(4)]
+    for z in range(4):
+        add_plane(z, sums_ref, parts, buffer)
+        copies[z].start()
+    for copy in copies:
+        copy.wait()
+
+
+def add_parts(sums, parts, last):
+    shape = (4, 4, 4, 48, 128)
+    return pl.pallas_call(
+        last_add_kernel if last else add_kernel,
         in_specs=[VMEM] * 3,
-        out_specs=VMEM,
-        out_shape=pltpu.VMEM((4, 4, 4, 48, 128), F32),
+        out_specs=pl.BlockSpec(memory_space=pl.ANY) if last else VMEM,
+        out_shape=jax.ShapeDtypeStruct(shape, F32) if last else pltpu.VMEM(shape, F32),
+        scratch_shapes=[pltpu.VMEM(shape, F32), pltpu.SemaphoreType.DMA((4,))] if last else [],
         compiler_params=pltpu.CompilerParams(vmem_limit_bytes=12 * 2**20),
         cost_estimate=pl.CostEstimate(flops=10**7, bytes_accessed=4 * 10**6, transcendentals=0),
     )(sums, *parts)
@@ -188,33 +206,31 @@
 ):
     table = table_ref[...]
     even = lax.axis_index("core") == 0
+    coarse, fine = [], []
     for t in range(3):
         for q in range(4):
-            parts = []
+            low = high = jnp.zeros((16, 128), F32)
             for a in range(4):
                 for b in range(4):
                     z, y, x = (a, jnp.where(even, b, q), jnp.where(even, q, b)) if t < 2 else (q, a, b)
-                    parts.append(words_ref[z, y, x, 16 * t : 16 * t + 16, :])
-            low = high = jnp.zeros((16, 128), F32)
-            for word in parts:
-                upper = jnp.floor(word * (1.0 / FIELD) + 0.5)
-                high = high + upper
-                low = low + (word - upper * FIELD)
+                    word = words_ref[z, y, x, 16 * t : 16 * t + 16, :]
+                    upper = nearest(word, FIELD)
+                    high = high + upper
+                    low = low + (word - upper * FIELD)
             total = jnp.concatenate([low, high], axis=0)
-            coarse = jnp.floor(total * (1.0 / 128.0) + 0.5)
-            fine = total - coarse * 128.0
-            back = 128.0 * jnp.dot(coarse.astype(BF16), table, preferred_element_type=F32) + jnp.dot(
-                fine.astype(BF16), table, preferred_element_type=F32
-            )
-            rows = pl.ds(128 * t + 32 * q, 32)
-            grad = (back * scalars[0]) * ROOT * sign_ref[pl.ds(32 * (q % 2), 32), :].astype(F32)
-            first = 0.9 * first_ref[rows, :] + 0.1 * grad
-            second = 0.95 * second_ref[rows, :] + 0.05 * grad * grad
-            weights = weights_ref[rows, :]
-            update = (first / scalars[1]) / (jnp.sqrt(second / scalars[2]) + 1e-08) + 0.1 * weights
-            weights_out[rows, :] = weights - 0.2 * update
-            first_out[rows, :] = first
-            second_out[rows, :] = second
+            coarse.append(nearest(total, 128.0))
+            fine.append(total - coarse[-1] * 128.0)
+    digits = jnp.concatenate(coarse + fine, axis=0).astype(BF16)
+    turned = jnp.dot(digits, table, preferred_element_type=F32)
+    signs = jnp.concatenate([sign_ref[...].astype(F32)] * 6, axis=0)
+    grad = ((128.0 * turned[:384] + turned[384:]) * scalars[0]) * ROOT * signs
+    first = 0.9 * first_ref[...] + 0.1 * grad
+    second = 0.95 * second_ref[...] + 0.05 * grad * grad
+    weights = weights_ref[...]
+    update = (first / scalars[1]) / (jnp.sqrt(second / scalars[2]) + 1e-08) + 0.1 * weights
+    weights_out[...] = weights - 0.2 * update
+    first_out[...] = first
+    second_out[...] = second
 
 
 def shift_flat(amount):
@@ -245,8 +261,8 @@
         flat = lax.ppermute(flat, MESH, shift_flat(offset))
         arrived.append((flat, lax.ppermute(tall, ("z", "core"), shift_tall(offset))))
     (words,) = levels_for(0, own, raws, twice, tops)
-    for parts in arrived:
-        words = add_parts(words, parts)
+    for number, parts in enumerate(arrived):
+        words = add_parts(words, parts, number == 2)
     words = words.reshape(64, 48, 128)
     words = lax.all_to_all(words, CHIPS, 0, 0, tiled=True)
 

time: 96.3 us -> 95.9 us (level)
  no operation moved by 1% of the time
where the time goes in v6:
time: 95.9 us; the launch traced here: 95.5 us
  waiting for transfers between devices  29.9 us (31%)
  Pallas kernels  21.7 us (23%)
  blocking collectives  20.4 us (21%)
  starting transfers between devices  19.1 us (20%)
  between operations  2.83 us (3%)
    all_to_all x1, blocking collectives, shards(): tops = lax.all_to_all(top_tile, ALL, 0, 0, tiled=True)  20.4 us
    all_to_all x1, waiting for transfers between devices, shards(): words = lax.all_to_all(words, CHIPS, 0, 0, tiled=True)  19.8 us
    ppermute x3, waiting for transfers between devices, shards(): lax.ppermute(tall, ('z', 'core'), shift_tall(offset))  10.1 us
    pallas_call x1, Pallas kernels, rotate_all(): pl.pallas_call(rotate_kernel, in_specs=[pl.BlockSpec(memory_space=pl.ANY)...  9.05 us
    all_to_all x1, starting transfers between devices, shards(): words = lax.all_to_all(words, CHIPS, 0, 0, tiled=True)  8.32 us
    pallas_call x4, Pallas kernels, levels_for(): pl.pallas_call(functools.partial(level_kernel, offset), in_specs=[VMEM] *...  7.93 us
    ppermute x3, starting transfers between devices, shards(): lax.ppermute(tall, ('z', 'core'), shift_tall(offset))  5.49 us
    ppermute x3, starting transfers between devices, shards(): flat = lax.ppermute(flat, MESH, shift_flat(offset))  4.61 us
  transfers between devices with their start and end apart: 10, of which 4 were waited for; matrix products, arithmetic and copies ran while one was open for 2% of the time, Pallas kernels for 8%

profile of v6, /device:TPU:0, one launch (start us, length us, event | category | flops | bytes accessed | tf_op | source)
XLA Modules:
  0.0 95.5 jit_solution(718479273033107690)
XLA Ops:
  0.6 0.0 copy-start
  0.6 9.1 %shard_map.112 = (f32[16,128,512]{2,1,0:T(8,128)S(1)}, f32[16,128,512]{2,1,0:T(8,128)S(1)}, f32[16,128,512]{2,1,0:T(8,128)S(1)}, bf16[16,384,512]{2,1,0:T(8,128)(2,1)S(1)}, f32[128,128]{1,0:T(8,128)}) custom-call(bf16[16,2,384,512]{3,2,1,0:T(8,128)(2,1)} %bitcast.35, s32[64,512]{1,0:T(8,128)} %sign_ref.1, bf16[256,256]{1,0:T(8,128)(2,1)} %constant.32.clone.table_ref), custom_call_target="tpu_custom_call" | custom-call | flops 6000000000 | bytes 12000000 | tf_op jit(solution)/shard_map/pallas_call | solution.py:67
  9.7 0.1 collective-permute-start
  9.8 0.5 collective-permute-start.1
  10.3 0.1 collective-permute-start.2
  10.4 20.4 %all_to_all.16 = f32[128,1,128]{2,1,0:T(1,128)S(1)} all-to-all(f32[128,1,128]{2,1,0:T(1,128)} %bitcast.34), channel_id=1, replica_groups=mesh['x'=4,'z'=4,'y'=4,'core'=2] {'z','y','x','core'}, dimensions={0} | all-to-all | bytes 131072 | tf_op jit(solution)/shard_map/all_to_all | solution.py:256
  30.8 0.0 collective-permute-done
  30.8 0.0 collective-permute-done.1
  30.8 0.0 collective-permute-done.2
  30.8 0.0 copy-done
  30.8 2.0 %shard_map.114 = (f32[2,4,2,3,8,512]{5,4,3,2,1,0:T(8,128)S(1)}, f32[4,2,3,8,512]{4,3,2,1,0:T(8,128)S(1)}) custom-call(bf16[16,12,32,512]{3,2,1,0:T(8,128)(2,1)S(1)} %bitcast.13, f32[16,4,32,512]{3,2,1,0:T(8,128)S(1)} %bitcast.17, f32[16,4,32,512]{3,2,1,0:T(8,128)S(1)} %bitcast.21, f32[16,4,32,512]{3,2,1,0:T(8,128)S(1)} %bitcast.25, ...), custom_call_target="tpu_custom_call" | custom-call | flops 1000000 | bytes 10000 | tf_op jit(solution)/shard_map/pallas_call | solution.py:149
  32.9 0.7 collective-permute-start.3
  33.5 2.0 %shard_map.116 = (f32[2,4,2,3,8,512]{5,4,3,2,1,0:T(8,128)S(1)}, f32[4,2,3,8,512]{4,3,2,1,0:T(8,128)S(1)}) custom-call(bf16[16,12,32,512]{3,2,1,0:T(8,128)(2,1)S(1)} %bitcast.14, f32[16,4,32,512]{3,2,1,0:T(8,128)S(1)} %bitcast.18, f32[16,4,32,512]{3,2,1,0:T(8,128)S(1)} %bitcast.22, f32[16,4,32,512]{3,2,1,0:T(8,128)S(1)} %bitcast.26, ...), custom_call_target="tpu_custom_call" | custom-call | flops 1000000 | bytes 10000 | tf_op jit(solution)/shard_map/pallas_call | solution.py:149
  35.6 2.7 %collective-permute-start.5 = (f32[2,4,2,3,8,512]{5,4,3,2,1,0:T(8,128)S(1)}, f32[2,4,2,3,8,512]{5,4,3,2,1,0:T(8,128)S(1)}, u32[]{:S(2)}, u32[]{:S(2)}) collective-permute-start(f32[2,4,2,3,8,512]{5,4,3,2,1,0:T(8,128)S(1)} %get-tuple-element.21), channel_id=1, source_target_pairs={{0,96},{1,7},{2,98},{3,1},{4,100},{5,3},{6,102},{7,5},{8,104},{9,1... | collective-permute-start | bytes 2359304 | tf_op jit(solution)/shard_map/ppermute | solution.py:261
  38.3 0.8 collective-permute-start.4
  39.1 2.0 %shard_map.118 = (f32[2,4,2,3,8,512]{5,4,3,2,1,0:T(8,128)S(1)}, f32[4,2,3,8,512]{4,3,2,1,0:T(8,128)S(1)}) custom-call(bf16[16,12,32,512]{3,2,1,0:T(8,128)(2,1)S(1)} %bitcast.15, f32[16,4,32,512]{3,2,1,0:T(8,128)S(1)} %bitcast.19, f32[16,4,32,512]{3,2,1,0:T(8,128)S(1)} %bitcast.23, f32[16,4,32,512]{3,2,1,0:T(8,128)S(1)} %bitcast.27, ...), custom_call_target="tpu_custom_call" | custom-call | flops 1000000 | bytes 10000 | tf_op jit(solution)/shard_map/pallas_call | solution.py:149
  41.1 1.2 %collective-permute-start.7 = (f32[2,4,2,3,8,512]{5,4,3,2,1,0:T(8,128)S(1)}, f32[2,4,2,3,8,512]{5,4,3,2,1,0:T(8,128)S(1)}, u32[]{:S(2)}, u32[]{:S(2)}) collective-permute-start(f32[2,4,2,3,8,512]{5,4,3,2,1,0:T(8,128)S(1)} %get-tuple-element.23), channel_id=1, source_target_pairs={{0,64},{1,5},{2,66},{3,7},{4,68},{5,1},{6,70},{7,3},{8,72},{9,13},... | collective-permute-start | bytes 2359304 | tf_op jit(solution)/shard_map/ppermute | solution.py:261
  42.4 2.1 %collective-permute-start.6 = (f32[4,2,3,8,512]{4,3,2,1,0:T(8,128)S(1)}, f32[4,2,3,8,512]{4,3,2,1,0:T(8,128)S(1)}, u32[]{:S(2)}, u32[]{:S(2)}) collective-permute-start(f32[4,2,3,8,512]{4,3,2,1,0:T(8,128)S(1)} %get-tuple-element.22), channel_id=1, source_target_pairs={{0,24},{1,9},{8,0},{9,17},{16,8},{17,25},{24,16},{25,1},{2,26},{3,... | collective-permute-start | bytes 1179656 | tf_op jit(solution)/shard_map/ppermute | solution.py:262
  44.5 2.8 %collective-permute-done.4.tall_ref = f32[4,2,3,8,512]{4,3,2,1,0:T(8,128)S(1)} collective-permute-done((f32[4,2,3,8,512]{4,3,2,1,0:T(8,128)S(1)}, f32[4,2,3,8,512]{4,3,2,1,0:T(8,128)S(1)}, u32[]{:S(2)}, u32[]{:S(2)}) %collective-permute-start.4) | collective-permute-done | bytes 393248 | tf_op jit(solution)/shard_map/ppermute | solution.py:262
  47.3 2.6 %collective-permute-start.8 = (f32[4,2,3,8,512]{4,3,2,1,0:T(8,128)S(1)}, f32[4,2,3,8,512]{4,3,2,1,0:T(8,128)S(1)}, u32[]{:S(2)}, u32[]{:S(2)}) collective-permute-start(f32[4,2,3,8,512]{4,3,2,1,0:T(8,128)S(1)} %get-tuple-element.24), channel_id=1, source_target_pairs={{0,16},{1,17},{8,24},{9,25},{16,0},{17,1},{24,8},{25,9},{2,18},{3,... | collective-permute-start | bytes 1179656 | tf_op jit(solution)/shard_map/ppermute | solution.py:262
  49.8 1.8 %shard_map.113.sums_ref = f32[4,4,4,48,128]{4,3,2,1,0:T(8,128)S(1)} custom-call(bf16[16,12,32,512]{3,2,1,0:T(8,128)(2,1)S(1)} %bitcast.16, f32[16,4,32,512]{3,2,1,0:T(8,128)S(1)} %bitcast.20, f32[16,4,32,512]{3,2,1,0:T(8,128)S(1)} %bitcast.24, f32[16,4,32,512]{3,2,1,0:T(8,128)S(1)} %bitcast.28, bf16[256,256]{1,0:T(8,128)(2,1)S(1)} %copy-done, ...), custom_call_target="tpu_custom_call" | custom-call | flops 1000000 | bytes 10000 | tf_op jit(solution)/shard_map/pallas_call | solution.py:149
  51.7 0.0 collective-permute-done.3.flat_ref
  51.7 0.7 shard_map.115.sums_ref
  52.3 5.9 %collective-permute-done.6.tall_ref = f32[4,2,3,8,512]{4,3,2,1,0:T(8,128)S(1)} collective-permute-done((f32[4,2,3,8,512]{4,3,2,1,0:T(8,128)S(1)}, f32[4,2,3,8,512]{4,3,2,1,0:T(8,128)S(1)}, u32[]{:S(2)}, u32[]{:S(2)}) %collective-permute-start.6) | collective-permute-done | bytes 393248 | tf_op jit(solution)/shard_map/ppermute | solution.py:262
  58.3 0.0 collective-permute-done.5.flat_ref
  58.3 0.7 shard_map.117.sums_ref
  58.9 0.0 copy-start.1
  58.9 0.0 copy-start.2
  59.0 0.0 copy-start.3
  59.0 0.0 copy-start.4
  59.0 1.4 %collective-permute-done.8.tall_ref = f32[4,2,3,8,512]{4,3,2,1,0:T(8,128)S(1)} collective-permute-done((f32[4,2,3,8,512]{4,3,2,1,0:T(8,128)S(1)}, f32[4,2,3,8,512]{4,3,2,1,0:T(8,128)S(1)}, u32[]{:S(2)}, u32[]{:S(2)}) %collective-permute-start.8) | collective-permute-done | bytes 393248 | tf_op jit(solution)/shard_map/ppermute | solution.py:262
  60.4 0.0 collective-permute-done.7.flat_ref
  60.4 1.4 %shard_map.119 = f32[4,4,4,48,128]{4,3,2,1,0:T(8,128)} custom-call(f32[4,4,4,48,128]{4,3,2,1,0:T(8,128)S(1)} %shard_map.117.sums_ref, f32[2,4,2,3,8,512]{5,4,3,2,1,0:T(8,128)S(1)} %collective-permute-done.7.flat_ref, f32[4,2,3,8,512]{4,3,2,1,0:T(8,128)S(1)} %collective-permute-done.8.tall_ref), custom_call_target="tpu_custom_call" | custom-call | flops 10000000 | bytes 4000000 | tf_op jit(solution)/shard_map/pallas_call | solution.py:193
  61.8 8.3 %all-to-all-start.1 = ((f32[64,48,128]{2,1,0:T(8,128)}), f32[64,48,128]{2,1,0:T(8,128)S(1)}, u32[]{:S(2)}, u32[]{:S(2)}) async-start(f32[64,48,128]{2,1,0:T(8,128)} %bitcast.10), calls=%async_computation.1 | async-start | bytes 3145728 | tf_op jit(solution)/shard_map/all_to_all | solution.py:267
  71.5 0.8 constant_dynamic-slice_fusion.sign_ref
  72.3 0.7 reduce_max.9
  73.7 0.1 pad_maximum_fusion.scalars
  73.8 19.8 %all-to-all-done.1 = f32[64,48,128]{2,1,0:T(8,128)S(1)} async-done(((f32[64,48,128]{2,1,0:T(8,128)}), f32[64,48,128]{2,1,0:T(8,128)S(1)}, u32[]{:S(2)}, u32[]{:S(2)}) %all-to-all-start.1) | async-done | bytes 1572896 | tf_op jit(solution)/shard_map/all_to_all | solution.py:267
  93.6 0.0 copy-done.1
  93.6 0.0 copy-done.2
  93.6 0.0 copy-done.3
  93.6 0.0 copy-done.4
  93.6 1.9 %shard_map.120 = (f32[384,128]{1,0:T(8,128)}, f32[384,128]{1,0:T(8,128)}, f32[384,128]{1,0:T(8,128)}) custom-call(f32[3]{0:T(128)S(1)} %pad_maximum_fusion.scalars, f32[4,4,4,48,128]{4,3,2,1,0:T(8,128)S(1)} %bitcast.29, bf16[128,128]{1,0:T(8,128)(2,1)S(1)} %copy-done.4, s32[64,128]{1,0:T(8,128)S(1)} %constant_dynamic-slice_fusion.sign_ref, ...), custom_call_target="tpu_custom_call" | custom-call | tf_op jit(solution)/shard_map/pallas_call | solution.py:280
Async XLA Ops:
  0.6 30.2 %copy-start = (bf16[256,256]{1,0:T(8,128)(2,1)S(1)}, bf16[256,256]{1,0:T(8,128)(2,1)}, u32[]{:S(2)}) copy-start(bf16[256,256]{1,0:T(8,128)(2,1)} %constant.32.clone.table_ref) | copy-start | bytes 393220
  9.7 21.1 %collective-permute-start = (f32[16,128,512]{2,1,0:T(8,128)S(1)}, f32[16,128,512]{2,1,0:T(8,128)S(1)}, u32[]{:S(2)}, u32[]{:S(2)}) collective-permute-start(f32[16,128,512]{2,1,0:T(8,128)S(1)} %get-tuple-element.16), channel_id=1, source_target_pairs={{0,1},{1,0},{2,3},{3,2},{4,5},{5,4},{6,7},{7,6},{8,9},{9,8},{10,11... | collective-permute-start | bytes 12582920 | tf_op jit(solution)/shard_map/ppermute | solution.py:255
  9.8 21.0 %collective-permute-start.1 = (f32[16,128,512]{2,1,0:T(8,128)S(1)}, f32[16,128,512]{2,1,0:T(8,128)S(1)}, u32[]{:S(2)}, u32[]{:S(2)}) collective-permute-start(f32[16,128,512]{2,1,0:T(8,128)S(1)} %get-tuple-element.17), channel_id=1, source_target_pairs={{0,1},{1,0},{2,3},{3,2},{4,5},{5,4},{6,7},{7,6},{8,9},{9,8},{10,11... | collective-permute-start | bytes 12582920 | tf_op jit(solution)/shard_map/ppermute | solution.py:255
  10.3 20.5 %collective-permute-start.2 = (f32[16,128,512]{2,1,0:T(8,128)S(1)}, f32[16,128,512]{2,1,0:T(8,128)S(1)}, u32[]{:S(2)}, u32[]{:S(2)}) collective-permute-start(f32[16,128,512]{2,1,0:T(8,128)S(1)} %get-tuple-element.18), channel_id=1, source_target_pairs={{0,1},{1,0},{2,3},{3,2},{4,5},{5,4},{6,7},{7,6},{8,9},{9,8},{10,11... | collective-permute-start | bytes 12582920 | tf_op jit(solution)/shard_map/ppermute | solution.py:255
  32.9 18.8 %collective-permute-start.3 = (f32[2,4,2,3,8,512]{5,4,3,2,1,0:T(8,128)S(1)}, f32[2,4,2,3,8,512]{5,4,3,2,1,0:T(8,128)S(1)}, u32[]{:S(2)}, u32[]{:S(2)}) collective-permute-start(f32[2,4,2,3,8,512]{5,4,3,2,1,0:T(8,128)S(1)} %get-tuple-element.19), channel_id=1, source_target_pairs={{0,32},{1,3},{2,34},{3,5},{4,36},{5,7},{6,38},{7,1},{8,40},{9,11},... | collective-permute-start | bytes 2359304 | tf_op jit(solution)/shard_map/ppermute | solution.py:261
  35.6 22.7 %collective-permute-start.5 = (f32[2,4,2,3,8,512]{5,4,3,2,1,0:T(8,128)S(1)}, f32[2,4,2,3,8,512]{5,4,3,2,1,0:T(8,128)S(1)}, u32[]{:S(2)}, u32[]{:S(2)}) collective-permute-start(f32[2,4,2,3,8,512]{5,4,3,2,1,0:T(8,128)S(1)} %get-tuple-element.21), channel_id=1, source_target_pairs={{0,96},{1,7},{2,98},{3,1},{4,100},{5,3},{6,102},{7,5},{8,104},{9,1... | collective-permute-start | bytes 2359304 | tf_op jit(solution)/shard_map/ppermute | solution.py:261
  38.3 9.0 %collective-permute-start.4 = (f32[4,2,3,8,512]{4,3,2,1,0:T(8,128)S(1)}, f32[4,2,3,8,512]{4,3,2,1,0:T(8,128)S(1)}, u32[]{:S(2)}, u32[]{:S(2)}) collective-permute-start(f32[4,2,3,8,512]{4,3,2,1,0:T(8,128)S(1)} %get-tuple-element.20), channel_id=1, source_target_pairs={{0,8},{1,25},{8,16},{9,1},{16,24},{17,9},{24,0},{25,17},{2,10},{3,... | collective-permute-start | bytes 1179656 | tf_op jit(solution)/shard_map/ppermute | solution.py:262
  41.1 19.3 %collective-permute-start.7 = (f32[2,4,2,3,8,512]{5,4,3,2,1,0:T(8,128)S(1)}, f32[2,4,2,3,8,512]{5,4,3,2,1,0:T(8,128)S(1)}, u32[]{:S(2)}, u32[]{:S(2)}) collective-permute-start(f32[2,4,2,3,8,512]{5,4,3,2,1,0:T(8,128)S(1)} %get-tuple-element.23), channel_id=1, source_target_pairs={{0,64},{1,5},{2,66},{3,7},{4,68},{5,1},{6,70},{7,3},{8,72},{9,13},... | collective-permute-start | bytes 2359304 | tf_op jit(solution)/shard_map/ppermute | solution.py:261
  42.4 15.9 %collective-permute-start.6 = (f32[4,2,3,8,512]{4,3,2,1,0:T(8,128)S(1)}, f32[4,2,3,8,512]{4,3,2,1,0:T(8,128)S(1)}, u32[]{:S(2)}, u32[]{:S(2)}) collective-permute-start(f32[4,2,3,8,512]{4,3,2,1,0:T(8,128)S(1)} %get-tuple-element.22), channel_id=1, source_target_pairs={{0,24},{1,9},{8,0},{9,17},{16,8},{17,25},{24,16},{25,1},{2,26},{3,... | collective-permute-start | bytes 1179656 | tf_op jit(solution)/shard_map/ppermute | solution.py:262
  47.3 13.1 %collective-permute-start.8 = (f32[4,2,3,8,512]{4,3,2,1,0:T(8,128)S(1)}, f32[4,2,3,8,512]{4,3,2,1,0:T(8,128)S(1)}, u32[]{:S(2)}, u32[]{:S(2)}) collective-permute-start(f32[4,2,3,8,512]{4,3,2,1,0:T(8,128)S(1)} %get-tuple-element.24), channel_id=1, source_target_pairs={{0,16},{1,17},{8,24},{9,25},{16,0},{17,1},{24,8},{25,9},{2,18},{3,... | collective-permute-start | bytes 1179656 | tf_op jit(solution)/shard_map/ppermute | solution.py:262
  58.9 34.7 %copy-start.1 = (f32[384,128]{1,0:T(8,128)S(1)}, f32[384,128]{1,0:T(8,128)}, u32[]{:S(2)}) copy-start(f32[384,128]{1,0:T(8,128)} %weights_ref.1) | copy-start | bytes 589828
  58.9 34.6 %copy-start.2 = (f32[384,128]{1,0:T(8,128)S(1)}, f32[384,128]{1,0:T(8,128)}, u32[]{:S(2)}) copy-start(f32[384,128]{1,0:T(8,128)} %first_ref.1) | copy-start | bytes 589828
  59.0 34.6 %copy-start.3 = (f32[384,128]{1,0:T(8,128)S(1)}, f32[384,128]{1,0:T(8,128)}, u32[]{:S(2)}) copy-start(f32[384,128]{1,0:T(8,128)} %second_ref.1) | copy-start | bytes 589828
  59.0 34.6 %copy-start.4 = (bf16[128,128]{1,0:T(8,128)(2,1)S(1)}, bf16[128,128]{1,0:T(8,128)(2,1)}, u32[]{:S(2)}) copy-start(bf16[128,128]{1,0:T(8,128)(2,1)} %constant.31.clone.table_ref) | copy-start | bytes 98308
  61.8 31.7 %all-to-all-start.1 = ((f32[64,48,128]{2,1,0:T(8,128)}), f32[64,48,128]{2,1,0:T(8,128)S(1)}, u32[]{:S(2)}, u32[]{:S(2)}) async-start(f32[64,48,128]{2,1,0:T(8,128)} %bitcast.10), calls=%async_computation.1 | async-start | bytes 3145728 | tf_op jit(solution)/shard_map/all_to_all | solution.py:267

commit v7 on v6

--- a/solution.py
+++ b/solution.py
@@ -29,9 +29,9 @@
     return table
 
 
-def rotate_kernel(grads_ref, sign_ref, table_ref, raw0, raw1, raw2, own_ref, top_ref, buffer, sems):
+def rotate_kernel(start, grads_ref, sign_ref, table_ref, raw_ref, own_ref, top_ref, buffer, sems):
     core = lax.axis_index("core")
-    copies = [pltpu.make_async_copy(grads_ref.at[i], buffer.at[i], sems.at[i]) for i in range(16)]
+    copies = [pltpu.make_async_copy(grads_ref.at[start + i], buffer.at[i], sems.at[i]) for i in range(8)]
     for copy in copies:
         copy.start()
     signs = sign_ref[...].astype(F32).astype(BF16)
@@ -41,10 +41,10 @@
         return jnp.max(jnp.abs(value).reshape(-1, 8, 256), axis=0)
 
     best = jnp.zeros((8, 256), F32)
-    for i in range(16):
+    for i in range(8):
         copies[i].wait()
 
-        for third, raw_ref in enumerate((raw0, raw1, raw2)):
+        for third in range(3):
             rows = pl.ds(128 * third, 128)
             wide = jnp.concatenate([signs, signs], axis=0)
             mine = buffer[i, core, rows, :] * wide
@@ -54,8 +54,8 @@
                 block = jnp.concatenate([v[:, :256], v[:, 256:]], axis=0)
                 turned = jnp.dot(block, table, preferred_element_type=F32)
                 if keep:
-                    raw_ref[i, :, :256] = turned[:128] * ROOT
-                    raw_ref[i, :, 256:] = turned[128:] * ROOT
+                    raw_ref[i, rows, :256] = turned[:128] * ROOT
+                    raw_ref[i, rows, 256:] = turned[128:] * ROOT
                 best = jnp.maximum(best, fold(turned))
     top_ref[...] = jnp.broadcast_to(jnp.max(best, axis=(0, 1), keepdims=True) * ROOT, (128, 128))
 
@@ -63,19 +63,19 @@
 VMEM = pl.BlockSpec(memory_space=pltpu.VMEM)
 
 
-def rotate_all(grads, signs, table):
+def rotate_half(start, grads, signs, table):
     return pl.pallas_call(
-        rotate_kernel,
+        functools.partial(rotate_kernel, start),
         in_specs=[pl.BlockSpec(memory_space=pl.ANY), VMEM, VMEM],
-        out_specs=[VMEM] * 5,
-        out_shape=[pltpu.VMEM((16, 128, 512), F32)] * 3
-        + [
-            pltpu.VMEM((16, 384, 512), BF16),
+        out_specs=[VMEM] * 3,
+        out_shape=[
+            pltpu.VMEM((8, 384, 512), F32),
+            pltpu.VMEM((8, 384, 512), BF16),
             jax.ShapeDtypeStruct((128, 128), F32),
         ],
-        scratch_shapes=[pltpu.VMEM((16, 2, 384, 512), BF16), pltpu.SemaphoreType.DMA((16,))],
-        compiler_params=pltpu.CompilerParams(vmem_limit_bytes=40 * 2**20),
-        cost_estimate=pl.CostEstimate(flops=6 * 10**9, bytes_accessed=12 * 10**6, transcendentals=0),
+        scratch_shapes=[pltpu.VMEM((8, 2, 384, 512), BF16), pltpu.SemaphoreType.DMA((8,))],
+        compiler_params=pltpu.CompilerParams(vmem_limit_bytes=(36 if start else 52) * 2**20),
+        cost_estimate=pl.CostEstimate(flops=3 * 10**9, bytes_accessed=13 * 10**6, transcendentals=0),
     )(grads.reshape(16, 2, 384, 512), signs, table)
 
 
@@ -102,17 +102,17 @@
     return values
 
 
-def level_kernel(offset, own_ref, raw0, raw1, raw2, table_ref, top_ref, *outs):
+def level_kernel(offset, own0, own1, raw0, raw1, table_ref, top_ref, *outs):
     table = table_ref[...]
     scale = 127.0 / jnp.max(top_ref[...], axis=(0, 1), keepdims=True)
     even = lax.axis_index("core") == 0
     flat = lax.rem(jnp.where(even, lax.axis_index("x"), lax.axis_index("y")) + offset, 4)
     ahead = jnp.where(even, offset, (4 - offset) % 4)
     quarters = [flat, flat, lax.rem(lax.axis_index("z") + ahead, 4)]
-    raws = (raw0, raw1, raw2)
-
-    def plane(z, carry):
-        blocks = [own_ref[4 * z + y, 4 * t + quarters[t]] for t in range(3) for y in range(4)]
+
+    def plane(own_ref, raw_ref, base, step, carry):
+        z = base + step
+        blocks = [own_ref[4 * step + y, 4 * t + quarters[t]] for t in range(3) for y in range(4)]
         stacked = jnp.concatenate([v[:, 256 * h : 256 * h + 256] for v in blocks for h in range(2)], axis=0)
         mine = jnp.dot(stacked, table, preferred_element_type=F32) * ROOT
         mine = jnp.floor(mine * scale + 0.5)
@@ -122,7 +122,7 @@
                     groups = []
                     for y in (2 * pair, 2 * pair + 1):
                         row = 32 * ((t * 4 + y) * 2 + h)
-                        other = raws[t][4 * z + y, quarters[t], :, 256 * h : 256 * h + 256]
+                        other = raw_ref[4 * step + y, 4 * t + quarters[t], :, 256 * h : 256 * h + 256]
                         total = mine[row : row + 32] + jnp.floor(other * scale + 0.5)
                         groups += [total[8 * g : 8 * g + 8] for g in range(4)]
                     if offset:
@@ -141,10 +141,11 @@
                             place[...] = word[:, 128 * x : 128 * x + 128]
         return carry
 
-    lax.fori_loop(0, 4, plane, 0)
-
-
-def levels_for(offset, own, raws, table, tops):
+    lax.fori_loop(0, 2, functools.partial(plane, own0, raw0, 0), 0)
+    lax.fori_loop(0, 2, functools.partial(plane, own1, raw1, 2), 0)
+
+
+def levels_for(offset, owns, raws, table, tops):
     shapes = [(2, 4, 2, 3, 8, 512), (4, 2, 3, 8, 512)] if offset else [(4, 4, 4, 48, 128)]
     return pl.pallas_call(
         functools.partial(level_kernel, offset),
@@ -153,7 +154,7 @@
         out_shape=[pltpu.VMEM(shape, F32) for shape in shapes],
         compiler_params=pltpu.CompilerParams(vmem_limit_bytes=12 * 2**20),
         cost_estimate=pl.CostEstimate(flops=10**6, bytes_accessed=10**4, transcendentals=0),
-    )(own.reshape(16, 12, 32, 512), *[raw.reshape(16, 4, 32, 512) for raw in raws], table, tops)
+    )(*[part.reshape(8, 12, 32, 512) for part in (*owns, *raws)], table, tops)
 
 
 def add_plane(z, sums_ref, parts, out_ref):
@@ -251,16 +252,20 @@
     grads = gradients[0, 0]
     table = jnp.asarray(hadamard(BLOCK), BF16)
     twice = jnp.asarray(np.kron(np.eye(2, dtype=np.float32), hadamard(BLOCK)), BF16)
-    *raws, own, top_tile = rotate_all(grads, sign_table, twice)
-    raws = [lax.ppermute(raw, "core", [(0, 1), (1, 0)]) for raw in raws]
-    tops = lax.all_to_all(top_tile, ALL, 0, 0, tiled=True)
+    raws, owns, tiles = [], [], []
+    for start in (0, 8):
+        raw, own, tile = rotate_half(start, grads, sign_table, twice)
+        raws.append(lax.ppermute(raw, "core", [(0, 1), (1, 0)]))
+        owns.append(own)
+        tiles.append(tile)
+    tops = lax.all_to_all(jnp.maximum(*tiles), ALL, 0, 0, tiled=True)
 
     arrived = []
     for offset in (1, 3, 2):
-        flat, tall = levels_for(offset, own, raws, twice, tops)
+        flat, tall = levels_for(offset, owns, raws, twice, tops)
         flat = lax.ppermute(flat, MESH, shift_flat(offset))
         arrived.append((flat, lax.ppermute(tall, ("z", "core"), shift_tall(offset))))
-    (words,) = levels_for(0, own, raws, twice, tops)
+    (words,) = levels_for(0, owns, raws, twice, tops)
     for number, parts in enumerate(arrived):
         words = add_parts(words, parts, number == 2)
     words = words.reshape(64, 48, 128)

time: 95.9 us -> 93.4 us (0.974)
  starting transfers between devices: 19.1 us -> 15.1 us
  waiting for transfers between devices: 29.9 us -> 31.2 us
  Pallas kernels: 21.7 us -> 22.9 us
    ppermute x3, waiting for transfers between devices: 10.1 us -> 13 us  [shards(): lax.ppermute(tall, ('z', 'core'), shift_tall(offset))]
    ppermute x3, starting transfers between devices: 5.49 us -> 3.31 us  [shards(): lax.ppermute(tall, ('z', 'core'), shift_tall(offset))]
    all_to_all x1, waiting for transfers between devices: 19.8 us -> 18.2 us  [shards(): words = lax.all_to_all(words, CHIPS, 0, 0, tiled=True)]
    pallas_call x1 -> x2, Pallas kernels: 9.05 us -> 10.3 us  [rotate_half(): pl.pallas_call(functools.partial(rotate_kernel, start), in_specs=[pl.Bloc...]
    ppermute x3, starting transfers between devices: 4.61 us -> 3.46 us  [shards(): flat = lax.ppermute(flat, MESH, shift_flat(offset))]
  transfers between devices with their start and end apart: 10 -> 9, of which waited for: 4 -> 4; matrix products, arithmetic and copies ran while one was open for 2% -> 1% of each run, Pallas kernels for 8% -> 12%
where the time goes in v7:
time: 93.4 us; the launch traced here: 93.1 us
  waiting for transfers between devices  31.2 us (33%)
  Pallas kernels  22.9 us (25%)
  blocking collectives  20.2 us (22%)
  starting transfers between devices  15.1 us (16%)
  between operations  2.88 us (3%)
    all_to_all x1, blocking collectives, shards(): tops = lax.all_to_all(jnp.maximum(*tiles), ALL, 0, 0, tiled=True)  20.2 us
    all_to_all x1, waiting for transfers between devices, shards(): words = lax.all_to_all(words, CHIPS, 0, 0, tiled=True)  18.2 us
    ppermute x3, waiting for transfers between devices, shards(): lax.ppermute(tall, ('z', 'core'), shift_tall(offset))  13 us
    pallas_call x2, Pallas kernels, rotate_half(): pl.pallas_call(functools.partial(rotate_kernel, start), in_specs=[pl.Bloc...  10.3 us
    pallas_call x4, Pallas kernels, levels_for(): pl.pallas_call(functools.partial(level_kernel, offset), in_specs=[VMEM] *...  7.87 us
    all_to_all x1, starting transfers between devices, shards(): words = lax.all_to_all(words, CHIPS, 0, 0, tiled=True)  7.65 us
    ppermute x3, starting transfers between devices, shards(): flat = lax.ppermute(flat, MESH, shift_flat(offset))  3.46 us
    ppermute x3, starting transfers between devices, shards(): lax.ppermute(tall, ('z', 'core'), shift_tall(offset))  3.31 us
  transfers between devices with their start and end apart: 9, of which 4 were waited for; matrix products, arithmetic and copies ran while one was open for 1% of the time, Pallas kernels for 12%

profile of v7, /device:TPU:0, one launch (start us, length us, event | category | flops | bytes accessed | tf_op | source)
XLA Modules:
  0.0 93.1 jit_solution(9645732011588841718)
XLA Ops:
  0.6 0.0 copy-start
  0.6 0.0 copy-start.1
  0.7 6.0 %shard_map.112 = (f32[8,384,512]{2,1,0:T(8,128)S(1)}, bf16[8,384,512]{2,1,0:T(8,128)(2,1)S(1)}, f32[128,128]{1,0:T(8,128)}) custom-call(bf16[16,2,384,512]{3,2,1,0:T(8,128)(2,1)} %bitcast.34, s32[64,512]{1,0:T(8,128)} %sign_ref.3, bf16[256,256]{1,0:T(8,128)(2,1)} %constant.32.clone.table_ref), custom_call_target="tpu_custom_call" | custom-call | flops 3000000000 | bytes 13000000 | tf_op jit(solution)/shard_map/pallas_call | solution.py:67
  6.6 0.0 copy-start.6
  6.7 0.1 collective-permute-start
  6.7 0.0 copy-done
  6.8 0.0 copy-done.1
  6.8 4.3 %shard_map.113 = (f32[8,384,512]{2,1,0:T(8,128)S(1)}, bf16[8,384,512]{2,1,0:T(8,128)(2,1)S(1)}, f32[128,128]{1,0:T(8,128)S(1)}) custom-call(bf16[16,2,384,512]{3,2,1,0:T(8,128)(2,1)} %bitcast.35, s32[64,512]{1,0:T(8,128)S(1)} %copy-done.1, bf16[256,256]{1,0:T(8,128)(2,1)S(1)} %copy-done), custom_call_target="tpu_custom_call" | custom-call | flops 3000000000 | bytes 13000000 | tf_op jit(solution)/shard_map/pallas_call | solution.py:67
  11.1 0.6 collective-permute-start.1
  11.7 0.0 copy-done.6
  11.7 20.2 %all_to_all.16 = f32[128,1,128]{2,1,0:T(1,128)S(1)} all-to-all(f32[128,1,128]{2,1,0:T(1,128)S(1)} %bitcast.36), channel_id=1, replica_groups=mesh['x'=4,'z'=4,'y'=4,'core'=2] {'z','y','x','core'}, dimensions={0} | all-to-all | bytes 131072 | tf_op jit(solution)/shard_map/all_to_all | solution.py:261
  31.9 0.0 collective-permute-done
  31.9 0.0 collective-permute-done.1
  31.9 2.0 %shard_map.115 = (f32[2,4,2,3,8,512]{5,4,3,2,1,0:T(8,128)S(1)}, f32[4,2,3,8,512]{4,3,2,1,0:T(8,128)S(1)}) custom-call(bf16[8,12,32,512]{3,2,1,0:T(8,128)(2,1)S(1)} %bitcast.21, bf16[8,12,32,512]{3,2,1,0:T(8,128)(2,1)S(1)} %bitcast.25, f32[8,12,32,512]{3,2,1,0:T(8,128)S(1)} %bitcast.13, f32[8,12,32,512]{3,2,1,0:T(8,128)S(1)} %bitcast.17, ...), custom_call_target="tpu_custom_call" | custom-call | flops 1000000 | bytes 10000 | tf_op jit(solution)/shard_map/pallas_call | solution.py:150
  34.0 0.6 collective-permute-start.2
  34.6 2.0 %shard_map.117 = (f32[2,4,2,3,8,512]{5,4,3,2,1,0:T(8,128)S(1)}, f32[4,2,3,8,512]{4,3,2,1,0:T(8,128)S(1)}) custom-call(bf16[8,12,32,512]{3,2,1,0:T(8,128)(2,1)S(1)} %bitcast.22, bf16[8,12,32,512]{3,2,1,0:T(8,128)(2,1)S(1)} %bitcast.26, f32[8,12,32,512]{3,2,1,0:T(8,128)S(1)} %bitcast.14, f32[8,12,32,512]{3,2,1,0:T(8,128)S(1)} %bitcast.18, ...), custom_call_target="tpu_custom_call" | custom-call | flops 1000000 | bytes 10000 | tf_op jit(solution)/shard_map/pallas_call | solution.py:150
  36.7 2.7 %collective-permute-start.4 = (f32[2,4,2,3,8,512]{5,4,3,2,1,0:T(8,128)S(1)}, f32[2,4,2,3,8,512]{5,4,3,2,1,0:T(8,128)S(1)}, u32[]{:S(2)}, u32[]{:S(2)}) collective-permute-start(f32[2,4,2,3,8,512]{5,4,3,2,1,0:T(8,128)S(1)} %get-tuple-element.23), channel_id=1, source_target_pairs={{0,96},{1,7},{2,98},{3,1},{4,100},{5,3},{6,102},{7,5},{8,104},{9,1... | collective-permute-start | bytes 2359304 | tf_op jit(solution)/shard_map/ppermute | solution.py:266
  39.4 0.8 collective-permute-start.3
  40.2 2.0 %shard_map.119 = (f32[2,4,2,3,8,512]{5,4,3,2,1,0:T(8,128)S(1)}, f32[4,2,3,8,512]{4,3,2,1,0:T(8,128)S(1)}) custom-call(bf16[8,12,32,512]{3,2,1,0:T(8,128)(2,1)S(1)} %bitcast.23, bf16[8,12,32,512]{3,2,1,0:T(8,128)(2,1)S(1)} %bitcast.27, f32[8,12,32,512]{3,2,1,0:T(8,128)S(1)} %bitcast.15, f32[8,12,32,512]{3,2,1,0:T(8,128)S(1)} %bitcast.19, ...), custom_call_target="tpu_custom_call" | custom-call | flops 1000000 | bytes 10000 | tf_op jit(solution)/shard_map/pallas_call | solution.py:150
  42.2 0.1 collective-permute-start.6
  42.3 2.5 %collective-permute-start.5 = (f32[4,2,3,8,512]{4,3,2,1,0:T(8,128)S(1)}, f32[4,2,3,8,512]{4,3,2,1,0:T(8,128)S(1)}, u32[]{:S(2)}, u32[]{:S(2)}) collective-permute-start(f32[4,2,3,8,512]{4,3,2,1,0:T(8,128)S(1)} %get-tuple-element.24), channel_id=1, source_target_pairs={{0,24},{1,9},{8,0},{9,17},{16,8},{17,25},{24,16},{25,1},{2,26},{3,... | collective-permute-start | bytes 1179656 | tf_op jit(solution)/shard_map/ppermute | solution.py:267
  44.8 6.9 %collective-permute-done.3.tall_ref = f32[4,2,3,8,512]{4,3,2,1,0:T(8,128)S(1)} collective-permute-done((f32[4,2,3,8,512]{4,3,2,1,0:T(8,128)S(1)}, f32[4,2,3,8,512]{4,3,2,1,0:T(8,128)S(1)}, u32[]{:S(2)}, u32[]{:S(2)}) %collective-permute-start.3) | collective-permute-done | bytes 393248 | tf_op jit(solution)/shard_map/ppermute | solution.py:267
  51.7 0.0 collective-permute-start.7
  51.7 1.8 %shard_map.114.sums_ref = f32[4,4,4,48,128]{4,3,2,1,0:T(8,128)S(1)} custom-call(bf16[8,12,32,512]{3,2,1,0:T(8,128)(2,1)S(1)} %bitcast.24, bf16[8,12,32,512]{3,2,1,0:T(8,128)(2,1)S(1)} %bitcast.28, f32[8,12,32,512]{3,2,1,0:T(8,128)S(1)} %bitcast.16, f32[8,12,32,512]{3,2,1,0:T(8,128)S(1)} %bitcast.20, bf16[256,256]{1,0:T(8,128)(2,1)S(1)} %copy-done, ...), custom_call_target="tpu_custom_call" | custom-call | flops 1000000 | bytes 10000 | tf_op jit(solution)/shard_map/pallas_call | solution.py:150
  53.5 0.0 collective-permute-done.2.flat_ref
  53.5 0.7 shard_map.116.sums_ref
  54.2 4.4 %collective-permute-done.5.tall_ref = f32[4,2,3,8,512]{4,3,2,1,0:T(8,128)S(1)} collective-permute-done((f32[4,2,3,8,512]{4,3,2,1,0:T(8,128)S(1)}, f32[4,2,3,8,512]{4,3,2,1,0:T(8,128)S(1)}, u32[]{:S(2)}, u32[]{:S(2)}) %collective-permute-start.5) | collective-permute-done | bytes 393248 | tf_op jit(solution)/shard_map/ppermute | solution.py:267
  58.6 0.0 collective-permute-done.4.flat_ref
  58.6 0.7 shard_map.118.sums_ref
  59.2 0.0 copy-start.2
  59.3 0.0 copy-start.3
  59.3 0.0 copy-start.4
  59.3 0.0 copy-start.5
  59.3 1.7 %collective-permute-done.7.tall_ref = f32[4,2,3,8,512]{4,3,2,1,0:T(8,128)S(1)} collective-permute-done((f32[4,2,3,8,512]{4,3,2,1,0:T(8,128)S(1)}, f32[4,2,3,8,512]{4,3,2,1,0:T(8,128)S(1)}, u32[]{:S(2)}, u32[]{:S(2)}) %collective-permute-start.7) | collective-permute-done | bytes 393248 | tf_op jit(solution)/shard_map/ppermute | solution.py:267
  61.0 0.0 collective-permute-done.6.flat_ref
  61.0 1.4 %shard_map.120 = f32[4,4,4,48,128]{4,3,2,1,0:T(8,128)} custom-call(f32[4,4,4,48,128]{4,3,2,1,0:T(8,128)S(1)} %shard_map.118.sums_ref, f32[2,4,2,3,8,512]{5,4,3,2,1,0:T(8,128)S(1)} %collective-permute-done.6.flat_ref, f32[4,2,3,8,512]{4,3,2,1,0:T(8,128)S(1)} %collective-permute-done.7.tall_ref), custom_call_target="tpu_custom_call" | custom-call | flops 10000000 | bytes 4000000 | tf_op jit(solution)/shard_map/pallas_call | solution.py:194
  62.5 7.6 %all-to-all-start.1 = ((f32[64,48,128]{2,1,0:T(8,128)}), f32[64,48,128]{2,1,0:T(8,128)S(1)}, u32[]{:S(2)}, u32[]{:S(2)}) async-start(f32[64,48,128]{2,1,0:T(8,128)} %bitcast.10), calls=%async_computation.1 | async-start | bytes 3145728 | tf_op jit(solution)/shard_map/all_to_all | solution.py:272
  71.5 0.7 reduce_max.9
  72.9 0.1 pad_maximum_fusion.scalars
  73.0 18.2 %all-to-all-done.1 = f32[64,48,128]{2,1,0:T(8,128)S(1)} async-done(((f32[64,48,128]{2,1,0:T(8,128)}), f32[64,48,128]{2,1,0:T(8,128)S(1)}, u32[]{:S(2)}, u32[]{:S(2)}) %all-to-all-start.1) | async-done | bytes 1572896 | tf_op jit(solution)/shard_map/all_to_all | solution.py:272
  91.2 0.0 copy-done.2
  91.2 0.0 copy-done.3
  91.2 0.0 copy-done.4
  91.2 0.0 copy-done.5
  91.2 1.9 %shard_map.121 = (f32[384,128]{1,0:T(8,128)}, f32[384,128]{1,0:T(8,128)}, f32[384,128]{1,0:T(8,128)}) custom-call(f32[3]{0:T(128)S(1)} %pad_maximum_fusion.scalars, f32[4,4,4,48,128]{4,3,2,1,0:T(8,128)S(1)} %bitcast.29, bf16[128,128]{1,0:T(8,128)(2,1)S(1)} %copy-done.5, s32[64,128]{1,0:T(8,128)S(1)} %constant_dynamic-slice_fusion.sign_ref, ...), custom_call_target="tpu_custom_call" | custom-call | tf_op jit(solution)/shard_map/pallas_call | solution.py:285
  (2 shorter events, 0.0 us)
Async XLA Ops:
  0.6 6.1 %copy-start = (bf16[256,256]{1,0:T(8,128)(2,1)S(1)}, bf16[256,256]{1,0:T(8,128)(2,1)}, u32[]{:S(2)}) copy-start(bf16[256,256]{1,0:T(8,128)(2,1)} %constant.32.clone.table_ref) | copy-start | bytes 393220
  0.6 6.1 %copy-start.1 = (s32[64,512]{1,0:T(8,128)S(1)}, s32[64,512]{1,0:T(8,128)}, u32[]{:S(2)}) copy-start(s32[64,512]{1,0:T(8,128)} %sign_ref.3) | copy-start | bytes 393220
  6.6 5.0 %copy-start.6 = (f32[128,128]{1,0:T(8,128)S(1)}, f32[128,128]{1,0:T(8,128)}, u32[]{:S(2)}) copy-start(f32[128,128]{1,0:T(8,128)} %get-tuple-element.15) | copy-start | bytes 196612
  6.7 25.3 %collective-permute-start = (f32[8,384,512]{2,1,0:T(8,128)S(1)}, f32[8,384,512]{2,1,0:T(8,128)S(1)}, u32[]{:S(2)}, u32[]{:S(2)}) collective-permute-start(f32[8,384,512]{2,1,0:T(8,128)S(1)} %get-tuple-element.19), channel_id=1, source_target_pairs={{0,1},{1,0},{2,3},{3,2},{4,5},{5,4},{6,7},{7,6},{8,9},{9,8},{10,11... | collective-permute-start | bytes 18874376 | tf_op jit(solution)/shard_map/ppermute | solution.py:258
  11.1 20.8 %collective-permute-start.1 = (f32[8,384,512]{2,1,0:T(8,128)S(1)}, f32[8,384,512]{2,1,0:T(8,128)S(1)}, u32[]{:S(2)}, u32[]{:S(2)}) collective-permute-start(f32[8,384,512]{2,1,0:T(8,128)S(1)} %get-tuple-element.20), channel_id=1, source_target_pairs={{0,1},{1,0},{2,3},{3,2},{4,5},{5,4},{6,7},{7,6},{8,9},{9,8},{10,11... | collective-permute-start | bytes 18874376 | tf_op jit(solution)/shard_map/ppermute | solution.py:258
  34.0 19.6 %collective-permute-start.2 = (f32[2,4,2,3,8,512]{5,4,3,2,1,0:T(8,128)S(1)}, f32[2,4,2,3,8,512]{5,4,3,2,1,0:T(8,128)S(1)}, u32[]{:S(2)}, u32[]{:S(2)}) collective-permute-start(f32[2,4,2,3,8,512]{5,4,3,2,1,0:T(8,128)S(1)} %get-tuple-element.21), channel_id=1, source_target_pairs={{0,32},{1,3},{2,34},{3,5},{4,36},{5,7},{6,38},{7,1},{8,40},{9,11},... | collective-permute-start | bytes 2359304 | tf_op jit(solution)/shard_map/ppermute | solution.py:266
  36.7 21.9 %collective-permute-start.4 = (f32[2,4,2,3,8,512]{5,4,3,2,1,0:T(8,128)S(1)}, f32[2,4,2,3,8,512]{5,4,3,2,1,0:T(8,128)S(1)}, u32[]{:S(2)}, u32[]{:S(2)}) collective-permute-start(f32[2,4,2,3,8,512]{5,4,3,2,1,0:T(8,128)S(1)} %get-tuple-element.23), channel_id=1, source_target_pairs={{0,96},{1,7},{2,98},{3,1},{4,100},{5,3},{6,102},{7,5},{8,104},{9,1... | collective-permute-start | bytes 2359304 | tf_op jit(solution)/shard_map/ppermute | solution.py:266
  39.4 12.3 %collective-permute-start.3 = (f32[4,2,3,8,512]{4,3,2,1,0:T(8,128)S(1)}, f32[4,2,3,8,512]{4,3,2,1,0:T(8,128)S(1)}, u32[]{:S(2)}, u32[]{:S(2)}) collective-permute-start(f32[4,2,3,8,512]{4,3,2,1,0:T(8,128)S(1)} %get-tuple-element.22), channel_id=1, source_target_pairs={{0,8},{1,25},{8,16},{9,1},{16,24},{17,9},{24,0},{25,17},{2,10},{3,... | collective-permute-start | bytes 1179656 | tf_op jit(solution)/shard_map/ppermute | solution.py:267
  42.2 18.8 %collective-permute-start.6 = (f32[2,4,2,3,8,512]{5,4,3,2,1,0:T(8,128)S(1)}, f32[2,4,2,3,8,512]{5,4,3,2,1,0:T(8,128)S(1)}, u32[]{:S(2)}, u32[]{:S(2)}) collective-permute-start(f32[2,4,2,3,8,512]{5,4,3,2,1,0:T(8,128)S(1)} %get-tuple-element.25), channel_id=1, source_target_pairs={{0,64},{1,5},{2,66},{3,7},{4,68},{5,1},{6,70},{7,3},{8,72},{9,13},... | collective-permute-start | bytes 2359304 | tf_op jit(solution)/shard_map/ppermute | solution.py:266
  42.3 16.3 %collective-permute-start.5 = (f32[4,2,3,8,512]{4,3,2,1,0:T(8,128)S(1)}, f32[4,2,3,8,512]{4,3,2,1,0:T(8,128)S(1)}, u32[]{:S(2)}, u32[]{:S(2)}) collective-permute-start(f32[4,2,3,8,512]{4,3,2,1,0:T(8,128)S(1)} %get-tuple-element.24), channel_id=1, source_target_pairs={{0,24},{1,9},{8,0},{9,17},{16,8},{17,25},{24,16},{25,1},{2,26},{3,... | collective-permute-start | bytes 1179656 | tf_op jit(solution)/shard_map/ppermute | solution.py:267
  51.7 9.3 %collective-permute-start.7 = (f32[4,2,3,8,512]{4,3,2,1,0:T(8,128)S(1)}, f32[4,2,3,8,512]{4,3,2,1,0:T(8,128)S(1)}, u32[]{:S(2)}, u32[]{:S(2)}) collective-permute-start(f32[4,2,3,8,512]{4,3,2,1,0:T(8,128)S(1)} %get-tuple-element.26), channel_id=1, source_target_pairs={{0,16},{1,17},{8,24},{9,25},{16,0},{17,1},{24,8},{25,9},{2,18},{3,... | collective-permute-start | bytes 1179656 | tf_op jit(solution)/shard_map/ppermute | solution.py:267
  59.2 31.9 %copy-start.2 = (f32[384,128]{1,0:T(8,128)S(1)}, f32[384,128]{1,0:T(8,128)}, u32[]{:S(2)}) copy-start(f32[384,128]{1,0:T(8,128)} %weights_ref.1) | copy-start | bytes 589828
  59.3 31.9 %copy-start.3 = (f32[384,128]{1,0:T(8,128)S(1)}, f32[384,128]{1,0:T(8,128)}, u32[]{:S(2)}) copy-start(f32[384,128]{1,0:T(8,128)} %first_ref.1) | copy-start | bytes 589828
  59.3 31.9 %copy-start.4 = (f32[384,128]{1,0:T(8,128)S(1)}, f32[384,128]{1,0:T(8,128)}, u32[]{:S(2)}) copy-start(f32[384,128]{1,0:T(8,128)} %second_ref.1) | copy-start | bytes 589828
  59.3 31.9 %copy-start.5 = (bf16[128,128]{1,0:T(8,128)(2,1)S(1)}, bf16[128,128]{1,0:T(8,128)(2,1)}, u32[]{:S(2)}) copy-start(bf16[128,128]{1,0:T(8,128)(2,1)} %constant.31.clone.table_ref) | copy-start | bytes 98308
  62.5 28.7 %all-to-all-start.1 = ((f32[64,48,128]{2,1,0:T(8,128)}), f32[64,48,128]{2,1,0:T(8,128)S(1)}, u32[]{:S(2)}, u32[]{:S(2)}) async-start(f32[64,48,128]{2,1,0:T(8,128)} %bitcast.10), calls=%async_computation.1 | async-start | bytes 3145728 | tf_op jit(solution)/shard_map/all_to_all | solution.py:272

commit v8 on v7

--- a/solution.py
+++ b/solution.py
@@ -261,7 +261,7 @@
     tops = lax.all_to_all(jnp.maximum(*tiles), ALL, 0, 0, tiled=True)
 
     arrived = []
-    for offset in (1, 3, 2):
+    for offset in (2, 1, 3):
         flat, tall = levels_for(offset, owns, raws, twice, tops)
         flat = lax.ppermute(flat, MESH, shift_flat(offset))
         arrived.append((flat, lax.ppermute(tall, ("z", "core"), shift_tall(offset))))

time: 93.4 us -> 93.4 us (level)
  starting transfers between devices: 15.1 us -> 18.5 us
  waiting for transfers between devices: 31.2 us -> 27.8 us
    ppermute x3, waiting for transfers between devices: 13 us -> 8.33 us  [shards(): lax.ppermute(tall, ('z', 'core'), shift_tall(offset))]
    ppermute x3, starting transfers between devices: 3.46 us -> 5.03 us  [shards(): flat = lax.ppermute(flat, MESH, shift_flat(offset))]
    all_to_all x1, starting transfers between devices: 7.65 us -> 9.03 us  [shards(): words = lax.all_to_all(words, CHIPS, 0, 0, tiled=True)]
    all_to_all x1, waiting for transfers between devices: 18.2 us -> 19.5 us  [shards(): words = lax.all_to_all(words, CHIPS, 0, 0, tiled=True)]
where the time goes in v8:
time: 93.4 us; the launch traced here: 93.2 us
  waiting for transfers between devices  27.8 us (30%)
  Pallas kernels  22.9 us (25%)
  blocking collectives  20.2 us (22%)
  starting transfers between devices  18.5 us (20%)
  between operations  2.87 us (3%)
    all_to_all x1, blocking collectives, shards(): tops = lax.all_to_all(jnp.maximum(*tiles), ALL, 0, 0, tiled=True)  20.2 us
    all_to_all x1, waiting for transfers between devices, shards(): words = lax.all_to_all(words, CHIPS, 0, 0, tiled=True)  19.5 us
    pallas_call x2, Pallas kernels, rotate_half(): pl.pallas_call(functools.partial(rotate_kernel, start), in_specs=[pl.Bloc...  10.3 us
    all_to_all x1, starting transfers between devices, shards(): words = lax.all_to_all(words, CHIPS, 0, 0, tiled=True)  9.03 us
    ppermute x3, waiting for transfers between devices, shards(): lax.ppermute(tall, ('z', 'core'), shift_tall(offset))  8.33 us
    pallas_call x4, Pallas kernels, levels_for(): pl.pallas_call(functools.partial(level_kernel, offset), in_specs=[VMEM] *...  7.89 us
    ppermute x3, starting transfers between devices, shards(): flat = lax.ppermute(flat, MESH, shift_flat(offset))  5.03 us
    ppermute x3, starting transfers between devices, shards(): lax.ppermute(tall, ('z', 'core'), shift_tall(offset))  3.76 us
  transfers between devices with their start and end apart: 9, of which 4 were waited for; matrix products, arithmetic and copies ran while one was open for 1% of the time, Pallas kernels for 12%

profile of v8, /device:TPU:0, one launch (start us, length us, event | category | flops | bytes accessed | tf_op | source)
XLA Modules:
  0.0 93.2 jit_solution(13429606983400614565)
XLA Ops:
  0.6 0.0 copy-start
  0.6 0.0 copy-start.1
  0.7 6.0 %shard_map.112 = (f32[8,384,512]{2,1,0:T(8,128)S(1)}, bf16[8,384,512]{2,1,0:T(8,128)(2,1)S(1)}, f32[128,128]{1,0:T(8,128)}) custom-call(bf16[16,2,384,512]{3,2,1,0:T(8,128)(2,1)} %bitcast.34, s32[64,512]{1,0:T(8,128)} %sign_ref.3, bf16[256,256]{1,0:T(8,128)(2,1)} %constant.32.clone.table_ref), custom_call_target="tpu_custom_call" | custom-call | flops 3000000000 | bytes 13000000 | tf_op jit(solution)/shard_map/pallas_call | solution.py:67
  6.6 0.0 copy-start.6
  6.7 0.1 collective-permute-start
  6.7 0.0 copy-done
  6.8 0.0 copy-done.1
  6.8 4.3 %shard_map.113 = (f32[8,384,512]{2,1,0:T(8,128)S(1)}, bf16[8,384,512]{2,1,0:T(8,128)(2,1)S(1)}, f32[128,128]{1,0:T(8,128)S(1)}) custom-call(bf16[16,2,384,512]{3,2,1,0:T(8,128)(2,1)} %bitcast.35, s32[64,512]{1,0:T(8,128)S(1)} %copy-done.1, bf16[256,256]{1,0:T(8,128)(2,1)S(1)} %copy-done), custom_call_target="tpu_custom_call" | custom-call | flops 3000000000 | bytes 13000000 | tf_op jit(solution)/shard_map/pallas_call | solution.py:67
  11.1 0.6 collective-permute-start.1
  11.7 0.0 copy-done.6
  11.7 20.2 %all_to_all.16 = f32[128,1,128]{2,1,0:T(1,128)S(1)} all-to-all(f32[128,1,128]{2,1,0:T(1,128)S(1)} %bitcast.36), channel_id=1, replica_groups=mesh['x'=4,'z'=4,'y'=4,'core'=2] {'z','y','x','core'}, dimensions={0} | all-to-all | bytes 131072 | tf_op jit(solution)/shard_map/all_to_all | solution.py:261
  31.9 0.0 collective-permute-done
  31.9 0.0 collective-permute-done.1
  31.9 2.0 %shard_map.115 = (f32[2,4,2,3,8,512]{5,4,3,2,1,0:T(8,128)S(1)}, f32[4,2,3,8,512]{4,3,2,1,0:T(8,128)S(1)}) custom-call(bf16[8,12,32,512]{3,2,1,0:T(8,128)(2,1)S(1)} %bitcast.21, bf16[8,12,32,512]{3,2,1,0:T(8,128)(2,1)S(1)} %bitcast.25, f32[8,12,32,512]{3,2,1,0:T(8,128)S(1)} %bitcast.13, f32[8,12,32,512]{3,2,1,0:T(8,128)S(1)} %bitcast.17, ...), custom_call_target="tpu_custom_call" | custom-call | flops 1000000 | bytes 10000 | tf_op jit(solution)/shard_map/pallas_call | solution.py:150
  34.0 1.3 %collective-permute-start.2 = (f32[2,4,2,3,8,512]{5,4,3,2,1,0:T(8,128)S(1)}, f32[2,4,2,3,8,512]{5,4,3,2,1,0:T(8,128)S(1)}, u32[]{:S(2)}, u32[]{:S(2)}) collective-permute-start(f32[2,4,2,3,8,512]{5,4,3,2,1,0:T(8,128)S(1)} %get-tuple-element.21), channel_id=1, source_target_pairs={{0,64},{1,5},{2,66},{3,7},{4,68},{5,1},{6,70},{7,3},{8,72},{9,13},... | collective-permute-start | bytes 2359304 | tf_op jit(solution)/shard_map/ppermute | solution.py:266
  35.3 2.0 %shard_map.117 = (f32[2,4,2,3,8,512]{5,4,3,2,1,0:T(8,128)S(1)}, f32[4,2,3,8,512]{4,3,2,1,0:T(8,128)S(1)}) custom-call(bf16[8,12,32,512]{3,2,1,0:T(8,128)(2,1)S(1)} %bitcast.22, bf16[8,12,32,512]{3,2,1,0:T(8,128)(2,1)S(1)} %bitcast.26, f32[8,12,32,512]{3,2,1,0:T(8,128)S(1)} %bitcast.14, f32[8,12,32,512]{3,2,1,0:T(8,128)S(1)} %bitcast.18, ...), custom_call_target="tpu_custom_call" | custom-call | flops 1000000 | bytes 10000 | tf_op jit(solution)/shard_map/pallas_call | solution.py:150
  37.3 0.9 collective-permute-start.4
  38.2 1.1 %collective-permute-start.3 = (f32[4,2,3,8,512]{4,3,2,1,0:T(8,128)S(1)}, f32[4,2,3,8,512]{4,3,2,1,0:T(8,128)S(1)}, u32[]{:S(2)}, u32[]{:S(2)}) collective-permute-start(f32[4,2,3,8,512]{4,3,2,1,0:T(8,128)S(1)} %get-tuple-element.22), channel_id=1, source_target_pairs={{0,16},{1,17},{8,24},{9,25},{16,0},{17,1},{24,8},{25,9},{2,18},{3,... | collective-permute-start | bytes 1179656 | tf_op jit(solution)/shard_map/ppermute | solution.py:267
  39.3 2.0 %shard_map.119 = (f32[2,4,2,3,8,512]{5,4,3,2,1,0:T(8,128)S(1)}, f32[4,2,3,8,512]{4,3,2,1,0:T(8,128)S(1)}) custom-call(bf16[8,12,32,512]{3,2,1,0:T(8,128)(2,1)S(1)} %bitcast.23, bf16[8,12,32,512]{3,2,1,0:T(8,128)(2,1)S(1)} %bitcast.27, f32[8,12,32,512]{3,2,1,0:T(8,128)S(1)} %bitcast.15, f32[8,12,32,512]{3,2,1,0:T(8,128)S(1)} %bitcast.19, ...), custom_call_target="tpu_custom_call" | custom-call | flops 1000000 | bytes 10000 | tf_op jit(solution)/shard_map/pallas_call | solution.py:150
  41.3 2.9 %collective-permute-start.6 = (f32[2,4,2,3,8,512]{5,4,3,2,1,0:T(8,128)S(1)}, f32[2,4,2,3,8,512]{5,4,3,2,1,0:T(8,128)S(1)}, u32[]{:S(2)}, u32[]{:S(2)}) collective-permute-start(f32[2,4,2,3,8,512]{5,4,3,2,1,0:T(8,128)S(1)} %get-tuple-element.25), channel_id=1, source_target_pairs={{0,96},{1,7},{2,98},{3,1},{4,100},{5,3},{6,102},{7,5},{8,104},{9,1... | collective-permute-start | bytes 2359304 | tf_op jit(solution)/shard_map/ppermute | solution.py:266
  44.2 0.0 collective-permute-start.5
  44.2 5.8 %collective-permute-done.3.tall_ref = f32[4,2,3,8,512]{4,3,2,1,0:T(8,128)S(1)} collective-permute-done((f32[4,2,3,8,512]{4,3,2,1,0:T(8,128)S(1)}, f32[4,2,3,8,512]{4,3,2,1,0:T(8,128)S(1)}, u32[]{:S(2)}, u32[]{:S(2)}) %collective-permute-start.3) | collective-permute-done | bytes 393248 | tf_op jit(solution)/shard_map/ppermute | solution.py:267
  50.0 2.7 %collective-permute-start.7 = (f32[4,2,3,8,512]{4,3,2,1,0:T(8,128)S(1)}, f32[4,2,3,8,512]{4,3,2,1,0:T(8,128)S(1)}, u32[]{:S(2)}, u32[]{:S(2)}) collective-permute-start(f32[4,2,3,8,512]{4,3,2,1,0:T(8,128)S(1)} %get-tuple-element.26), channel_id=1, source_target_pairs={{0,24},{1,9},{8,0},{9,17},{16,8},{17,25},{24,16},{25,1},{2,26},{3,... | collective-permute-start | bytes 1179656 | tf_op jit(solution)/shard_map/ppermute | solution.py:267
  52.7 1.8 %shard_map.114.sums_ref = f32[4,4,4,48,128]{4,3,2,1,0:T(8,128)S(1)} custom-call(bf16[8,12,32,512]{3,2,1,0:T(8,128)(2,1)S(1)} %bitcast.24, bf16[8,12,32,512]{3,2,1,0:T(8,128)(2,1)S(1)} %bitcast.28, f32[8,12,32,512]{3,2,1,0:T(8,128)S(1)} %bitcast.16, f32[8,12,32,512]{3,2,1,0:T(8,128)S(1)} %bitcast.20, bf16[256,256]{1,0:T(8,128)(2,1)S(1)} %copy-done, ...), custom_call_target="tpu_custom_call" | custom-call | flops 1000000 | bytes 10000 | tf_op jit(solution)/shard_map/pallas_call | solution.py:150
  54.5 0.0 collective-permute-done.2.flat_ref
  54.5 0.7 shard_map.116.sums_ref
  55.1 1.1 %collective-permute-done.5.tall_ref = f32[4,2,3,8,512]{4,3,2,1,0:T(8,128)S(1)} collective-permute-done((f32[4,2,3,8,512]{4,3,2,1,0:T(8,128)S(1)}, f32[4,2,3,8,512]{4,3,2,1,0:T(8,128)S(1)}, u32[]{:S(2)}, u32[]{:S(2)}) %collective-permute-start.5) | collective-permute-done | bytes 393248 | tf_op jit(solution)/shard_map/ppermute | solution.py:267
  56.2 0.0 collective-permute-done.4.flat_ref
  56.2 0.7 shard_map.118.sums_ref
  56.9 0.0 copy-start.2
  56.9 0.0 copy-start.3
  56.9 0.0 copy-start.4
  56.9 0.0 copy-start.5
  56.9 1.5 %collective-permute-done.7.tall_ref = f32[4,2,3,8,512]{4,3,2,1,0:T(8,128)S(1)} collective-permute-done((f32[4,2,3,8,512]{4,3,2,1,0:T(8,128)S(1)}, f32[4,2,3,8,512]{4,3,2,1,0:T(8,128)S(1)}, u32[]{:S(2)}, u32[]{:S(2)}) %collective-permute-start.7) | collective-permute-done | bytes 393248 | tf_op jit(solution)/shard_map/ppermute | solution.py:267
  58.4 0.0 collective-permute-done.6.flat_ref
  58.4 1.4 %shard_map.120 = f32[4,4,4,48,128]{4,3,2,1,0:T(8,128)} custom-call(f32[4,4,4,48,128]{4,3,2,1,0:T(8,128)S(1)} %shard_map.118.sums_ref, f32[2,4,2,3,8,512]{5,4,3,2,1,0:T(8,128)S(1)} %collective-permute-done.6.flat_ref, f32[4,2,3,8,512]{4,3,2,1,0:T(8,128)S(1)} %collective-permute-done.7.tall_ref), custom_call_target="tpu_custom_call" | custom-call | flops 10000000 | bytes 4000000 | tf_op jit(solution)/shard_map/pallas_call | solution.py:194
  59.8 9.0 %all-to-all-start.1 = ((f32[64,48,128]{2,1,0:T(8,128)}), f32[64,48,128]{2,1,0:T(8,128)S(1)}, u32[]{:S(2)}, u32[]{:S(2)}) async-start(f32[64,48,128]{2,1,0:T(8,128)} %bitcast.10), calls=%async_computation.1 | async-start | bytes 3145728 | tf_op jit(solution)/shard_map/all_to_all | solution.py:272
  70.3 0.7 reduce_max.9
  71.7 0.1 pad_maximum_fusion.scalars
  71.7 19.5 %all-to-all-done.1 = f32[64,48,128]{2,1,0:T(8,128)S(1)} async-done(((f32[64,48,128]{2,1,0:T(8,128)}), f32[64,48,128]{2,1,0:T(8,128)S(1)}, u32[]{:S(2)}, u32[]{:S(2)}) %all-to-all-start.1) | async-done | bytes 1572896 | tf_op jit(solution)/shard_map/all_to_all | solution.py:272
  91.2 0.0 copy-done.2
  91.2 0.0 copy-done.3
  91.2 0.0 copy-done.4
  91.2 0.0 copy-done.5
  91.2 1.9 %shard_map.121 = (f32[384,128]{1,0:T(8,128)}, f32[384,128]{1,0:T(8,128)}, f32[384,128]{1,0:T(8,128)}) custom-call(f32[3]{0:T(128)S(1)} %pad_maximum_fusion.scalars, f32[4,4,4,48,128]{4,3,2,1,0:T(8,128)S(1)} %bitcast.29, bf16[128,128]{1,0:T(8,128)(2,1)S(1)} %copy-done.5, s32[64,128]{1,0:T(8,128)S(1)} %constant_dynamic-slice_fusion.sign_ref, ...), custom_call_target="tpu_custom_call" | custom-call | tf_op jit(solution)/shard_map/pallas_call | solution.py:285
  (2 shorter events, 0.0 us)
Async XLA Ops:
  0.6 6.1 %copy-start = (bf16[256,256]{1,0:T(8,128)(2,1)S(1)}, bf16[256,256]{1,0:T(8,128)(2,1)}, u32[]{:S(2)}) copy-start(bf16[256,256]{1,0:T(8,128)(2,1)} %constant.32.clone.table_ref) | copy-start | bytes 393220
  0.6 6.1 %copy-start.1 = (s32[64,512]{1,0:T(8,128)S(1)}, s32[64,512]{1,0:T(8,128)}, u32[]{:S(2)}) copy-start(s32[64,512]{1,0:T(8,128)} %sign_ref.3) | copy-start | bytes 393220
  6.6 5.0 %copy-start.6 = (f32[128,128]{1,0:T(8,128)S(1)}, f32[128,128]{1,0:T(8,128)}, u32[]{:S(2)}) copy-start(f32[128,128]{1,0:T(8,128)} %get-tuple-element.15) | copy-start | bytes 196612
  6.7 25.3 %collective-permute-start = (f32[8,384,512]{2,1,0:T(8,128)S(1)}, f32[8,384,512]{2,1,0:T(8,128)S(1)}, u32[]{:S(2)}, u32[]{:S(2)}) collective-permute-start(f32[8,384,512]{2,1,0:T(8,128)S(1)} %get-tuple-element.19), channel_id=1, source_target_pairs={{0,1},{1,0},{2,3},{3,2},{4,5},{5,4},{6,7},{7,6},{8,9},{9,8},{10,11... | collective-permute-start | bytes 18874376 | tf_op jit(solution)/shard_map/ppermute | solution.py:258
  11.1 20.8 %collective-permute-start.1 = (f32[8,384,512]{2,1,0:T(8,128)S(1)}, f32[8,384,512]{2,1,0:T(8,128)S(1)}, u32[]{:S(2)}, u32[]{:S(2)}) collective-permute-start(f32[8,384,512]{2,1,0:T(8,128)S(1)} %get-tuple-element.20), channel_id=1, source_target_pairs={{0,1},{1,0},{2,3},{3,2},{4,5},{5,4},{6,7},{7,6},{8,9},{9,8},{10,11... | collective-permute-start | bytes 18874376 | tf_op jit(solution)/shard_map/ppermute | solution.py:258
  34.0 20.5 %collective-permute-start.2 = (f32[2,4,2,3,8,512]{5,4,3,2,1,0:T(8,128)S(1)}, f32[2,4,2,3,8,512]{5,4,3,2,1,0:T(8,128)S(1)}, u32[]{:S(2)}, u32[]{:S(2)}) collective-permute-start(f32[2,4,2,3,8,512]{5,4,3,2,1,0:T(8,128)S(1)} %get-tuple-element.21), channel_id=1, source_target_pairs={{0,64},{1,5},{2,66},{3,7},{4,68},{5,1},{6,70},{7,3},{8,72},{9,13},... | collective-permute-start | bytes 2359304 | tf_op jit(solution)/shard_map/ppermute | solution.py:266
  37.3 18.9 %collective-permute-start.4 = (f32[2,4,2,3,8,512]{5,4,3,2,1,0:T(8,128)S(1)}, f32[2,4,2,3,8,512]{5,4,3,2,1,0:T(8,128)S(1)}, u32[]{:S(2)}, u32[]{:S(2)}) collective-permute-start(f32[2,4,2,3,8,512]{5,4,3,2,1,0:T(8,128)S(1)} %get-tuple-element.23), channel_id=1, source_target_pairs={{0,32},{1,3},{2,34},{3,5},{4,36},{5,7},{6,38},{7,1},{8,40},{9,11},... | collective-permute-start | bytes 2359304 | tf_op jit(solution)/shard_map/ppermute | solution.py:266
  38.2 11.8 %collective-permute-start.3 = (f32[4,2,3,8,512]{4,3,2,1,0:T(8,128)S(1)}, f32[4,2,3,8,512]{4,3,2,1,0:T(8,128)S(1)}, u32[]{:S(2)}, u32[]{:S(2)}) collective-permute-start(f32[4,2,3,8,512]{4,3,2,1,0:T(8,128)S(1)} %get-tuple-element.22), channel_id=1, source_target_pairs={{0,16},{1,17},{8,24},{9,25},{16,0},{17,1},{24,8},{25,9},{2,18},{3,... | collective-permute-start | bytes 1179656 | tf_op jit(solution)/shard_map/ppermute | solution.py:267
  41.3 17.0 %collective-permute-start.6 = (f32[2,4,2,3,8,512]{5,4,3,2,1,0:T(8,128)S(1)}, f32[2,4,2,3,8,512]{5,4,3,2,1,0:T(8,128)S(1)}, u32[]{:S(2)}, u32[]{:S(2)}) collective-permute-start(f32[2,4,2,3,8,512]{5,4,3,2,1,0:T(8,128)S(1)} %get-tuple-element.25), channel_id=1, source_target_pairs={{0,96},{1,7},{2,98},{3,1},{4,100},{5,3},{6,102},{7,5},{8,104},{9,1... | collective-permute-start | bytes 2359304 | tf_op jit(solution)/shard_map/ppermute | solution.py:266
  44.2 12.0 %collective-permute-start.5 = (f32[4,2,3,8,512]{4,3,2,1,0:T(8,128)S(1)}, f32[4,2,3,8,512]{4,3,2,1,0:T(8,128)S(1)}, u32[]{:S(2)}, u32[]{:S(2)}) collective-permute-start(f32[4,2,3,8,512]{4,3,2,1,0:T(8,128)S(1)} %get-tuple-element.24), channel_id=1, source_target_pairs={{0,8},{1,25},{8,16},{9,1},{16,24},{17,9},{24,0},{25,17},{2,10},{3,... | collective-permute-start | bytes 1179656 | tf_op jit(solution)/shard_map/ppermute | solution.py:267
  50.0 8.4 %collective-permute-start.7 = (f32[4,2,3,8,512]{4,3,2,1,0:T(8,128)S(1)}, f32[4,2,3,8,512]{4,3,2,1,0:T(8,128)S(1)}, u32[]{:S(2)}, u32[]{:S(2)}) collective-permute-start(f32[4,2,3,8,512]{4,3,2,1,0:T(8,128)S(1)} %get-tuple-element.26), channel_id=1, source_target_pairs={{0,24},{1,9},{8,0},{9,17},{16,8},{17,25},{24,16},{25,1},{2,26},{3,... | collective-permute-start | bytes 1179656 | tf_op jit(solution)/shard_map/ppermute | solution.py:267
  56.9 34.3 %copy-start.2 = (f32[384,128]{1,0:T(8,128)S(1)}, f32[384,128]{1,0:T(8,128)}, u32[]{:S(2)}) copy-start(f32[384,128]{1,0:T(8,128)} %weights_ref.1) | copy-start | bytes 589828
  56.9 34.3 %copy-start.3 = (f32[384,128]{1,0:T(8,128)S(1)}, f32[384,128]{1,0:T(8,128)}, u32[]{:S(2)}) copy-start(f32[384,128]{1,0:T(8,128)} %first_ref.1) | copy-start | bytes 589828
  56.9 34.3 %copy-start.4 = (f32[384,128]{1,0:T(8,128)S(1)}, f32[384,128]{1,0:T(8,128)}, u32[]{:S(2)}) copy-start(f32[384,128]{1,0:T(8,128)} %second_ref.1) | copy-start | bytes 589828
  56.9 34.3 %copy-start.5 = (bf16[128,128]{1,0:T(8,128)(2,1)S(1)}, bf16[128,128]{1,0:T(8,128)(2,1)}, u32[]{:S(2)}) copy-start(bf16[128,128]{1,0:T(8,128)(2,1)} %constant.31.clone.table_ref) | copy-start | bytes 98308
  59.8 31.4 %all-to-all-start.1 = ((f32[64,48,128]{2,1,0:T(8,128)}), f32[64,48,128]{2,1,0:T(8,128)S(1)}, u32[]{:S(2)}, u32[]{:S(2)}) async-start(f32[64,48,128]{2,1,0:T(8,128)} %bitcast.10), calls=%async_computation.1 | async-start | bytes 3145728 | tf_op jit(solution)/shard_map/all_to_all | solution.py:272
